TPU v7x, 32 devices: a whole 2x2x4 slice. The times are simulated.
32 devices in a mesh: row: 8 (over z, y), col: 4 (over x, core).
Axes of the slice: x: 2, y: 2, z: 4, core: 2. Of those that a mesh axis runs over, the one named last changes fastest.
Arguments:
- p_values: bfloat16 [128, 16, 128, 128], P('row', 'col'), may hold values from -0.5 to 0.5
- p_cols: int32 [128, 16], P('row', 'col'), may hold values from -1 to 127, as said below
- s_values: bfloat16 [128, 16, 128, 128], P('row', 'col'), may hold values from -1.796875 to 1.796875
- s_cols: int32 [128, 16], P('row', 'col'), may hold values from -1 to 127, as said below
- c_cols: int32 [128, 32], P('row', 'col'), may hold values from -1 to 127, as said below
Outputs:
- product: float32 [128, 32, 128, 128], P('row', 'col')
Inputs may be any that keep to these rules, and one draw needn't show every extreme that they name: `p_cols`: each block row r of P holds distinct block columns c with (c - r) mod 128 in [-8, 8] taken cyclically; other slots are -1. `s_cols`: in block row q of S, slots g * 4 to (g + 1) * 4 - 1 hold distinct block columns c with c mod 4 = g and (c - q) mod 128 in [-8, 8] taken cyclically; other slots are -1. `c_cols`: in block row r, slots g * 8 to (g + 1) * 8 - 1 hold distinct block columns c with c mod 4 = g and (c - r) mod 128 in [-16, 16] taken cyclically; other slots are -1.
All inputs are finite; a program needn't handle non-finite values.
Results may differ from a plain program's by a relative error of at most 0.0003.
Values may be sent and summed in bfloat16 or wider, within the bound.
No kernel may reach another device: no remote copies, remote signals or barrier semaphores. Data moves between devices by JAX's collectives and lax.ppermute only.
A program may use at most 192 MiB of HBM per device.

v0:
```python
import jax
import jax.numpy as jnp
from jax import lax
from jax.sharding import PartitionSpec as P


def with_halo(block, sides, width):
    for axis, dim in sides:
        count = lax.axis_size(axis)
        forward = [(i, i + 1) for i in range(count - 1)]
        forward.append((count - 1, 0))
        backward = [(target, source) for source, target in forward]
        low = lax.ppermute(
            lax.slice_in_dim(block, block.shape[dim] - width, None, axis=dim), axis, forward
        )
        high = lax.ppermute(lax.slice_in_dim(block, 0, width, axis=dim), axis, backward)
        block = jnp.concatenate([low, block, high], axis=dim)
    return block


def shards(p_values, p_cols, s_values, s_cols, c_cols):
    block_rows = p_values.shape[0]
    reach = block_rows // 2
    total_rows = block_rows * lax.axis_size("row")
    first_row = lax.axis_index("row") * block_rows - reach
    near_values, near_cols = (
        with_halo(s_values, (("row", 0),), reach),
        with_halo(s_cols, (("row", 0),), reach),
    )
    piece_vals = lax.all_gather(p_values, "col", axis=1, tiled=True)
    piece_cols = lax.all_gather(p_cols, "col", axis=1, tiled=True)
    live = piece_cols >= 0
    local = jnp.where(live, (piece_cols - first_row) % total_rows, 0).astype(jnp.int32)
    s_rows = near_values[local]
    s_row_cols = near_cols[local]
    match = (
        (s_row_cols[:, :, :, None] == c_cols[:, None, None, :])
        & (s_row_cols[:, :, :, None] >= 0)
        & live[:, :, None, None]
    )
    placed = jnp.einsum(
        "rklm,rklbc->rkmbc", match.astype(jnp.bfloat16), s_rows, preferred_element_type=jnp.float32
    ).astype(jnp.bfloat16)
    return jnp.einsum("rkab,rkmbc->rmac", piece_vals, placed, preferred_element_type=jnp.float32)


def solution(mesh):
    return jax.shard_map(
        shards,
        mesh=mesh,
        in_specs=(
            P("row", "col", None, None),
            P("row", "col"),
            P("row", "col", None, None),
            P("row", "col"),
            P("row", "col"),
        ),
        out_specs=P("row", "col", None, None),
        check_vma=False,
    )
```

profile of v0, /device:TPU:0, one launch (start us, length us, event | category | flops | bytes accessed | tf_op | source)
XLA Modules:
  0.0 185.2 jit_solution(16814423249935856745)
XLA Ops:
  6.5 0.0 copy-start
  6.5 0.0 all-gather.3.cloned.1.call-start
  6.5 0.7 all-gather.3.cloned.1.call-update
  7.3 0.8 fusion.20
  8.1 3.0 %collective-permute-start = (s32[8,4]{0,1:T(4,128)S(1)}, s32[8,4]{0,1:T(4,128)S(1)}, u32[]{:S(2)}, u32[]{:S(2)}) collective-permute-start(s32[8,4]{0,1:T(4,128)S(1)} %get-tuple-element.7), channel_id=1, source_target_pairs={{0,4},{4,8},{8,12},{12,16},{16,20},{20,24},{24,28},{28,0},{1,5},{5... | collective-permute-start | bytes 392 | tf_op jit(solution)/shard_map/ppermute | solution.py:13
  11.1 3.0 %collective-permute-start.1 = (s32[8,4]{0,1:T(4,128)S(1)}, s32[8,4]{0,1:T(4,128)S(1)}, u32[]{:S(2)}, u32[]{:S(2)}) collective-permute-start(s32[8,4]{0,1:T(4,128)S(1)} %get-tuple-element.8), channel_id=1, source_target_pairs={{4,0},{8,4},{12,8},{16,12},{20,16},{24,20},{28,24},{0,28},{5,1},{9... | collective-permute-start | bytes 392 | tf_op jit(solution)/shard_map/ppermute | solution.py:16
  14.1 2.7 %fusion.19 = (bf16[8,4,128,128]{3,2,1,0:T(8,128)(2,1)}, bf16[8,4,128,128]{3,2,1,0:T(8,128)(2,1)S(1)}) fusion(bf16[16,4,128,128]{3,2,1,0:T(8,128)(2,1)} %param.7), kind=kLoop, calls=%fused_computation.28 | loop fusion | bytes 4194304 | tf_op jit(solution)/shard_map/slice | solution.py:14
  16.8 0.0 collective-permute-start.2
  16.8 4.7 %collective-permute-start.3 = (bf16[8,4,128,128]{3,2,1,0:T(8,128)(2,1)S(1)}, bf16[8,4,128,128]{3,2,1,0:T(8,128)(2,1)}, u32[]{:S(2)}, u32[]{:S(2)}) collective-permute-start(bf16[8,4,128,128]{3,2,1,0:T(8,128)(2,1)S(1)} %get-tuple-element.6), channel_id=1, source_target_pairs={{4,0},{8,4},{12,8},{16,12},{20,16},{24,20},{28,24},{0,28},{5,1},{9... | collective-permute-start | bytes 3145736 | tf_op jit(solution)/shard_map/ppermute | solution.py:16
  21.6 5.5 %all-gather = s32[4,4,16]{2,1,0:T(4,128)S(1)} all-gather(s32[1,4,16]{2,1,0:T(4,128)} %bitcast.41), channel_id=1, replica_groups=mesh['row'=8,'col'=4] {'col'}, dimensions={0}, use_global_device_ids=true | all-gather | bytes 1280 | tf_op jit(solution)/shard_map/all_gather | solution.py:31
  27.0 0.1 copy.19
  27.1 0.1 copy.20
  27.2 0.1 reshape.9
  27.3 0.8 copy.22
  28.1 0.0 collective-permute-done
  28.1 0.0 collective-permute-done.1
  28.1 0.8 pad_add_fusion
  28.8 0.1 copy.21
  28.9 0.7 gather_fusion
  29.7 32.3 %collective-permute-done.2 = bf16[8,4,128,128]{3,2,1,0:T(8,128)(2,1)} collective-permute-done((bf16[8,4,128,128]{3,2,1,0:T(8,128)(2,1)}, bf16[8,4,128,128]{3,2,1,0:T(8,128)(2,1)}, u32[]{:S(2)}, u32[]{:S(2)}) %collective-permute-start.2) | collective-permute-done | bytes 1048608 | tf_op jit(solution)/shard_map/ppermute | solution.py:13
  62.0 2.0 %collective-permute-done.3 = bf16[8,4,128,128]{3,2,1,0:T(8,128)(2,1)} collective-permute-done((bf16[8,4,128,128]{3,2,1,0:T(8,128)(2,1)S(1)}, bf16[8,4,128,128]{3,2,1,0:T(8,128)(2,1)}, u32[]{:S(2)}, u32[]{:S(2)}) %collective-permute-start.3) | collective-permute-done | bytes 1048608 | tf_op jit(solution)/shard_map/ppermute | solution.py:16
  64.0 0.0 copy-done
  64.0 3.5 %pad_maximum_fusion = bf16[32,4,128,128]{3,2,1,0:T(8,128)(2,1)} fusion(bf16[8,4,128,128]{3,2,1,0:T(8,128)(2,1)} %collective-permute-done.3, bf16[16,4,128,128]{3,2,1,0:T(8,128)(2,1)S(1)} %copy-done, bf16[8,4,128,128]{3,2,1,0:T(8,128)(2,1)} %collective-permute-done.2), kind=kLoop, calls=%fused_computation.7 | loop fusion | flops 4194304 | bytes 8388608 | tf_op jit(solution)/shard_map/concatenate | solution.py:17
  67.5 16.2 %gather_fusion.1 = bf16[256,4,128,128]{3,2,1,0:T(8,128)(2,1)} fusion(bf16[32,4,128,128]{3,2,1,0:T(8,128)(2,1)} %pad_maximum_fusion, s32[1024]{0:T(1024)S(1)} %pad_clamp_fusion), kind=kCustom, calls=%fused_computation.1 | custom fusion | bytes 67109888 | tf_op jit(solution)/shard_map/gather | solution.py:34
  83.7 48.8 %convolution_convert_fusion = bf16[16,16,8,128,128]{4,2,3,1,0:T(8,128)(2,1)} fusion(bf16[16,16,4,128,128]{4,3,2,1,0:T(8,128)(2,1)} %bitcast.34, s32[16,8]{1,0:T(8,128)S(1)} %copy.22, s32[16,16,4]{2,1,0:T(8,128)S(1)} %bitcast.36, pred[16,16]{1,0:T(8,128)(4,1)S(1)} %bitcast.37, pred[16,16,4]{2,1,0:T(8,128)(4,1)S(1)} %broadcast_compare_fusion), kind=kOutput, calls=%fused_computation.4 | convolution fusion | flops 302014464 | bytes 100669184 | tf_op jit(solution)/shard_map/rklm,rklbc->rkmbc/dot_general | solution.py:41
  132.5 0.0 all-gather.3.cloned.1.call-done
  132.5 36.7 %fusion.4 = f32[16,8,128,128]{2,3,1,0:T(8,128)} fusion(bf16[16,16,128,128]{3,2,1,0:T(8,128)(2,1)} %all-gather.3.cloned.1.call-done, bf16[16,16,8,128,128]{4,2,3,1,0:T(8,128)(2,1)} %convolution_convert_fusion), kind=kOutput, calls=%fused_computation.8 | convolution fusion | flops 8589934592 | bytes 83886080 | tf_op jit(solution)/shard_map/rkab,rkmbc->rmac/dot_general | solution.py:44
  169.1 9.2 %copy.25 = f32[16,8,128,128]{3,2,1,0:T(8,128)} copy(f32[16,8,128,128]{2,3,1,0:T(8,128)} %fusion.4) | data formatting | bytes 16777216 | tf_op jit(solution)/shard_map/rkab,rkmbc->rmac/transpose | solution.py:44
  (5 shorter events, 0.1 us)
Async XLA Ops:
  6.5 57.5 %copy-start = (bf16[16,4,128,128]{3,2,1,0:T(8,128)(2,1)S(1)}, bf16[16,4,128,128]{3,2,1,0:T(8,128)(2,1)}, u32[]{:S(2)}) copy-start(bf16[16,4,128,128]{3,2,1,0:T(8,128)(2,1)} %param.7) | copy-start | bytes 6291460
  6.5 126.0 %all-gather.3.cloned.1.call-start = ((), (), s32[]{:S(2)}) async-start(), calls=%async_computation | async-start | bytes 10485760 | tf_op jit(solution)/shard_map/all_gather | solution.py:30
  8.1 20.0 %collective-permute-start = (s32[8,4]{0,1:T(4,128)S(1)}, s32[8,4]{0,1:T(4,128)S(1)}, u32[]{:S(2)}, u32[]{:S(2)}) collective-permute-start(s32[8,4]{0,1:T(4,128)S(1)} %get-tuple-element.7), channel_id=1, source_target_pairs={{0,4},{4,8},{8,12},{12,16},{16,20},{20,24},{24,28},{28,0},{1,5},{5... | collective-permute-start | bytes 392 | tf_op jit(solution)/shard_map/ppermute | solution.py:13
  11.1 17.0 %collective-permute-start.1 = (s32[8,4]{0,1:T(4,128)S(1)}, s32[8,4]{0,1:T(4,128)S(1)}, u32[]{:S(2)}, u32[]{:S(2)}) collective-permute-start(s32[8,4]{0,1:T(4,128)S(1)} %get-tuple-element.8), channel_id=1, source_target_pairs={{4,0},{8,4},{12,8},{16,12},{20,16},{24,20},{28,24},{0,28},{5,1},{9... | collective-permute-start | bytes 392 | tf_op jit(solution)/shard_map/ppermute | solution.py:16
  16.8 45.2 %collective-permute-start.2 = (bf16[8,4,128,128]{3,2,1,0:T(8,128)(2,1)}, bf16[8,4,128,128]{3,2,1,0:T(8,128)(2,1)}, u32[]{:S(2)}, u32[]{:S(2)}) collective-permute-start(bf16[8,4,128,128]{3,2,1,0:T(8,128)(2,1)} %get-tuple-element.5), channel_id=1, source_target_pairs={{0,4},{4,8},{8,12},{12,16},{16,20},{20,24},{24,28},{28,0},{1,5},{5... | collective-permute-start | bytes 3145736 | tf_op jit(solution)/shard_map/ppermute | solution.py:13
  16.8 47.2 %collective-permute-start.3 = (bf16[8,4,128,128]{3,2,1,0:T(8,128)(2,1)S(1)}, bf16[8,4,128,128]{3,2,1,0:T(8,128)(2,1)}, u32[]{:S(2)}, u32[]{:S(2)}) collective-permute-start(bf16[8,4,128,128]{3,2,1,0:T(8,128)(2,1)S(1)} %get-tuple-element.6), channel_id=1, source_target_pairs={{4,0},{8,4},{12,8},{16,12},{20,16},{24,20},{28,24},{0,28},{5,1},{9... | collective-permute-start | bytes 3145736 | tf_op jit(solution)/shard_map/ppermute | solution.py:16
Sparse Core Ops, SparseCore 0:
  8.9 61.0 all-gather.2
where the time goes:
time: 186 us; the launch traced here: 185 us
  matrix products  85.4 us (46%)
  waiting for transfers between devices  35.1 us (19%)
  local copies, waits for them, and re-layouts  30.8 us (17%)
  between operations  13.4 us (7%)
  starting transfers between devices  10.8 us (6%)
  blocking collectives  5.48 us (3%)
  other arithmetic  4.26 us (2%)
    dot_general x1, matrix products, shards(): jnp.einsum('rklm,rklbc->rkmbc', match.astype(jnp.bfloat16), s_rows, prefe...  48.8 us
    dot_general x1, matrix products, shards(): jnp.einsum('rkab,rkmbc->rmac', piece_vals, placed, preferred_element_type...  36.7 us
    ppermute x2, waiting for transfers between devices, with_halo(): lax.ppermute(lax.slice_in_dim(block, block.shape[dim] - width, None, axis...  32.4 us
    gather x1, local copies, waits for them, and re-layouts, shards(): s_rows = near_values[local]  16.2 us
    transpose x1, local copies, waits for them, and re-layouts, shards(): jnp.einsum('rkab,rkmbc->rmac', piece_vals, placed, preferred_element_type...  9.24 us
    ppermute x2, starting transfers between devices, with_halo(): lax.ppermute(lax.slice_in_dim(block, 0, width, axis=dim), axis, backward)  7.76 us
    all_gather x1, blocking collectives, shards(): piece_cols = lax.all_gather(p_cols, 'col', axis=1, tiled=True)  5.48 us
    concatenate x2, other arithmetic, with_halo(): block = jnp.concatenate([low, block, high], axis=dim)  4.21 us
  transfers between devices with their start and end apart: 5, of which 2 were waited for; matrix products, arithmetic and copies ran while one was open for 40% of the time, Pallas kernels for 0%

commit v1 on v0

v1 whole, which is shorter than its diff:
```python
import functools

import jax
import jax.numpy as jnp
from jax import lax
from jax.experimental import pallas as pl
from jax.experimental.pallas import tpu as pltpu
from jax.sharding import PartitionSpec as P

VMEM_GRANT = 16 << 20
ANY = pl.BlockSpec(memory_space=pl.ANY)
SMEM = pl.BlockSpec(memory_space=pltpu.SMEM)
VMEM = pl.BlockSpec(memory_space=pltpu.VMEM)


def in_vmem(array):
    return pltpu.with_memory_space_constraint(array, pltpu.VMEM)


def in_hbm(array):
    return pltpu.with_memory_space_constraint(array, pltpu.HBM)


def row_chunks(block_rows):
    reach = block_rows // 2
    edges = [0, reach]
    for left in (reach // 2, reach // 4, 0):
        if block_rows - left > edges[-1]:
            edges.append(block_rows - left)
    return list(zip(edges[:-1], edges[1:]))


def local_start(part, block_rows, flip):
    start, stop = part
    return jnp.where(flip == 1, block_rows - stop, start)


def window_start(part, block_rows, flip):
    start, stop = part
    reach = block_rows // 2
    if start < reach:
        return jnp.where(flip == 1, reach + block_rows + start, reach - stop)
    return jnp.where(flip == 1, start - block_rows + reach, reach + 2 * block_rows - stop)


def cut(flips, p_values, s_values, cuts):
    block_rows = p_values.shape[0]
    sources = (p_values, s_values)

    def body(flips_ref, *refs):
        ins, outs, sems = refs[:2], refs[2:-1], refs[-1]
        copies = [
            pltpu.make_async_copy(
                ins[source].at[
                    pl.ds(local_start(part, block_rows, flips_ref[source]), out.shape[0])
                ],
                out,
                sems.at[n],
            )
            for n, ((source, part), out) in enumerate(zip(cuts, outs))
        ]
        for copy in copies:
            copy.start()
        for copy in copies:
            copy.wait()

    shapes = [
        jax.ShapeDtypeStruct((part[1] - part[0],) + sources[source].shape[1:], p_values.dtype)
        for source, part in cuts
    ]
    return list(
        pl.pallas_call(
            body,
            out_shape=shapes,
            in_specs=[SMEM, ANY, ANY],
            out_specs=[VMEM] * len(shapes),
            scratch_shapes=[pltpu.SemaphoreType.DMA((len(cuts),))],
            compiler_params=pltpu.CompilerParams(vmem_limit_bytes=VMEM_GRANT),
        )(flips, in_hbm(p_values), in_hbm(s_values))
    )


def find_places(first_ref, flip_ref, near_ref, own_ref, far_ref, kept_ref, *refs, total_rows):
    p_refs, place_ref = refs[:-1], refs[-1]
    kept, block_rows = kept_ref.shape
    s_slots, reach = own_ref.shape[0], block_rows // 2
    shape = place_ref.shape
    lane = lax.broadcasted_iota(jnp.int32, shape, 1)
    p_cols = jnp.full(shape, -1, jnp.int32)
    k = 0
    for ref in p_refs:
        cols = ref[...].T
        for slot in range(cols.shape[1]):
            p_cols = jnp.where(lane // kept == k, cols[:, slot : slot + 1], p_cols)
            k += 1
    wanted = jnp.full(shape, -2, jnp.int32)
    cols = kept_ref[...].T
    for m in range(kept):
        wanted = jnp.where(lane % kept == m, cols[:, m : m + 1], wanted)
    wanted = jnp.where(wanted < 0, -2, wanted)
    first_row = first_ref[0]
    local = p_cols - first_row
    local = jnp.where(local < 0, local + total_rows, local)
    local = jnp.where(local >= total_rows, local - total_rows, local)
    local = jnp.where(p_cols < 0, -1, local)
    flipped = flip_ref[0] == 1
    none = 2 * block_rows * s_slots
    place = jnp.full(shape, none, jnp.int32)
    for q in range(2 * block_rows):
        here = local == q
        for slot in range(s_slots):
            if q < reach:
                near, far = near_ref[slot, q + reach], far_ref[slot, q + reach]
                col = jnp.where(flipped, far, near)
            elif q < reach + block_rows:
                col = own_ref[slot, q - reach]
            else:
                row = q - reach - block_rows
                col = jnp.where(flipped, near_ref[slot, row], far_ref[slot, row])
            place = jnp.where(here & (wanted == col), q * s_slots + slot, place)
    place_ref[...] = place


def multiply(flip_ref, place_ref, *refs, pieces, chunk, block_rows, kept, news, first):
    p_refs = refs[: len(pieces)]
    new_refs = refs[len(pieces) : len(pieces) + len(news)]
    rest = refs[len(pieces) + len(news) + (0 if first else 2) :]
    out_ref, window, lefts, results, new_sem, p_sems, out_sems = rest
    flip = flip_ref[0]
    start = local_start(chunk, block_rows, flip)
    count = chunk[1] - chunk[0]
    slots, s_slots = lefts.shape[1], (window.shape[0] - 1) // (2 * block_rows)
    own_slots = slots // len(pieces)
    wide = max(w for w in (4, 2, 1) if kept % w == 0)
    order = window.shape[1]

    def fetch(i, n):
        return pltpu.make_async_copy(
            p_refs[n].at[start + i if pieces[n] else i],
            lefts.at[i, pl.ds(n * own_slots, own_slots)],
            p_sems.at[i],
        )

    def store(i, m):
        return pltpu.make_async_copy(
            results.at[i % 2, pl.ds(m, wide)],
            out_ref.at[start + i, pl.ds(m, wide)],
            out_sems.at[i % 2],
        )

    def stored(i):
        return pltpu.make_async_copy(
            results.at[i % 2], out_ref.at[start + i], out_sems.at[i % 2]
        )

    def fetch_row(i):
        for n in range(len(pieces)):
            fetch(i, n).start()

    copies = []
    for n, (ref, part) in enumerate(zip(new_refs, news)):
        at = block_rows // 2 if part is None else window_start(part, block_rows, flip)
        target = window.at[pl.ds(at * s_slots, ref.shape[0] * s_slots)]
        target = target.reshape(ref.shape)
        copies.append(pltpu.make_async_copy(ref, target, new_sem.at[n]))
    for copy in copies:
        copy.start()
    for i in range(min(2, count)):
        fetch_row(i)
    if first:
        window[window.shape[0] - 1] = jnp.zeros(window.shape[1:], window.dtype)
    for copy in copies:
        copy.wait()

    def one_row(i, carry):
        pltpu.make_async_copy(lefts.at[i], lefts.at[i], p_sems.at[i]).wait()

        @pl.when(i + 2 < count)
        def _():
            fetch_row(i + 2)

        @pl.when(i >= 2)
        def _():
            stored(i - 2).wait()

        left = jnp.concatenate([lefts[i, slot] for slot in range(slots)], axis=1)
        for m in range(0, kept, wide):
            right = jnp.concatenate(
                [
                    jnp.concatenate(
                        [
                            window[place_ref[start + i, k * kept + m + n]]
                            for n in range(wide)
                        ],
                        axis=1,
                    )
                    for k in range(slots)
                ],
                axis=0,
            )
            result = jnp.dot(left, right, preferred_element_type=jnp.float32)
            for n in range(wide):
                results[i % 2, m + n] = result[:, n * order : (n + 1) * order]
            store(i, m).start()
        return carry

    lax.fori_loop(0, count, one_row, 0)
    for i in range(max(0, count - 2), count):
        stored(i).wait()


def turn_pairs(count, step):
    return [(i, (i + step) % count) for i in range(count)]


def far_pieces(own):
    count = lax.axis_size("col")
    held = [own]
    if count & (count - 1):
        for step in range(1, count):
            held.append(lax.ppermute(own, "col", turn_pairs(count, step)))
        return held
    step = count // 2
    while step > 1:
        swap = [(i, i ^ step) for i in range(count)]
        held = held + [lax.ppermute(piece, "col", swap) for piece in held]
        step //= 2
    return held


def passed_pieces(pieces):
    count = lax.axis_size("col")
    if count == 1 or count & (count - 1):
        return []
    return [
        lax.ppermute(piece, "col", [(i, i ^ 1) for i in range(count)]) for piece in pieces
    ]


def steps(p_values, p_cols, s_values, s_cols, c_cols):
    block_rows, own_slots, order, _ = p_values.shape
    s_slots, kept = s_values.shape[1], c_cols.shape[1]
    reach = block_rows // 2
    row_count = lax.axis_size("row")
    first_row = lax.axis_index("row") * block_rows - reach
    if row_count % 2 == 0:
        first_pairs = [(i, (i + (1 if i % 2 else -1)) % row_count) for i in range(row_count)]
        second_pairs = [(i, i ^ 1) for i in range(row_count)]
        odd = (lax.axis_index("row") % 2).astype(jnp.int32)
        flips = jnp.stack([odd, odd])
    else:
        first_pairs, second_pairs = turn_pairs(row_count, 1), turn_pairs(row_count, -1)
        flips = jnp.arange(2, dtype=jnp.int32)
    chunks = row_chunks(block_rows)
    sides = [chunks[0]] + [(block_rows + reach - b, block_rows + reach - a) for a, b in chunks[1:]]

    parts = cut(flips, p_values, s_values, [(0, chunks[0]), (1, sides[0])])
    rest = [(0, chunk) for chunk in chunks[1:]] + [(1, side) for side in sides[1:]]
    rest = cut(flips, p_values, s_values, rest)
    own = [parts[0]] + rest[: len(sides) - 1]
    sent = [parts[1]] + rest[len(sides) - 1 :]

    far = [far_pieces(piece) for piece in own]
    halo = []
    for n, piece in enumerate(sent):
        halo.append(lax.ppermute(piece, "row", second_pairs if n else first_pairs))
    core = passed_pieces([p_values])
    far_cols = far_pieces(p_cols.T)
    passed_cols = passed_pieces(far_cols)
    first_cols = lax.ppermute(s_cols.T, "row", first_pairs)
    second_cols = lax.ppermute(s_cols.T, "row", second_pairs)

    place = pl.pallas_call(
        functools.partial(find_places, total_rows=block_rows * row_count),
        out_shape=jax.ShapeDtypeStruct(
            (block_rows, len(far_cols + passed_cols) * own_slots * kept), jnp.int32
        ),
        in_specs=[SMEM] * 5 + [VMEM] * (1 + len(far_cols + passed_cols)),
        out_specs=VMEM,
        compiler_params=pltpu.CompilerParams(vmem_limit_bytes=VMEM_GRANT),
        name="places",
    )(first_row[None], flips, first_cols, s_cols.T, second_cols, c_cols.T, *far_cols, *passed_cols)

    product = None
    window_shape = (2 * block_rows * s_slots + 1, order, order)
    for n, chunk in enumerate(chunks):
        first = product is None
        count = chunk[1] - chunk[0]
        passed = passed_pieces(far[n][1:])
        held = [(piece, False) for piece in far[n]]
        held += [(piece, True) for piece in core] + [(piece, False) for piece in passed]
        if first:
            news, arrived = [None, sides[n]], [s_values, halo[n]]
        else:
            news, arrived = [sides[n]], [halo[n]]
        inputs = [flips, place] + [in_hbm(piece) for piece, _ in held]
        inputs += [in_hbm(piece) for piece in arrived]
        specs = [SMEM] * 2 + [ANY] * (len(inputs) - 2)
        aliases = {}
        if not first:
            aliases = {len(inputs): 1, len(inputs) + 1: 0}
            inputs += [in_vmem(window), product]
            specs += [VMEM, ANY]
        product, window = pl.pallas_call(
            functools.partial(
                multiply,
                pieces=tuple(whole for _, whole in held),
                chunk=chunk,
                block_rows=block_rows,
                kept=kept,
                news=tuple(news),
                first=first,
            ),
            out_shape=[
                jax.ShapeDtypeStruct((block_rows, kept, order, order), jnp.float32),
                pltpu.VMEM(window_shape, s_values.dtype),
            ],
            in_specs=specs,
            out_specs=[ANY, VMEM],
            scratch_shapes=[
                pltpu.VMEM((count, len(held) * own_slots, order, order), p_values.dtype),
                pltpu.VMEM((2, kept, order, order), jnp.float32),
                pltpu.SemaphoreType.DMA((len(news),)),
                pltpu.SemaphoreType.DMA((count,)),
                pltpu.SemaphoreType.DMA((2,)),
            ],
            input_output_aliases=aliases,
            compiler_params=pltpu.CompilerParams(vmem_limit_bytes=VMEM_GRANT),
        )(*inputs)
    return product


def solution(mesh):
    return jax.shard_map(
        steps,
        mesh=mesh,
        in_specs=(
            P("row", "col", None, None),
            P("row", "col"),
            P("row", "col", None, None),
            P("row", "col"),
            P("row", "col"),
        ),
        out_specs=P("row", "col", None, None),
        check_vma=False,
    )
```

time: 186 us -> 107 us (0.58)
  matrix products: 85.4 us -> 0 us
  local copies, waits for them, and re-layouts: 30.8 us -> 0.05 us
  Pallas kernels: 0 us -> 29.1 us
  waiting for transfers between devices: 35.1 us -> 57.5 us
  between operations: 13.4 us -> 0.24 us
  starting transfers between devices: 10.8 us -> 19.7 us
  blocking collectives: 5.48 us -> 0 us
  other arithmetic: 4.26 us -> 0.07 us
    dot_general x2 -> x0, matrix products: 85.4 us -> none  [the longest x1 48.8 us: shards(): jnp.einsum('rklm,rklbc->rkmbc', match.astype(jnp.bfloat16), s_rows, prefe...]
    pallas_call x0 -> x7, Pallas kernels: none -> 29.1 us  [the longest x4 23.9 us: steps(): pl.pallas_call(functools.partial(multiply, pieces=tuple((whole for _, who...]
    ppermute x4 -> x18, waiting for transfers between devices: 34.3 us -> 57.5 us  [the longest x5 37.1 us: far_pieces(): held = held + [lax.ppermute(piece, 'col', swap) for piece in held]]
    gather x2 -> x0, local copies, waits for them, and re-layouts: 16.9 us -> none  [the longest x1 16.2 us: shards(): s_rows = near_values[local]]
    transpose x1 -> x0, local copies, waits for them, and re-layouts: 9.24 us -> none  [shards(): jnp.einsum('rkab,rkmbc->rmac', piece_vals, placed, preferred_element_type...]
    ppermute x4 -> x18, starting transfers between devices: 10.8 us -> 19.7 us  [the longest x5 7.32 us: far_pieces(): held = held + [lax.ppermute(piece, 'col', swap) for piece in held]]
    all_gather x1 -> x0, blocking collectives: 5.48 us -> none  [shards(): piece_cols = lax.all_gather(p_cols, 'col', axis=1, tiled=True)]
    concatenate x2 -> x0, other arithmetic: 4.21 us -> none  [with_halo(): block = jnp.concatenate([low, block, high], axis=dim)]
  transfers between devices with their start and end apart: 5 -> 18, of which waited for: 2 -> 8; matrix products, arithmetic and copies ran while one was open for 40% -> 0% of each run, Pallas kernels for 0% -> 21%
where the time goes in v1:
time: 107 us
  waiting for transfers between devices  57.5 us (54%)
  Pallas kernels  29.1 us (27%)
  starting transfers between devices  19.7 us (18%)
    ppermute x5, waiting for transfers between devices, far_pieces(): held = held + [lax.ppermute(piece, 'col', swap) for piece in held]  37.1 us
    pallas_call x4, Pallas kernels, steps(): pl.pallas_call(functools.partial(multiply, pieces=tuple((whole for _, who...  23.9 us
    ppermute x4, waiting for transfers between devices, steps(): halo.append(lax.ppermute(piece, 'row', second_pairs if n else first_pairs))  13.1 us
    ppermute x5, starting transfers between devices, far_pieces(): held = held + [lax.ppermute(piece, 'col', swap) for piece in held]  7.32 us
    ppermute x4, starting transfers between devices, steps(): halo.append(lax.ppermute(piece, 'row', second_pairs if n else first_pairs))  7.09 us
    ppermute x1, starting transfers between devices, steps(): first_cols = lax.ppermute(s_cols.T, 'row', first_pairs)  4.81 us
    pallas_call x2, Pallas kernels, cut(): pl.pallas_call(body, out_shape=shapes, in_specs=[SMEM, ANY, ANY], out_spe...  4.2 us
    ppermute x1, waiting for transfers between devices, steps(): second_cols = lax.ppermute(s_cols.T, 'row', second_pairs)  3.58 us
  transfers between devices with their start and end apart: 18, of which 8 were waited for; matrix products, arithmetic and copies ran while one was open for 0% of the time, Pallas kernels for 21%

profile of v1, /device:TPU:0, one launch (start us, length us, event | category | flops | bytes accessed | tf_op | source)
XLA Modules:
  0.0 106.6 jit_solution(2325222040472078206)
XLA Ops:
  0.0 0.0 copy-start.6
  0.0 0.0 copy-start.5
  0.0 0.1 pad_add_fusion.flip_ref.flips_ref
  0.1 2.1 %shard_map.56 = (bf16[8,4,128,128]{3,2,1,0:T(8,128)(2,1)S(1)}, bf16[8,4,128,128]{3,2,1,0:T(8,128)(2,1)S(1)}) custom-call(s32[2]{0:T(128)S(1)} %pad_add_fusion.flip_ref.flips_ref, bf16[16,4,128,128]{3,2,1,0:T(8,128)(2,1)} %refs_0_.3, bf16[16,4,128,128]{3,2,1,0:T(8,128)(2,1)} %refs_4_.1), custom_call_target="tpu_custom_call" | custom-call | tf_op jit(solution)/shard_map/pallas_call | solution.py:72
  2.2 0.0 copy-start
  2.2 3.0 %collective-permute-start.15 = (bf16[8,4,128,128]{3,2,1,0:T(8,128)(2,1)S(1)}, bf16[8,4,128,128]{3,2,1,0:T(8,128)(2,1)S(1)}, u32[]{:S(2)}, u32[]{:S(2)}) collective-permute-start(bf16[8,4,128,128]{3,2,1,0:T(8,128)(2,1)S(1)} %get-tuple-element.26.refs_0_), channel_id=1, source_target_pairs={{0,2},{1,3},{2,0},{3,1},{4,6},{5,7},{6,4},{7,5},{8,10},{9,11},{10,... | collective-permute-start | bytes 3145736 | tf_op jit(solution)/shard_map/ppermute | solution.py:226
  5.2 0.0 collective-permute-start.6
  5.3 2.1 %shard_map.55 = (bf16[4,4,128,128]{3,2,1,0:T(8,128)(2,1)S(1)}, bf16[2,4,128,128]{3,2,1,0:T(8,128)(2,1)S(1)}, bf16[2,4,128,128]{3,2,1,0:T(8,128)(2,1)S(1)}, bf16[...) custom-call(s32[2]{0:T(128)S(1)} %pad_add_fusion.flip_ref.flips_ref, ...), custom_call_target="tpu_custom_call" | custom-call | tf_op jit(solution)/shard_map/pallas_call | solution.py:72
  7.4 0.0 copy-start.1
  7.4 0.0 copy-start.2
  7.4 0.0 copy-start.3
  7.4 0.2 collective-permute-start.9
  7.6 5.0 %collective-permute-start.17 = (bf16[8,4,128,128]{3,2,1,0:T(8,128)(2,1)S(1)}, bf16[8,4,128,128]{3,2,1,0:T(8,128)(2,1)S(1)}, u32[]{:S(2)}, u32[]{:S(2)}) collective-permute-start(bf16[8,4,128,128]{3,2,1,0:T(8,128)(2,1)S(1)} %get-tuple-element.27), channel_id=1, source_target_pairs={{0,28},{4,8},{8,4},{12,16},{16,12},{20,24},{24,20},{28,0},{1,29},{... | collective-permute-start | bytes 3145736 | tf_op jit(solution)/shard_map/ppermute | solution.py:266
  12.5 16.7 %collective-permute-done.15.refs_1_ = bf16[8,4,128,128]{3,2,1,0:T(8,128)(2,1)S(1)} collective-permute-done((bf16[8,4,128,128]{3,2,1,0:T(8,128)(2,1)S(1)}, bf16[8,4,128,128]{3,2,1,0:T(8,128)(2,1)S(1)}, u32[]{:S(2)}, u32[]{:S(2)}) %collective-permute-start.15) | collective-permute-done | bytes 1048608 | tf_op jit(solution)/shard_map/ppermute | solution.py:226
  29.3 0.0 collective-permute-start.16
  29.3 0.0 copy-done.6
  29.3 2.1 %collective-permute-start.2 = (s32[4,16]{1,0:T(4,128)S(1)}, s32[4,16]{1,0:T(4,128)S(1)}, u32[]{:S(2)}, u32[]{:S(2)}) collective-permute-start(s32[4,16]{1,0:T(4,128)S(1)} %bitcast.9), channel_id=1, source_target_pairs={{0,2},{1,3},{2,0},{3,1},{4,6},{5,7},{6,4},{7,5},{8,10},{9,11},{10,... | collective-permute-start | bytes 776 | tf_op jit(solution)/shard_map/ppermute | solution.py:226
  31.4 2.7 %collective-permute-done.2.refs_1_ = s32[4,16]{1,0:T(4,128)S(1)} collective-permute-done((s32[4,16]{1,0:T(4,128)S(1)}, s32[4,16]{1,0:T(4,128)S(1)}, u32[]{:S(2)}, u32[]{:S(2)}) %collective-permute-start.2) | collective-permute-done | bytes 288 | tf_op jit(solution)/shard_map/ppermute | solution.py:226
  34.1 0.0 copy-done.5
  34.1 4.8 %collective-permute-start = (s32[4,16]{1,0:T(4,128)S(1)}, s32[4,16]{1,0:T(4,128)S(1)}, u32[]{:S(2)}, u32[]{:S(2)}) collective-permute-start(s32[4,16]{1,0:T(4,128)S(1)} %bitcast.6), channel_id=1, source_target_pairs={{0,28},{4,8},{8,4},{12,16},{16,12},{20,24},{24,20},{28,0},{1,29},{... | collective-permute-start | bytes 776 | tf_op jit(solution)/shard_map/ppermute | solution.py:270
  38.9 1.6 %collective-permute-done.near_ref = s32[4,16]{1,0:T(4,128)S(1)} collective-permute-done((s32[4,16]{1,0:T(4,128)S(1)}, s32[4,16]{1,0:T(4,128)S(1)}, u32[]{:S(2)}, u32[]{:S(2)}) %collective-permute-start) | collective-permute-done | bytes 288 | tf_op jit(solution)/shard_map/ppermute | solution.py:270
  40.4 0.0 collective-permute-start.1
  40.4 3.6 %collective-permute-done.1.far_ref = s32[4,16]{1,0:T(4,128)S(1)} collective-permute-done((s32[4,16]{1,0:T(4,128)S(1)}, s32[4,16]{1,0:T(4,128)S(1)}, u32[]{:S(2)}, u32[]{:S(2)}) %collective-permute-start.1) | collective-permute-done | bytes 288 | tf_op jit(solution)/shard_map/ppermute | solution.py:271
  44.0 0.0 collective-permute-start.3
  44.0 1.2 %collective-permute-done.3.refs_2_ = s32[4,16]{1,0:T(4,128)S(1)} collective-permute-done((s32[4,16]{1,0:T(4,128)S(1)}, s32[4,16]{1,0:T(4,128)S(1)}, u32[]{:S(2)}, u32[]{:S(2)}) %collective-permute-start.3) | collective-permute-done | bytes 288 | tf_op jit(solution)/shard_map/ppermute | solution.py:236
  45.2 0.2 collective-permute-start.4
  45.4 1.0 collective-permute-done.4.refs_3_
  46.4 1.7 %collective-permute-start.12 = (bf16[4,4,128,128]{3,2,1,0:T(8,128)(2,1)S(1)}, bf16[4,4,128,128]{3,2,1,0:T(8,128)(2,1)S(1)}, u32[]{:S(2)}, u32[]{:S(2)}) collective-permute-start(bf16[4,4,128,128]{3,2,1,0:T(8,128)(2,1)S(1)} %get-tuple-element.24.refs_0_), channel_id=1, source_target_pairs={{0,2},{1,3},{2,0},{3,1},{4,6},{5,7},{6,4},{7,5},{8,10},{9,11},{10,... | collective-permute-start | bytes 1572872 | tf_op jit(solution)/shard_map/ppermute | solution.py:226
  48.0 0.0 collective-permute-done.9.refs_1_
  48.0 0.4 collective-permute-start.5
  48.4 17.7 %collective-permute-done.5.refs_1_ = bf16[2,4,128,128]{3,2,1,0:T(8,128)(2,1)} collective-permute-done((bf16[2,4,128,128]{3,2,1,0:T(8,128)(2,1)S(1)}, bf16[2,4,128,128]{3,2,1,0:T(8,128)(2,1)}, u32[]{:S(2)}, u32[]{:S(2)}) %collective-permute-start.5) | collective-permute-done | bytes 262176 | tf_op jit(solution)/shard_map/ppermute | solution.py:226
  66.1 0.0 collective-permute-start.14
  66.1 0.0 collective-permute-done.12.refs_1_
  66.1 0.1 collective-permute-start.13
  66.2 13.0 %collective-permute-done.14.refs_4_ = bf16[4,4,128,128]{3,2,1,0:T(8,128)(2,1)S(1)} collective-permute-done((bf16[4,4,128,128]{3,2,1,0:T(8,128)(2,1)S(1)}, bf16[4,4,128,128]{3,2,1,0:T(8,128)(2,1)S(1)}, u32[]{:S(2)}, u32[]{:S(2)}) %collective-permute-start.14) | collective-permute-done | bytes 524320 | tf_op jit(solution)/shard_map/ppermute | solution.py:266
  79.2 0.3 collective-permute-start.11
  79.5 0.0 collective-permute-done.17.refs_5_
  79.5 0.0 collective-permute-start.10
  79.5 0.0 collective-permute-done.16.refs_3_
  79.5 0.0 copy-start.9
  79.5 1.8 %collective-permute-start.8 = (bf16[2,4,128,128]{3,2,1,0:T(8,128)(2,1)S(1)}, bf16[2,4,128,128]{3,2,1,0:T(8,128)(2,1)}, u32[]{:S(2)}, u32[]{:S(2)}) collective-permute-start(bf16[2,4,128,128]{3,2,1,0:T(8,128)(2,1)S(1)} %get-tuple-element.21), channel_id=1, source_target_pairs={{0,4},{4,0},{8,12},{12,8},{16,20},{20,16},{24,28},{28,24},{1,5},{5... | collective-permute-start | bytes 786440 | tf_op jit(solution)/shard_map/ppermute | solution.py:266
  81.3 0.0 copy-done.7
  81.3 0.0 collective-permute-done.6.refs_2_
  81.3 0.0 copy-done.11
  81.4 0.0 copy-done.8
  81.4 0.0 copy-done.9
  81.4 0.2 collective-permute-start.7
  81.6 0.0 copy-done.4
  81.6 1.0 places.1.place_ref
  82.6 0.0 copy-done
  82.6 9.6 %shard_map.57 = (f32[16,8,128,128]{3,2,1,0:T(8,128)}, bf16[129,128,128]{2,1,0:T(8,128)(2,1)S(1)}) custom-call(s32[2]{0:T(128)S(1)} %pad_add_fusion.flip_ref.flips_ref, s32[16,128]{1,0:T(8,128)S(1)} %places.1.place_ref, bf16[8,4,128,128]{3,2,1,0:T(8,128)(2,1)} %copy-done, bf16[8,4,128,128]{3,2,1,0:T(8,128)(2,1)} %copy-done.7, ...), custom_call_target="tpu_custom_call" | custom-call | tf_op jit(solution)/shard_map/pallas_call | solution.py:304
  92.2 0.0 collective-permute-done.13.refs_3_
  92.2 0.0 copy-done.1
  92.2 0.0 copy-done.10
  92.3 5.8 %shard_map.58 = (f32[16,8,128,128]{3,2,1,0:T(8,128)}, bf16[129,128,128]{2,1,0:T(8,128)(2,1)S(1)}) custom-call(s32[2]{0:T(128)S(1)} %pad_add_fusion.flip_ref.flips_ref, s32[16,128]{1,0:T(8,128)S(1)} %places.1.place_ref, bf16[4,4,128,128]{3,2,1,0:T(8,128)(2,1)} %copy-done.1, ...), custom_call_target="tpu_custom_call", output_to_operand_aliasing={{1}: (7, {}), {0}: (8, {})} | custom-call | tf_op jit(solution)/shard_map/pallas_call | solution.py:304
  98.1 0.0 copy-done.2
  98.1 0.0 copy-done.3
  98.1 0.0 collective-permute-done.11.refs_4_
  98.1 0.0 collective-permute-done.10.refs_3_
  98.1 0.0 copy-done.12
  98.1 4.2 %shard_map.59 = (f32[16,8,128,128]{3,2,1,0:T(8,128)}, bf16[129,128,128]{2,1,0:T(8,128)(2,1)S(1)}) custom-call(s32[2]{0:T(128)S(1)} %pad_add_fusion.flip_ref.flips_ref, s32[16,128]{1,0:T(8,128)S(1)} %places.1.place_ref, bf16[2,4,128,128]{3,2,1,0:T(8,128)(2,1)} %copy-done.3, ...), custom_call_target="tpu_custom_call", output_to_operand_aliasing={{1}: (7, {}), {0}: (8, {})} | custom-call | tf_op jit(solution)/shard_map/pallas_call | solution.py:304
  102.4 0.0 collective-permute-done.8.refs_4_
  102.4 0.0 collective-permute-done.7.refs_3_
  102.4 4.2 %shard_map.60 = (f32[16,8,128,128]{3,2,1,0:T(8,128)}, bf16[129,128,128]{2,1,0:T(8,128)(2,1)S(1)}) custom-call(s32[2]{0:T(128)S(1)} %pad_add_fusion.flip_ref.flips_ref, s32[16,128]{1,0:T(8,128)S(1)} %places.1.place_ref, bf16[2,4,128,128]{3,2,1,0:T(8,128)(2,1)} %copy-done.2, ...), custom_call_target="tpu_custom_call", output_to_operand_aliasing={{1}: (7, {}), {0}: (8, {})} | custom-call | tf_op jit(solution)/shard_map/pallas_call | solution.py:304
  (6 shorter events, 0.0 us)
Async XLA Ops:
  0.0 29.3 %copy-start.6 = (s32[16,4]{0,1:T(4,128)S(1)}, s32[16,4]{0,1:T(4,128)}, u32[]{:S(2)}) copy-start(s32[16,4]{0,1:T(4,128)} %param.6) | copy-start | bytes 772
  0.0 34.1 %copy-start.5 = (s32[16,4]{0,1:T(4,128)S(1)}, s32[16,4]{0,1:T(4,128)}, u32[]{:S(2)}) copy-start(s32[16,4]{0,1:T(4,128)} %param.8) | copy-start | bytes 772
  0.0 81.6 %copy-start.4 = (s32[16,8]{0,1:T(8,128)S(1)}, s32[16,8]{0,1:T(8,128)}, u32[]{:S(2)}) copy-start(s32[16,8]{0,1:T(8,128)} %param.9) | copy-start | bytes 1540
  2.2 80.4 %copy-start = (bf16[8,4,128,128]{3,2,1,0:T(8,128)(2,1)}, bf16[8,4,128,128]{3,2,1,0:T(8,128)(2,1)S(1)}, u32[]{:S(2)}) copy-start(bf16[8,4,128,128]{3,2,1,0:T(8,128)(2,1)S(1)} %get-tuple-element.26.refs_0_) | copy-start | bytes 3145732
  2.2 27.1 %collective-permute-start.15 = (bf16[8,4,128,128]{3,2,1,0:T(8,128)(2,1)S(1)}, bf16[8,4,128,128]{3,2,1,0:T(8,128)(2,1)S(1)}, u32[]{:S(2)}, u32[]{:S(2)}) collective-permute-start(bf16[8,4,128,128]{3,2,1,0:T(8,128)(2,1)S(1)} %get-tuple-element.26.refs_0_), channel_id=1, source_target_pairs={{0,2},{1,3},{2,0},{3,1},{4,6},{5,7},{6,4},{7,5},{8,10},{9,11},{10,... | collective-permute-start | bytes 3145736 | tf_op jit(solution)/shard_map/ppermute | solution.py:226
  5.2 76.1 %collective-permute-start.6 = (bf16[16,4,128,128]{3,2,1,0:T(8,128)(2,1)}, bf16[16,4,128,128]{3,2,1,0:T(8,128)(2,1)}, u32[]{:S(2)}, u32[]{:S(2)}) collective-permute-start(bf16[16,4,128,128]{3,2,1,0:T(8,128)(2,1)} %refs_0_.3), channel_id=1, source_target_pairs={{0,1},{1,0},{2,3},{3,2},{4,5},{5,4},{6,7},{7,6},{8,9},{9,8},{10,11... | collective-permute-start | bytes 6291464 | tf_op jit(solution)/shard_map/ppermute | solution.py:236
  7.4 84.9 %copy-start.1 = (bf16[4,4,128,128]{3,2,1,0:T(8,128)(2,1)}, bf16[4,4,128,128]{3,2,1,0:T(8,128)(2,1)S(1)}, u32[]{:S(2)}) copy-start(bf16[4,4,128,128]{3,2,1,0:T(8,128)(2,1)S(1)} %get-tuple-element.24.refs_0_) | copy-start | bytes 1572868
  7.4 90.7 %copy-start.2 = (bf16[2,4,128,128]{3,2,1,0:T(8,128)(2,1)}, bf16[2,4,128,128]{3,2,1,0:T(8,128)(2,1)S(1)}, u32[]{:S(2)}) copy-start(bf16[2,4,128,128]{3,2,1,0:T(8,128)(2,1)S(1)} %get-tuple-element.20.refs_0_) | copy-start | bytes 786436
  7.4 90.7 %copy-start.3 = (bf16[2,4,128,128]{3,2,1,0:T(8,128)(2,1)}, bf16[2,4,128,128]{3,2,1,0:T(8,128)(2,1)S(1)}, u32[]{:S(2)}) copy-start(bf16[2,4,128,128]{3,2,1,0:T(8,128)(2,1)S(1)} %get-tuple-element.22.refs_0_) | copy-start | bytes 786436
  7.4 40.6 %collective-permute-start.9 = (bf16[2,4,128,128]{3,2,1,0:T(8,128)(2,1)S(1)}, bf16[2,4,128,128]{3,2,1,0:T(8,128)(2,1)S(1)}, u32[]{:S(2)}, u32[]{:S(2)}) collective-permute-start(bf16[2,4,128,128]{3,2,1,0:T(8,128)(2,1)S(1)} %get-tuple-element.22.refs_0_), channel_id=1, source_target_pairs={{0,2},{1,3},{2,0},{3,1},{4,6},{5,7},{6,4},{7,5},{8,10},{9,11},{10,... | collective-permute-start | bytes 786440 | tf_op jit(solution)/shard_map/ppermute | solution.py:226
  7.6 72.0 %collective-permute-start.17 = (bf16[8,4,128,128]{3,2,1,0:T(8,128)(2,1)S(1)}, bf16[8,4,128,128]{3,2,1,0:T(8,128)(2,1)S(1)}, u32[]{:S(2)}, u32[]{:S(2)}) collective-permute-start(bf16[8,4,128,128]{3,2,1,0:T(8,128)(2,1)S(1)} %get-tuple-element.27), channel_id=1, source_target_pairs={{0,28},{4,8},{8,4},{12,16},{16,12},{20,24},{24,20},{28,0},{1,29},{... | collective-permute-start | bytes 3145736 | tf_op jit(solution)/shard_map/ppermute | solution.py:266
  29.3 52.1 %copy-start.7 = (bf16[8,4,128,128]{3,2,1,0:T(8,128)(2,1)}, bf16[8,4,128,128]{3,2,1,0:T(8,128)(2,1)S(1)}, u32[]{:S(2)}) copy-start(bf16[8,4,128,128]{3,2,1,0:T(8,128)(2,1)S(1)} %collective-permute-done.15.refs_1_) | copy-start | bytes 3145732
  29.3 50.3 %collective-permute-start.16 = (bf16[8,4,128,128]{3,2,1,0:T(8,128)(2,1)S(1)}, bf16[8,4,128,128]{3,2,1,0:T(8,128)(2,1)S(1)}, u32[]{:S(2)}, u32[]{:S(2)}) collective-permute-start(bf16[8,4,128,128]{3,2,1,0:T(8,128)(2,1)S(1)} %collective-permute-done.15.refs_1_), channel_id=1, source_target_pairs={{0,1},{1,0},{2,3},{3,2},{4,5},{5,4},{6,7},{7,6},{8,9},{9,8},{10,11... | collective-permute-start | bytes 3145736 | tf_op jit(solution)/shard_map/ppermute | solution.py:236
  29.3 4.8 %collective-permute-start.2 = (s32[4,16]{1,0:T(4,128)S(1)}, s32[4,16]{1,0:T(4,128)S(1)}, u32[]{:S(2)}, u32[]{:S(2)}) collective-permute-start(s32[4,16]{1,0:T(4,128)S(1)} %bitcast.9), channel_id=1, source_target_pairs={{0,2},{1,3},{2,0},{3,1},{4,6},{5,7},{6,4},{7,5},{8,10},{9,11},{10,... | collective-permute-start | bytes 776 | tf_op jit(solution)/shard_map/ppermute | solution.py:226
  34.1 6.4 %collective-permute-start = (s32[4,16]{1,0:T(4,128)S(1)}, s32[4,16]{1,0:T(4,128)S(1)}, u32[]{:S(2)}, u32[]{:S(2)}) collective-permute-start(s32[4,16]{1,0:T(4,128)S(1)} %bitcast.6), channel_id=1, source_target_pairs={{0,28},{4,8},{8,4},{12,16},{16,12},{20,24},{24,20},{28,0},{1,29},{... | collective-permute-start | bytes 776 | tf_op jit(solution)/shard_map/ppermute | solution.py:270
  40.4 3.6 %collective-permute-start.1 = (s32[4,16]{1,0:T(4,128)S(1)}, s32[4,16]{1,0:T(4,128)S(1)}, u32[]{:S(2)}, u32[]{:S(2)}) collective-permute-start(s32[4,16]{1,0:T(4,128)S(1)} %bitcast.7), channel_id=1, source_target_pairs={{0,4},{4,0},{8,12},{12,8},{16,20},{20,16},{24,28},{28,24},{1,5},{5... | collective-permute-start | bytes 776 | tf_op jit(solution)/shard_map/ppermute | solution.py:271
  44.0 1.2 %collective-permute-start.3 = (s32[4,16]{1,0:T(4,128)S(1)}, s32[4,16]{1,0:T(4,128)S(1)}, u32[]{:S(2)}, u32[]{:S(2)}) collective-permute-start(s32[4,16]{1,0:T(4,128)S(1)} %bitcast.10), channel_id=1, source_target_pairs={{0,1},{1,0},{2,3},{3,2},{4,5},{5,4},{6,7},{7,6},{8,9},{9,8},{10,11... | collective-permute-start | bytes 776 | tf_op jit(solution)/shard_map/ppermute | solution.py:236
  45.2 1.2 %collective-permute-start.4 = (s32[4,16]{1,0:T(4,128)S(1)}, s32[4,16]{1,0:T(4,128)S(1)}, u32[]{:S(2)}, u32[]{:S(2)}) collective-permute-start(s32[4,16]{1,0:T(4,128)S(1)} %collective-permute-done.2.refs_1_), channel_id=1, source_target_pairs={{0,1},{1,0},{2,3},{3,2},{4,5},{5,4},{6,7},{7,6},{8,9},{9,8},{10,11... | collective-permute-start | bytes 776 | tf_op jit(solution)/shard_map/ppermute | solution.py:236
  46.4 19.7 %collective-permute-start.12 = (bf16[4,4,128,128]{3,2,1,0:T(8,128)(2,1)S(1)}, bf16[4,4,128,128]{3,2,1,0:T(8,128)(2,1)S(1)}, u32[]{:S(2)}, u32[]{:S(2)}) collective-permute-start(bf16[4,4,128,128]{3,2,1,0:T(8,128)(2,1)S(1)} %get-tuple-element.24.refs_0_), channel_id=1, source_target_pairs={{0,2},{1,3},{2,0},{3,1},{4,6},{5,7},{6,4},{7,5},{8,10},{9,11},{10,... | collective-permute-start | bytes 1572872 | tf_op jit(solution)/shard_map/ppermute | solution.py:226
  48.0 50.1 %copy-start.12 = (bf16[2,4,128,128]{3,2,1,0:T(8,128)(2,1)}, bf16[2,4,128,128]{3,2,1,0:T(8,128)(2,1)S(1)}, u32[]{:S(2)}) copy-start(bf16[2,4,128,128]{3,2,1,0:T(8,128)(2,1)S(1)} %collective-permute-done.9.refs_1_) | copy-start | bytes 786436
  48.0 18.1 %collective-permute-start.5 = (bf16[2,4,128,128]{3,2,1,0:T(8,128)(2,1)S(1)}, bf16[2,4,128,128]{3,2,1,0:T(8,128)(2,1)}, u32[]{:S(2)}, u32[]{:S(2)}) collective-permute-start(bf16[2,4,128,128]{3,2,1,0:T(8,128)(2,1)S(1)} %get-tuple-element.20.refs_0_), channel_id=1, source_target_pairs={{0,2},{1,3},{2,0},{3,1},{4,6},{5,7},{6,4},{7,5},{8,10},{9,11},{10,... | collective-permute-start | bytes 786440 | tf_op jit(solution)/shard_map/ppermute | solution.py:226
  66.1 13.1 %collective-permute-start.14 = (bf16[4,4,128,128]{3,2,1,0:T(8,128)(2,1)S(1)}, bf16[4,4,128,128]{3,2,1,0:T(8,128)(2,1)S(1)}, u32[]{:S(2)}, u32[]{:S(2)}) collective-permute-start(bf16[4,4,128,128]{3,2,1,0:T(8,128)(2,1)S(1)} %get-tuple-element.25), channel_id=1, source_target_pairs={{0,4},{4,0},{8,12},{12,8},{16,20},{20,16},{24,28},{28,24},{1,5},{5... | collective-permute-start | bytes 1572872 | tf_op jit(solution)/shard_map/ppermute | solution.py:266
  66.1 26.2 %copy-start.10 = (bf16[4,4,128,128]{3,2,1,0:T(8,128)(2,1)}, bf16[4,4,128,128]{3,2,1,0:T(8,128)(2,1)S(1)}, u32[]{:S(2)}) copy-start(bf16[4,4,128,128]{3,2,1,0:T(8,128)(2,1)S(1)} %collective-permute-done.12.refs_1_) | copy-start | bytes 1572868
  66.1 26.1 %collective-permute-start.13 = (bf16[4,4,128,128]{3,2,1,0:T(8,128)(2,1)S(1)}, bf16[4,4,128,128]{3,2,1,0:T(8,128)(2,1)}, u32[]{:S(2)}, u32[]{:S(2)}) collective-permute-start(bf16[4,4,128,128]{3,2,1,0:T(8,128)(2,1)S(1)} %collective-permute-done.12.refs_1_), channel_id=1, source_target_pairs={{0,1},{1,0},{2,3},{3,2},{4,5},{5,4},{6,7},{7,6},{8,9},{9,8},{10,11... | collective-permute-start | bytes 1572872 | tf_op jit(solution)/shard_map/ppermute | solution.py:236
  79.2 2.1 %copy-start.11 = (bf16[4,4,128,128]{3,2,1,0:T(8,128)(2,1)}, bf16[4,4,128,128]{3,2,1,0:T(8,128)(2,1)S(1)}, u32[]{:S(2)}) copy-start(bf16[4,4,128,128]{3,2,1,0:T(8,128)(2,1)S(1)} %collective-permute-done.14.refs_4_) | copy-start | bytes 1572868
  79.2 18.9 %collective-permute-start.11 = (bf16[2,4,128,128]{3,2,1,0:T(8,128)(2,1)S(1)}, bf16[2,4,128,128]{3,2,1,0:T(8,128)(2,1)}, u32[]{:S(2)}, u32[]{:S(2)}) collective-permute-start(bf16[2,4,128,128]{3,2,1,0:T(8,128)(2,1)S(1)} %get-tuple-element.23), channel_id=1, source_target_pairs={{0,4},{4,0},{8,12},{12,8},{16,20},{20,16},{24,28},{28,24},{1,5},{5... | collective-permute-start | bytes 786440 | tf_op jit(solution)/shard_map/ppermute | solution.py:266
  79.5 1.9 %copy-start.8 = (bf16[8,4,128,128]{3,2,1,0:T(8,128)(2,1)}, bf16[8,4,128,128]{3,2,1,0:T(8,128)(2,1)S(1)}, u32[]{:S(2)}) copy-start(bf16[8,4,128,128]{3,2,1,0:T(8,128)(2,1)S(1)} %collective-permute-done.17.refs_5_) | copy-start | bytes 3145732
  79.5 18.6 %collective-permute-start.10 = (bf16[2,4,128,128]{3,2,1,0:T(8,128)(2,1)S(1)}, bf16[2,4,128,128]{3,2,1,0:T(8,128)(2,1)}, u32[]{:S(2)}, u32[]{:S(2)}) collective-permute-start(bf16[2,4,128,128]{3,2,1,0:T(8,128)(2,1)S(1)} %collective-permute-done.9.refs_1_), channel_id=1, source_target_pairs={{0,1},{1,0},{2,3},{3,2},{4,5},{5,4},{6,7},{7,6},{8,9},{9,8},{10,11... | collective-permute-start | bytes 786440 | tf_op jit(solution)/shard_map/ppermute | solution.py:236
  79.5 1.8 %copy-start.9 = (bf16[8,4,128,128]{3,2,1,0:T(8,128)(2,1)}, bf16[8,4,128,128]{3,2,1,0:T(8,128)(2,1)S(1)}, u32[]{:S(2)}) copy-start(bf16[8,4,128,128]{3,2,1,0:T(8,128)(2,1)S(1)} %collective-permute-done.16.refs_3_) | copy-start | bytes 3145732
  79.5 22.9 %collective-permute-start.8 = (bf16[2,4,128,128]{3,2,1,0:T(8,128)(2,1)S(1)}, bf16[2,4,128,128]{3,2,1,0:T(8,128)(2,1)}, u32[]{:S(2)}, u32[]{:S(2)}) collective-permute-start(bf16[2,4,128,128]{3,2,1,0:T(8,128)(2,1)S(1)} %get-tuple-element.21), channel_id=1, source_target_pairs={{0,4},{4,0},{8,12},{12,8},{16,20},{20,16},{24,28},{28,24},{1,5},{5... | collective-permute-start | bytes 786440 | tf_op jit(solution)/shard_map/ppermute | solution.py:266
  81.4 21.0 %collective-permute-start.7 = (bf16[2,4,128,128]{3,2,1,0:T(8,128)(2,1)}, bf16[2,4,128,128]{3,2,1,0:T(8,128)(2,1)}, u32[]{:S(2)}, u32[]{:S(2)}) collective-permute-start(bf16[2,4,128,128]{3,2,1,0:T(8,128)(2,1)} %collective-permute-done.5.refs_1_), channel_id=1, source_target_pairs={{0,1},{1,0},{2,3},{3,2},{4,5},{5,4},{6,7},{7,6},{8,9},{9,8},{10,11... | collective-permute-start | bytes 786440 | tf_op jit(solution)/shard_map/ppermute | solution.py:236

commit v2 on v1

--- a/solution.py
+++ b/solution.py
@@ -8,6 +8,7 @@
 from jax.sharding import PartitionSpec as P
 
 VMEM_GRANT = 16 << 20
+SECOND_EIGHTHS = (5, 3)
 ANY = pl.BlockSpec(memory_space=pl.ANY)
 SMEM = pl.BlockSpec(memory_space=pltpu.SMEM)
 VMEM = pl.BlockSpec(memory_space=pltpu.VMEM)
@@ -23,11 +24,25 @@
 
 def row_chunks(block_rows):
     reach = block_rows // 2
-    edges = [0, reach]
-    for left in (reach // 2, reach // 4, 0):
-        if block_rows - left > edges[-1]:
-            edges.append(block_rows - left)
-    return list(zip(edges[:-1], edges[1:]))
+    middle = reach // 2
+    chunks = [(middle, reach), (0, middle)] if middle else [(0, reach)]
+    start = reach
+    for eighths in SECOND_EIGHTHS:
+        stop = min(block_rows, start + max(1, eighths * reach // 8))
+        if start < stop:
+            chunks.append((start, stop))
+            start = stop
+    if start < block_rows:
+        chunks.append((start, block_rows))
+    return chunks
+
+
+def halo_part(chunk, block_rows):
+    start, stop = chunk
+    reach = block_rows // 2
+    if start < reach:
+        return reach - stop, reach - start
+    return block_rows + reach - stop, block_rows + reach - start
 
 
 def local_start(part, block_rows, flip):
@@ -80,8 +95,9 @@
     )
 
 
-def find_places(first_ref, flip_ref, near_ref, own_ref, far_ref, kept_ref, *refs, total_rows):
-    p_refs, place_ref = refs[:-1], refs[-1]
+def find_places(first_ref, flip_ref, own_ref, near_ref, *refs, total_rows, both):
+    far_ref = refs[0] if both else None
+    kept_ref, *p_refs, place_ref = refs[1 if both else 0 :]
     kept, block_rows = kept_ref.shape
     s_slots, reach = own_ref.shape[0], block_rows // 2
     shape = place_ref.shape
@@ -109,35 +125,42 @@
     for q in range(2 * block_rows):
         here = local == q
         for slot in range(s_slots):
-            if q < reach:
-                near, far = near_ref[slot, q + reach], far_ref[slot, q + reach]
-                col = jnp.where(flipped, far, near)
-            elif q < reach + block_rows:
+            if reach <= q < reach + block_rows:
                 col = own_ref[slot, q - reach]
             else:
-                row = q - reach - block_rows
-                col = jnp.where(flipped, near_ref[slot, row], far_ref[slot, row])
+                row = q + reach if q < reach else q - reach - block_rows
+                far = far_ref[slot, row] if both else jnp.int32(-1)
+                low_near = (q < reach) != flipped
+                col = jnp.where(low_near, near_ref[slot, row], far)
             place = jnp.where(here & (wanted == col), q * s_slots + slot, place)
     place_ref[...] = place
 
 
-def multiply(flip_ref, place_ref, *refs, pieces, chunk, block_rows, kept, news, first):
-    p_refs = refs[: len(pieces)]
-    new_refs = refs[len(pieces) : len(pieces) + len(news)]
-    rest = refs[len(pieces) + len(news) + (0 if first else 2) :]
-    out_ref, window, lefts, results, new_sem, p_sems, out_sems = rest
-    flip = flip_ref[0]
+def multiply(*refs, kinds, chunk, ahead, block_rows, kept, news, first):
+    refs = list(refs)
+    take = lambda count: [refs.pop(0) for _ in range(count)]
+    flips_ref, place_ref = take(2)
+    p_refs, new_refs = take(len(kinds)), take(len(news))
+    take(0 if first else 2)
+    ahead_refs = take(kinds.count("fetch") if ahead else 0)
+    out_ref, window = take(2)
+    next_ref = take(1)[0] if ahead else None
+    lefts = take(1)[0] if first else None
+    results, new_sem, p_sems, out_sems, next_sem = refs
+    flip = flips_ref[0]
     start = local_start(chunk, block_rows, flip)
     count = chunk[1] - chunk[0]
-    slots, s_slots = lefts.shape[1], (window.shape[0] - 1) // (2 * block_rows)
-    own_slots = slots // len(pieces)
+    s_slots = (window.shape[0] - 1) // (2 * block_rows)
+    own_slots = place_ref.shape[1] // (kept * len(kinds))
     wide = max(w for w in (4, 2, 1) if kept % w == 0)
     order = window.shape[1]
+    slots = own_slots * len(kinds)
+    fetched = [n for n, kind in enumerate(kinds) if kind == "fetch"]
 
     def fetch(i, n):
         return pltpu.make_async_copy(
-            p_refs[n].at[start + i if pieces[n] else i],
-            lefts.at[i, pl.ds(n * own_slots, own_slots)],
+            p_refs[n].at[i if n == 0 else start + i],
+            lefts.at[i, pl.ds(fetched.index(n) * own_slots, own_slots)],
             p_sems.at[i],
         )
 
@@ -153,37 +176,60 @@
             results.at[i % 2], out_ref.at[start + i], out_sems.at[i % 2]
         )
 
-    def fetch_row(i):
-        for n in range(len(pieces)):
-            fetch(i, n).start()
-
-    copies = []
+    def left_blocks(i):
+        for n, ref in enumerate(p_refs):
+            for slot in range(own_slots):
+                if kinds[n] != "fetch":
+                    yield ref[i, slot]
+                else:
+                    source = lefts if first else p_refs[0]
+                    yield source[i, fetched.index(n) * own_slots + slot]
+
+    copies, moves = [], []
     for n, (ref, part) in enumerate(zip(new_refs, news)):
         at = block_rows // 2 if part is None else window_start(part, block_rows, flip)
-        target = window.at[pl.ds(at * s_slots, ref.shape[0] * s_slots)]
-        target = target.reshape(ref.shape)
-        copies.append(pltpu.make_async_copy(ref, target, new_sem.at[n]))
+        if first:
+            target = window.at[pl.ds(at * s_slots, ref.shape[0] * s_slots)]
+            target = target.reshape(ref.shape)
+            copies.append(pltpu.make_async_copy(ref, target, new_sem.at[n]))
+        else:
+            moves.append((ref, at))
     for copy in copies:
         copy.start()
-    for i in range(min(2, count)):
-        fetch_row(i)
     if first:
+        for i in range(count):
+            for n in fetched:
+                fetch(i, n).start()
         window[window.shape[0] - 1] = jnp.zeros(window.shape[1:], window.dtype)
+    if ahead:
+        next_start = local_start(ahead, block_rows, flip)
+        next_count = ahead[1] - ahead[0]
+        later = [
+            pltpu.make_async_copy(
+                ref.at[pl.ds(next_start if n else 0, next_count)],
+                next_ref.at[:, pl.ds(n * own_slots, own_slots)],
+                next_sem.at[n],
+            )
+            for n, ref in enumerate(ahead_refs)
+        ]
+        for copy in later:
+            copy.start()
+    for ref, at in moves:
+        for row in range(ref.shape[0]):
+            for slot in range(s_slots):
+                window[(at + row) * s_slots + slot] = ref[row, slot]
     for copy in copies:
         copy.wait()
 
     def one_row(i, carry):
-        pltpu.make_async_copy(lefts.at[i], lefts.at[i], p_sems.at[i]).wait()
-
-        @pl.when(i + 2 < count)
-        def _():
-            fetch_row(i + 2)
+        if first:
+            pltpu.make_async_copy(lefts.at[i], lefts.at[i], p_sems.at[i]).wait()
 
         @pl.when(i >= 2)
         def _():
             stored(i - 2).wait()
 
-        left = jnp.concatenate([lefts[i, slot] for slot in range(slots)], axis=1)
+        left = jnp.concatenate(list(left_blocks(i)), axis=1)
         for m in range(0, kept, wide):
             right = jnp.concatenate(
                 [
@@ -207,6 +253,9 @@
     lax.fori_loop(0, count, one_row, 0)
     for i in range(max(0, count - 2), count):
         stored(i).wait()
+    if ahead:
+        for copy in later:
+            copy.wait()
 
 
 def turn_pairs(count, step):
@@ -252,81 +301,112 @@
         first_pairs, second_pairs = turn_pairs(row_count, 1), turn_pairs(row_count, -1)
         flips = jnp.arange(2, dtype=jnp.int32)
     chunks = row_chunks(block_rows)
-    sides = [chunks[0]] + [(block_rows + reach - b, block_rows + reach - a) for a, b in chunks[1:]]
-
-    parts = cut(flips, p_values, s_values, [(0, chunks[0]), (1, sides[0])])
-    rest = [(0, chunk) for chunk in chunks[1:]] + [(1, side) for side in sides[1:]]
-    rest = cut(flips, p_values, s_values, rest)
-    own = [parts[0]] + rest[: len(sides) - 1]
-    sent = [parts[1]] + rest[len(sides) - 1 :]
+    sides = [halo_part(chunk, block_rows) for chunk in chunks]
+
+    lead = next(n for n, chunk in enumerate(chunks) if chunk[0] >= reach)
+    wanted = [(0, chunk) for chunk in chunks] + [(1, side) for side in sides]
+    early = [0, len(chunks) + lead, len(chunks)]
+    late = [n for n in range(len(wanted)) if n not in early]
+    pieces = dict(zip(early, cut(flips, p_values, s_values, [wanted[n] for n in early])))
+    pieces |= zip(late, cut(flips, p_values, s_values, [wanted[n] for n in late]))
+    own = [pieces[n] for n in range(len(chunks))]
+    sent = [pieces[len(chunks) + n] for n in range(len(chunks))]
 
     far = [far_pieces(piece) for piece in own]
     halo = []
     for n, piece in enumerate(sent):
-        halo.append(lax.ppermute(piece, "row", second_pairs if n else first_pairs))
+        pairs = first_pairs if chunks[n][0] < reach else second_pairs
+        halo.append(lax.ppermute(piece, "row", pairs))
     core = passed_pieces([p_values])
     far_cols = far_pieces(p_cols.T)
     passed_cols = passed_pieces(far_cols)
     first_cols = lax.ppermute(s_cols.T, "row", first_pairs)
     second_cols = lax.ppermute(s_cols.T, "row", second_pairs)
 
-    place = pl.pallas_call(
-        functools.partial(find_places, total_rows=block_rows * row_count),
-        out_shape=jax.ShapeDtypeStruct(
-            (block_rows, len(far_cols + passed_cols) * own_slots * kept), jnp.int32
-        ),
-        in_specs=[SMEM] * 5 + [VMEM] * (1 + len(far_cols + passed_cols)),
-        out_specs=VMEM,
-        compiler_params=pltpu.CompilerParams(vmem_limit_bytes=VMEM_GRANT),
-        name="places",
-    )(first_row[None], flips, first_cols, s_cols.T, second_cols, c_cols.T, *far_cols, *passed_cols)
-
-    product = None
+    col_pieces = far_cols + passed_cols
+
+    def places(both):
+        tables = [first_row[None], flips, s_cols.T, first_cols] + ([second_cols] if both else [])
+        return pl.pallas_call(
+            functools.partial(find_places, total_rows=block_rows * row_count, both=both),
+            out_shape=jax.ShapeDtypeStruct(
+                (block_rows, len(col_pieces) * own_slots * kept), jnp.int32
+            ),
+            in_specs=[SMEM] * len(tables) + [VMEM] * (1 + len(col_pieces)),
+            out_specs=VMEM,
+            compiler_params=pltpu.CompilerParams(vmem_limit_bytes=VMEM_GRANT),
+        )(*tables, c_cols.T, *col_pieces)
+
+    place_of = [places(False), places(True)]
+
+    product = window = ready = None
     window_shape = (2 * block_rows * s_slots + 1, order, order)
+    fetches = 1 + len(core)
     for n, chunk in enumerate(chunks):
         first = product is None
         count = chunk[1] - chunk[0]
+        ahead = chunks[n + 1] if n + 1 < len(chunks) else None
         passed = passed_pieces(far[n][1:])
-        held = [(piece, False) for piece in far[n]]
-        held += [(piece, True) for piece in core] + [(piece, False) for piece in passed]
+        kinds = ["fetch"] + ["here"] * len(far[n][1:]) + ["fetch"] * len(core)
+        kinds += ["here"] * len(passed)
+        fetch_from = [far[n][0]] + core
+        here = far[n][1:] + passed
+        inputs, specs = [flips, place_of[chunk[0] >= reach]], [SMEM] * 2
+        for kind in kinds:
+            if kind == "here":
+                inputs.append(in_vmem(here.pop(0)))
+            else:
+                inputs.append(in_hbm(fetch_from.pop(0)) if first else ready)
+            specs.append(ANY if first and kind == "fetch" else VMEM)
+        aliases = {}
         if first:
-            news, arrived = [None, sides[n]], [s_values, halo[n]]
+            news = [None, sides[n]]
+            inputs += [in_hbm(s_values), in_hbm(halo[n])]
+            specs += [ANY] * 2
         else:
-            news, arrived = [sides[n]], [halo[n]]
-        inputs = [flips, place] + [in_hbm(piece) for piece, _ in held]
-        inputs += [in_hbm(piece) for piece in arrived]
-        specs = [SMEM] * 2 + [ANY] * (len(inputs) - 2)
-        aliases = {}
-        if not first:
+            news = [sides[n]]
+            inputs.append(in_vmem(halo[n]))
+            specs.append(VMEM)
             aliases = {len(inputs): 1, len(inputs) + 1: 0}
             inputs += [in_vmem(window), product]
             specs += [VMEM, ANY]
-        product, window = pl.pallas_call(
+        outs = [
+            jax.ShapeDtypeStruct((block_rows, kept, order, order), jnp.float32),
+            pltpu.VMEM(window_shape, s_values.dtype),
+        ]
+        if ahead:
+            inputs += [in_hbm(own[n + 1])] + [in_hbm(piece) for piece in core]
+            specs += [ANY] * fetches
+            shape = (ahead[1] - ahead[0], fetches * own_slots, order, order)
+            outs.append(pltpu.VMEM(shape, p_values.dtype))
+        scratch = [
+            pltpu.VMEM((2, kept, order, order), jnp.float32),
+            pltpu.SemaphoreType.DMA((2,)),
+            pltpu.SemaphoreType.DMA((count,)),
+            pltpu.SemaphoreType.DMA((2,)),
+            pltpu.SemaphoreType.DMA((fetches,)),
+        ]
+        if first:
+            scratch.insert(0, pltpu.VMEM((count, fetches * own_slots, order, order), p_values.dtype))
+        product, window, *more = pl.pallas_call(
             functools.partial(
                 multiply,
-                pieces=tuple(whole for _, whole in held),
+                kinds=tuple(kinds),
                 chunk=chunk,
+                ahead=ahead,
                 block_rows=block_rows,
                 kept=kept,
                 news=tuple(news),
                 first=first,
             ),
-            out_shape=[
-                jax.ShapeDtypeStruct((block_rows, kept, order, order), jnp.float32),
-                pltpu.VMEM(window_shape, s_values.dtype),
-            ],
+            out_shape=outs,
             in_specs=specs,
-            out_specs=[ANY, VMEM],
-            scratch_shapes=[
-                pltpu.VMEM((count, len(held) * own_slots, order, order), p_values.dtype),
-                pltpu.VMEM((2, kept, order, order), jnp.float32),
-                pltpu.SemaphoreType.DMA((len(news),)),
-                pltpu.SemaphoreType.DMA((count,)),
-                pltpu.SemaphoreType.DMA((2,)),
-            ],
+            out_specs=[ANY] + [VMEM] * (len(outs) - 1),
+            scratch_shapes=scratch,
             input_output_aliases=aliases,
             compiler_params=pltpu.CompilerParams(vmem_limit_bytes=VMEM_GRANT),
         )(*inputs)
+        ready = in_vmem(more[0]) if ahead else None
     return product
 
 

time: 107 us -> 99.5 us (0.930)
  waiting for transfers between devices: 57.5 us -> 40.2 us
  local copies, waits for them, and re-layouts: 0.05 us -> 11.3 us
    ppermute x5, waiting for transfers between devices: 37.1 us -> 22.9 us  [far_pieces(): held = held + [lax.ppermute(piece, 'col', swap) for piece in held]]
    ppermute x4, waiting for transfers between devices: 13.1 us -> 0.01 us  [steps(): halo.append(lax.ppermute(piece, 'row', pairs))]
    unnamed x26 -> x48, local copies, waits for them, and re-layouts: 0.05 us -> 11.3 us
    ppermute x1, waiting for transfers between devices: 1.56 us -> 12.1 us  [steps(): first_cols = lax.ppermute(s_cols.T, 'row', first_pairs)]
    ppermute x1, starting transfers between devices: 4.81 us -> 0.02 us  [steps(): first_cols = lax.ppermute(s_cols.T, 'row', first_pairs)]
    ppermute x4, starting transfers between devices: 7.09 us -> 11.5 us  [steps(): halo.append(lax.ppermute(piece, 'row', pairs))]
    pallas_call x5 -> x6, Pallas kernels: 24.9 us -> 22.6 us  [the longest x4 20.6 us: steps(): pl.pallas_call(functools.partial(multiply, kinds=tuple(kinds), chunk=chun...]
    pallas_call x2, Pallas kernels: 4.2 us -> 5.76 us  [cut(): pl.pallas_call(body, out_shape=shapes, in_specs=[SMEM, ANY, ANY], out_spe...]
  transfers between devices with their start and end apart: 18 -> 18, of which waited for: 8 -> 6; matrix products, arithmetic and copies ran while one was open for 0% -> 0% of each run, Pallas kernels for 21% -> 24%
where the time goes in v2:
time: 99.5 us; the launch traced here: 99.1 us
  waiting for transfers between devices  40.2 us (40%)
  Pallas kernels  28.4 us (29%)
  starting transfers between devices  19 us (19%)
  local copies, waits for them, and re-layouts  11.3 us (11%)
    ppermute x5, waiting for transfers between devices, far_pieces(): held = held + [lax.ppermute(piece, 'col', swap) for piece in held]  22.9 us
    pallas_call x4, Pallas kernels, steps(): pl.pallas_call(functools.partial(multiply, kinds=tuple(kinds), chunk=chun...  20.6 us
    ppermute x1, waiting for transfers between devices, steps(): first_cols = lax.ppermute(s_cols.T, 'row', first_pairs)  12.1 us
    ppermute x4, starting transfers between devices, steps(): halo.append(lax.ppermute(piece, 'row', pairs))  11.5 us
    unnamed x48, local copies, waits for them, and re-layouts  11.3 us
    ppermute x5, starting transfers between devices, far_pieces(): held = held + [lax.ppermute(piece, 'col', swap) for piece in held]  6.17 us
    pallas_call x2, Pallas kernels, cut(): pl.pallas_call(body, out_shape=shapes, in_specs=[SMEM, ANY, ANY], out_spe...  5.76 us
    ppermute x1, waiting for transfers between devices, steps(): second_cols = lax.ppermute(s_cols.T, 'row', second_pairs)  3.58 us
  transfers between devices with their start and end apart: 18, of which 6 were waited for; matrix products, arithmetic and copies ran while one was open for 0% of the time, Pallas kernels for 24%

profile of v2, /device:TPU:0, one launch (start us, length us, event | category | flops | bytes accessed | tf_op | source)
XLA Modules:
  0.0 99.1 jit_solution(27665179498018365)
XLA Ops:
  0.0 0.6 collective-permute-start.6
  0.6 0.1 pad_add_fusion.flip_ref.flips_ref.refs_0_
  0.6 2.8 %shard_map.57 = (bf16[4,4,128,128]{3,2,1,0:T(8,128)(2,1)S(1)}, bf16[5,4,128,128]{3,2,1,0:T(8,128)(2,1)}, bf16[4,4,128,128]{3,2,1,0:T(8,128)(2,1)S(1)}) custom-call(s32[2]{0:T(128)S(1)} %pad_add_fusion.flip_ref.flips_ref.refs_0_, bf16[16,4,128,128]{3,2,1,0:T(8,128)(2,1)} %refs_0_.3, bf16[16,4,128,128]{3,2,1,0:T(8,128)(2,1)} %refs_6_.1), custom_call_target="tpu_custom_call" | custom-call | tf_op jit(solution)/shard_map/pallas_call | solution.py:87
  3.5 0.0 copy-start.3
  3.5 2.6 %collective-permute-start.5 = (bf16[4,4,128,128]{3,2,1,0:T(8,128)(2,1)S(1)}, bf16[4,4,128,128]{3,2,1,0:T(8,128)(2,1)S(1)}, u32[]{:S(2)}, u32[]{:S(2)}) collective-permute-start(bf16[4,4,128,128]{3,2,1,0:T(8,128)(2,1)S(1)} %get-tuple-element.23.refs_2_), channel_id=1, source_target_pairs={{0,2},{1,3},{2,0},{3,1},{4,6},{5,7},{6,4},{7,5},{8,10},{9,11},{10,... | collective-permute-start | bytes 1572872 | tf_op jit(solution)/shard_map/ppermute | solution.py:275
  6.0 3.0 %shard_map.58 = (bf16[4,4,128,128]{3,2,1,0:T(8,128)(2,1)S(1)}, bf16[5,4,128,128]{3,2,1,0:T(8,128)(2,1)S(1)}, bf16[3,4,128,128]{3,2,1,0:T(8,128)(2,1)S(1)}, bf16[...) custom-call(s32[2]{0:T(128)S(1)} %pad_add_fusion.flip_ref.flips_ref.refs_0_, bf16[16,4,128,128]{3,2,1,0:T(8,128)(2,1)} %refs_0_.3, ...), custom_call_target="tpu_custom_call" | custom-call | tf_op jit(solution)/shard_map/pallas_call | solution.py:87
  9.0 0.1 collective-permute-start.15
  9.1 5.1 %collective-permute-start.8 = (bf16[4,4,128,128]{3,2,1,0:T(8,128)(2,1)S(1)}, bf16[4,4,128,128]{3,2,1,0:T(8,128)(2,1)}, u32[]{:S(2)}, u32[]{:S(2)}) collective-permute-start(bf16[4,4,128,128]{3,2,1,0:T(8,128)(2,1)S(1)} %get-tuple-element.24), channel_id=1, source_target_pairs={{0,28},{4,8},{8,4},{12,16},{16,12},{20,24},{24,20},{28,0},{1,29},{... | collective-permute-start | bytes 1572872 | tf_op jit(solution)/shard_map/ppermute | solution.py:319
  14.2 0.0 collective-permute-start
  14.2 12.1 %collective-permute-done.near_ref = s32[4,16]{1,0:T(4,128)S(1)} collective-permute-done((s32[4,16]{1,0:T(4,128)S(1)}, s32[4,16]{1,0:T(4,128)S(1)}, u32[]{:S(2)}, u32[]{:S(2)}) %collective-permute-start) | collective-permute-done | bytes 288 | tf_op jit(solution)/shard_map/ppermute | solution.py:323
  26.3 0.6 copy-done.13
  26.9 0.0 collective-permute-start.1
  26.9 3.6 %collective-permute-done.1.refs_0_ = s32[4,16]{1,0:T(4,128)S(1)} collective-permute-done((s32[4,16]{1,0:T(4,128)S(1)}, s32[4,16]{1,0:T(4,128)S(1)}, u32[]{:S(2)}, u32[]{:S(2)}) %collective-permute-start.1) | collective-permute-done | bytes 288 | tf_op jit(solution)/shard_map/ppermute | solution.py:324
  30.5 0.6 copy-done.22
  31.1 1.5 %collective-permute-start.2 = (s32[4,16]{1,0:T(4,128)S(1)}, s32[4,16]{1,0:T(4,128)S(1)}, u32[]{:S(2)}, u32[]{:S(2)}) collective-permute-start(s32[4,16]{1,0:T(4,128)S(1)} %bitcast.11), channel_id=1, source_target_pairs={{0,2},{1,3},{2,0},{3,1},{4,6},{5,7},{6,4},{7,5},{8,10},{9,11},{10,... | collective-permute-start | bytes 776 | tf_op jit(solution)/shard_map/ppermute | solution.py:275
  32.5 2.1 %collective-permute-done.2.refs_3_.refs_2_ = s32[4,16]{1,0:T(4,128)S(1)} collective-permute-done((s32[4,16]{1,0:T(4,128)S(1)}, s32[4,16]{1,0:T(4,128)S(1)}, u32[]{:S(2)}, u32[]{:S(2)}) %collective-permute-start.2) | collective-permute-done | bytes 288 | tf_op jit(solution)/shard_map/ppermute | solution.py:275
  34.6 0.0 collective-permute-start.3
  34.6 1.2 %collective-permute-done.3.refs_4_.refs_3_ = s32[4,16]{1,0:T(4,128)S(1)} collective-permute-done((s32[4,16]{1,0:T(4,128)S(1)}, s32[4,16]{1,0:T(4,128)S(1)}, u32[]{:S(2)}, u32[]{:S(2)}) %collective-permute-start.3) | collective-permute-done | bytes 288 | tf_op jit(solution)/shard_map/ppermute | solution.py:285
  35.8 0.5 copy-done.17
  36.3 0.2 collective-permute-start.4
  36.5 0.6 copy-done.15
  37.1 0.4 collective-permute-done.4.refs_5_.refs_4_
  37.5 0.6 copy-done.19
  38.1 1.5 %collective-permute-start.12 = (bf16[5,4,128,128]{3,2,1,0:T(8,128)(2,1)S(1)}, bf16[5,4,128,128]{3,2,1,0:T(8,128)(2,1)S(1)}, u32[]{:S(2)}, u32[]{:S(2)}) collective-permute-start(bf16[5,4,128,128]{3,2,1,0:T(8,128)(2,1)S(1)} %get-tuple-element.30.refs_9_), channel_id=1, source_target_pairs={{0,2},{1,3},{2,0},{3,1},{4,6},{5,7},{6,4},{7,5},{8,10},{9,11},{10,... | collective-permute-start | bytes 1966088 | tf_op jit(solution)/shard_map/ppermute | solution.py:275
  39.6 0.0 collective-permute-done.15.refs_3_
  39.6 0.5 collective-permute-start.9
  40.1 0.0 collective-permute-done.5.refs_3_
  40.1 4.4 %collective-permute-start.11 = (bf16[4,4,128,128]{3,2,1,0:T(8,128)(2,1)S(1)}, bf16[4,4,128,128]{3,2,1,0:T(8,128)(2,1)S(1)}, u32[]{:S(2)}, u32[]{:S(2)}) collective-permute-start(bf16[4,4,128,128]{3,2,1,0:T(8,128)(2,1)S(1)} %get-tuple-element.27), channel_id=1, source_target_pairs={{0,28},{4,8},{8,4},{12,16},{16,12},{20,24},{24,20},{28,0},{1,29},{... | collective-permute-start | bytes 1572872 | tf_op jit(solution)/shard_map/ppermute | solution.py:319
  44.6 0.0 collective-permute-done.8.refs_7_
  44.6 0.0 collective-permute-start.7
  44.6 0.8 copy-done.4
  45.4 20.8 %collective-permute-done.9.refs_3_ = bf16[4,4,128,128]{3,2,1,0:T(8,128)(2,1)S(1)} collective-permute-done((bf16[4,4,128,128]{3,2,1,0:T(8,128)(2,1)S(1)}, bf16[4,4,128,128]{3,2,1,0:T(8,128)(2,1)S(1)}, u32[]{:S(2)}, u32[]{:S(2)}) %collective-permute-start.9) | collective-permute-done | bytes 524320 | tf_op jit(solution)/shard_map/ppermute | solution.py:275
  66.1 0.0 collective-permute-start.14
  66.1 0.0 collective-permute-done.12.refs_3_
  66.1 0.1 collective-permute-start.13
  66.2 0.0 collective-permute-done.11.refs_6_
  66.2 0.8 copy-done.1
  67.0 0.5 collective-permute-start.10
  67.5 0.0 collective-permute-done.7.refs_5_
  67.5 0.0 copy-done.6
  67.5 0.8 copy-done.7
  68.3 2.0 %collective-permute-start.17 = (bf16[3,4,128,128]{3,2,1,0:T(8,128)(2,1)}, bf16[3,4,128,128]{3,2,1,0:T(8,128)(2,1)}, u32[]{:S(2)}, u32[]{:S(2)}) collective-permute-start(bf16[3,4,128,128]{3,2,1,0:T(8,128)(2,1)} %get-tuple-element.37), channel_id=1, source_target_pairs={{0,4},{4,0},{8,12},{12,8},{16,20},{20,16},{24,28},{28,24},{1,5},{5... | collective-permute-start | bytes 1179656 | tf_op jit(solution)/shard_map/ppermute | solution.py:319
  70.3 0.0 collective-permute-done.6.refs_4_.refs_9_.refs_10_
  70.3 0.0 collective-permute-start.16
  70.3 0.6 copy-done.14
  71.0 0.7 copy-done.16
  71.7 0.6 copy-done.18
  72.3 0.7 copy-done.20
  72.9 1.0 shard_map.56.refs_1_
  73.9 0.7 copy-done.21
  74.6 0.7 copy-done.23
  75.3 1.0 %shard_map.55.refs_1_ = s32[16,128]{1,0:T(8,128)S(1)} custom-call(s32[1]{0:T(128)} %bitcast.1.first_ref, s32[2]{0:T(128)S(1)} %pad_add_fusion.flip_ref.flips_ref.refs_0_, s32[4,16]{1,0:T(4,128)S(1)} %bitcast.10, s32[4,16]{1,0:T(4,128)S(1)} %copy-done.14, s32[4,16]{1,0:T(4,128)S(1)} %copy-done.23, s32[8,16]{1,0:T(8,128)S(1)} %bitcast.6, ...), custom_call_target="tpu_custom_call" | custom-call | tf_op jit(solution)/shard_map/pallas_call | solution.py:330
  76.3 0.0 copy-start.5
  76.3 1.0 %copy-done.5 = bf16[4,4,128,128]{3,2,1,0:T(8,128)(2,1)S(1)} copy-done((bf16[4,4,128,128]{3,2,1,0:T(8,128)(2,1)S(1)}, bf16[4,4,128,128]{3,2,1,0:T(8,128)(2,1)}, u32[]{:S(2)}) %copy-start.5) | copy-done | bytes 524312
  77.3 1.0 %copy-done.8 = bf16[4,4,128,128]{3,2,1,0:T(8,128)(2,1)S(1)} copy-done((bf16[4,4,128,128]{3,2,1,0:T(8,128)(2,1)S(1)}, bf16[4,4,128,128]{3,2,1,0:T(8,128)(2,1)}, u32[]{:S(2)}) %copy-start.8) | copy-done | bytes 524312
  78.4 6.4 %shard_map.59 = (f32[16,8,128,128]{3,2,1,0:T(8,128)}, bf16[129,128,128]{2,1,0:T(8,128)(2,1)S(1)}, bf16[4,8,128,128]{3,2,1,0:T(8,128)(2,1)S(1)}) custom-call(s32[2]{0:T(128)S(1)} %pad_add_fusion.flip_ref.flips_ref.refs_0_, s32[16,128]{1,0:T(8,128)S(1)} %shard_map.56.refs_1_, bf16[4,4,128,128]{3,2,1,0:T(8,128)(2,1)} %copy-done.3, ...), custom_call_target="tpu_custom_call" | custom-call | tf_op jit(solution)/shard_map/pallas_call | solution.py:391
  84.8 0.0 collective-permute-done.10.refs_5_
  84.8 4.8 %shard_map.60 = (f32[16,8,128,128]{3,2,1,0:T(8,128)}, bf16[129,128,128]{2,1,0:T(8,128)(2,1)S(1)}, bf16[5,8,128,128]{3,2,1,0:T(8,128)(2,1)S(1)}) custom-call(s32[2]{0:T(128)S(1)} %pad_add_fusion.flip_ref.flips_ref.refs_0_, s32[16,128]{1,0:T(8,128)S(1)} %shard_map.56.refs_1_, ...), custom_call_target="tpu_custom_call", output_to_operand_aliasing={{1}: (7, {}), {0}: (8, {})} | custom-call | tf_op jit(solution)/shard_map/pallas_call | solution.py:391
  89.7 0.0 collective-permute-done.14.refs_6_
  89.7 0.0 collective-permute-done.13.refs_5_
  89.7 5.2 %shard_map.61 = (f32[16,8,128,128]{3,2,1,0:T(8,128)}, bf16[129,128,128]{2,1,0:T(8,128)(2,1)S(1)}, bf16[3,8,128,128]{3,2,1,0:T(8,128)(2,1)S(1)}) custom-call(s32[2]{0:T(128)S(1)} %pad_add_fusion.flip_ref.flips_ref.refs_0_, s32[16,128]{1,0:T(8,128)S(1)} %shard_map.55.refs_1_, ...), custom_call_target="tpu_custom_call", output_to_operand_aliasing={{1}: (7, {}), {0}: (8, {})} | custom-call | tf_op jit(solution)/shard_map/pallas_call | solution.py:391
  94.9 0.0 collective-permute-done.17.refs_6_
  94.9 0.0 collective-permute-done.16.refs_5_
  94.9 4.1 %shard_map.62 = (f32[16,8,128,128]{3,2,1,0:T(8,128)}, bf16[129,128,128]{2,1,0:T(8,128)(2,1)S(1)}) custom-call(s32[2]{0:T(128)S(1)} %pad_add_fusion.flip_ref.flips_ref.refs_0_, s32[16,128]{1,0:T(8,128)S(1)} %shard_map.55.refs_1_, bf16[3,8,128,128]{3,2,1,0:T(8,128)(2,1)S(1)} %get-tuple-element.36.refs_2_.refs_4_, ...), custom_call_target="tpu_custom_call", output_to_operand_aliasing={{1}: (7, {}), {0}: (8, {})} | custom-call | tf_op jit(solution)/shard_map/pallas_call | solution.py:391
  (29 shorter events, 0.1 us)
Async XLA Ops:
  0.0 14.2 %copy-start.11 = (s32[16,4]{0,1:T(4,128)S(1)}, s32[16,4]{0,1:T(4,128)}, u32[]{:S(2)}) copy-start(s32[16,4]{0,1:T(4,128)} %param.8) | copy-start | bytes 772
  0.0 31.0 %copy-start.12 = (s32[16,4]{0,1:T(4,128)S(1)}, s32[16,4]{0,1:T(4,128)}, u32[]{:S(2)}) copy-start(s32[16,4]{0,1:T(4,128)} %param.6) | copy-start | bytes 772
  0.0 70.3 %copy-start.10 = (s32[16,8]{0,1:T(8,128)S(1)}, s32[16,8]{0,1:T(8,128)}, u32[]{:S(2)}) copy-start(s32[16,8]{0,1:T(8,128)} %param.9) | copy-start | bytes 1540
  0.0 70.3 %collective-permute-start.6 = (bf16[16,4,128,128]{3,2,1,0:T(8,128)(2,1)}, bf16[16,4,128,128]{3,2,1,0:T(8,128)(2,1)}, u32[]{:S(2)}, u32[]{:S(2)}) collective-permute-start(bf16[16,4,128,128]{3,2,1,0:T(8,128)(2,1)} %refs_0_.3), channel_id=1, source_target_pairs={{0,1},{1,0},{2,3},{3,2},{4,5},{5,4},{6,7},{7,6},{8,9},{9,8},{10,11... | collective-permute-start | bytes 6291464 | tf_op jit(solution)/shard_map/ppermute | solution.py:285
  3.5 62.7 %copy-start.3 = (bf16[4,4,128,128]{3,2,1,0:T(8,128)(2,1)}, bf16[4,4,128,128]{3,2,1,0:T(8,128)(2,1)S(1)}, u32[]{:S(2)}) copy-start(bf16[4,4,128,128]{3,2,1,0:T(8,128)(2,1)S(1)} %get-tuple-element.23.refs_2_) | copy-start | bytes 1572868
  3.5 36.6 %collective-permute-start.5 = (bf16[4,4,128,128]{3,2,1,0:T(8,128)(2,1)S(1)}, bf16[4,4,128,128]{3,2,1,0:T(8,128)(2,1)S(1)}, u32[]{:S(2)}, u32[]{:S(2)}) collective-permute-start(bf16[4,4,128,128]{3,2,1,0:T(8,128)(2,1)S(1)} %get-tuple-element.23.refs_2_), channel_id=1, source_target_pairs={{0,2},{1,3},{2,0},{3,1},{4,6},{5,7},{6,4},{7,5},{8,10},{9,11},{10,... | collective-permute-start | bytes 1572872 | tf_op jit(solution)/shard_map/ppermute | solution.py:275
  9.0 58.5 %copy-start.6 = (bf16[4,4,128,128]{3,2,1,0:T(8,128)(2,1)}, bf16[4,4,128,128]{3,2,1,0:T(8,128)(2,1)S(1)}, u32[]{:S(2)}) copy-start(bf16[4,4,128,128]{3,2,1,0:T(8,128)(2,1)S(1)} %get-tuple-element.25.refs_8_) | copy-start | bytes 1572868
  9.0 61.3 %copy-start.9 = (bf16[3,4,128,128]{3,2,1,0:T(8,128)(2,1)}, bf16[3,4,128,128]{3,2,1,0:T(8,128)(2,1)S(1)}, u32[]{:S(2)}) copy-start(bf16[3,4,128,128]{3,2,1,0:T(8,128)(2,1)S(1)} %get-tuple-element.35.refs_9_) | copy-start | bytes 1179652
  9.0 75.8 %copy-start = (bf16[5,4,128,128]{3,2,1,0:T(8,128)(2,1)}, bf16[5,4,128,128]{3,2,1,0:T(8,128)(2,1)S(1)}, u32[]{:S(2)}) copy-start(bf16[5,4,128,128]{3,2,1,0:T(8,128)(2,1)S(1)} %get-tuple-element.30.refs_9_) | copy-start | bytes 1966084
  9.0 30.5 %collective-permute-start.15 = (bf16[3,4,128,128]{3,2,1,0:T(8,128)(2,1)S(1)}, bf16[3,4,128,128]{3,2,1,0:T(8,128)(2,1)S(1)}, u32[]{:S(2)}, u32[]{:S(2)}) collective-permute-start(bf16[3,4,128,128]{3,2,1,0:T(8,128)(2,1)S(1)} %get-tuple-element.35.refs_9_), channel_id=1, source_target_pairs={{0,2},{1,3},{2,0},{3,1},{4,6},{5,7},{6,4},{7,5},{8,10},{9,11},{10,... | collective-permute-start | bytes 1179656 | tf_op jit(solution)/shard_map/ppermute | solution.py:275
  9.1 35.4 %collective-permute-start.8 = (bf16[4,4,128,128]{3,2,1,0:T(8,128)(2,1)S(1)}, bf16[4,4,128,128]{3,2,1,0:T(8,128)(2,1)}, u32[]{:S(2)}, u32[]{:S(2)}) collective-permute-start(bf16[4,4,128,128]{3,2,1,0:T(8,128)(2,1)S(1)} %get-tuple-element.24), channel_id=1, source_target_pairs={{0,28},{4,8},{8,4},{12,16},{16,12},{20,24},{24,20},{28,0},{1,29},{... | collective-permute-start | bytes 1572872 | tf_op jit(solution)/shard_map/ppermute | solution.py:319
  14.2 12.1 %collective-permute-start = (s32[4,16]{1,0:T(4,128)S(1)}, s32[4,16]{1,0:T(4,128)S(1)}, u32[]{:S(2)}, u32[]{:S(2)}) collective-permute-start(s32[4,16]{1,0:T(4,128)S(1)} %bitcast.7), channel_id=1, source_target_pairs={{0,28},{4,8},{8,4},{12,16},{16,12},{20,24},{24,20},{28,0},{1,29},{... | collective-permute-start | bytes 776 | tf_op jit(solution)/shard_map/ppermute | solution.py:323
  26.3 0.6 copy-start.13
  26.9 3.6 %collective-permute-start.1 = (s32[4,16]{1,0:T(4,128)S(1)}, s32[4,16]{1,0:T(4,128)S(1)}, u32[]{:S(2)}, u32[]{:S(2)}) collective-permute-start(s32[4,16]{1,0:T(4,128)S(1)} %bitcast.8), channel_id=1, source_target_pairs={{0,4},{4,0},{8,12},{12,8},{16,20},{20,16},{24,28},{28,24},{1,5},{5... | collective-permute-start | bytes 776 | tf_op jit(solution)/shard_map/ppermute | solution.py:324
  30.5 0.6 copy-start.22
  31.1 3.6 %collective-permute-start.2 = (s32[4,16]{1,0:T(4,128)S(1)}, s32[4,16]{1,0:T(4,128)S(1)}, u32[]{:S(2)}, u32[]{:S(2)}) collective-permute-start(s32[4,16]{1,0:T(4,128)S(1)} %bitcast.11), channel_id=1, source_target_pairs={{0,2},{1,3},{2,0},{3,1},{4,6},{5,7},{6,4},{7,5},{8,10},{9,11},{10,... | collective-permute-start | bytes 776 | tf_op jit(solution)/shard_map/ppermute | solution.py:275
  34.6 1.2 %collective-permute-start.3 = (s32[4,16]{1,0:T(4,128)S(1)}, s32[4,16]{1,0:T(4,128)S(1)}, u32[]{:S(2)}, u32[]{:S(2)}) collective-permute-start(s32[4,16]{1,0:T(4,128)S(1)} %bitcast.12), channel_id=1, source_target_pairs={{0,1},{1,0},{2,3},{3,2},{4,5},{5,4},{6,7},{7,6},{8,9},{9,8},{10,11... | collective-permute-start | bytes 776 | tf_op jit(solution)/shard_map/ppermute | solution.py:285
  35.8 0.5 copy-start.17
  36.3 1.2 %collective-permute-start.4 = (s32[4,16]{1,0:T(4,128)S(1)}, s32[4,16]{1,0:T(4,128)S(1)}, u32[]{:S(2)}, u32[]{:S(2)}) collective-permute-start(s32[4,16]{1,0:T(4,128)S(1)} %collective-permute-done.2.refs_3_.refs_2_), channel_id=1, source_target_pairs={{0,1},{1,0},{2,3},{3,2},{4,5},{5,4},{6,7},{7,6},{8,9},{9,8},{10,11... | collective-permute-start | bytes 776 | tf_op jit(solution)/shard_map/ppermute | solution.py:285
  36.5 0.6 copy-start.15
  37.5 0.6 copy-start.19
  38.1 28.0 %collective-permute-start.12 = (bf16[5,4,128,128]{3,2,1,0:T(8,128)(2,1)S(1)}, bf16[5,4,128,128]{3,2,1,0:T(8,128)(2,1)S(1)}, u32[]{:S(2)}, u32[]{:S(2)}) collective-permute-start(bf16[5,4,128,128]{3,2,1,0:T(8,128)(2,1)S(1)} %get-tuple-element.30.refs_9_), channel_id=1, source_target_pairs={{0,2},{1,3},{2,0},{3,1},{4,6},{5,7},{6,4},{7,5},{8,10},{9,11},{10,... | collective-permute-start | bytes 1966088 | tf_op jit(solution)/shard_map/ppermute | solution.py:275
  39.6 26.5 %collective-permute-start.9 = (bf16[4,4,128,128]{3,2,1,0:T(8,128)(2,1)S(1)}, bf16[4,4,128,128]{3,2,1,0:T(8,128)(2,1)S(1)}, u32[]{:S(2)}, u32[]{:S(2)}) collective-permute-start(bf16[4,4,128,128]{3,2,1,0:T(8,128)(2,1)S(1)} %get-tuple-element.25.refs_8_), channel_id=1, source_target_pairs={{0,2},{1,3},{2,0},{3,1},{4,6},{5,7},{6,4},{7,5},{8,10},{9,11},{10,... | collective-permute-start | bytes 1572872 | tf_op jit(solution)/shard_map/ppermute | solution.py:275
  40.1 26.1 %collective-permute-start.11 = (bf16[4,4,128,128]{3,2,1,0:T(8,128)(2,1)S(1)}, bf16[4,4,128,128]{3,2,1,0:T(8,128)(2,1)S(1)}, u32[]{:S(2)}, u32[]{:S(2)}) collective-permute-start(bf16[4,4,128,128]{3,2,1,0:T(8,128)(2,1)S(1)} %get-tuple-element.27), channel_id=1, source_target_pairs={{0,28},{4,8},{8,4},{12,16},{16,12},{20,24},{24,20},{28,0},{1,29},{... | collective-permute-start | bytes 1572872 | tf_op jit(solution)/shard_map/ppermute | solution.py:319
  44.6 23.0 %collective-permute-start.7 = (bf16[4,4,128,128]{3,2,1,0:T(8,128)(2,1)S(1)}, bf16[4,4,128,128]{3,2,1,0:T(8,128)(2,1)S(1)}, u32[]{:S(2)}, u32[]{:S(2)}) collective-permute-start(bf16[4,4,128,128]{3,2,1,0:T(8,128)(2,1)S(1)} %collective-permute-done.5.refs_3_), channel_id=1, source_target_pairs={{0,1},{1,0},{2,3},{3,2},{4,5},{5,4},{6,7},{7,6},{8,9},{9,8},{10,11... | collective-permute-start | bytes 1572872 | tf_op jit(solution)/shard_map/ppermute | solution.py:285
  44.6 0.8 copy-start.4
  66.1 23.6 %collective-permute-start.14 = (bf16[5,4,128,128]{3,2,1,0:T(8,128)(2,1)}, bf16[5,4,128,128]{3,2,1,0:T(8,128)(2,1)S(1)}, u32[]{:S(2)}, u32[]{:S(2)}) collective-permute-start(bf16[5,4,128,128]{3,2,1,0:T(8,128)(2,1)} %get-tuple-element.32), channel_id=1, source_target_pairs={{0,4},{4,0},{8,12},{12,8},{16,20},{20,16},{24,28},{28,24},{1,5},{5... | collective-permute-start | bytes 1966088 | tf_op jit(solution)/shard_map/ppermute | solution.py:319
  66.1 23.6 %collective-permute-start.13 = (bf16[5,4,128,128]{3,2,1,0:T(8,128)(2,1)S(1)}, bf16[5,4,128,128]{3,2,1,0:T(8,128)(2,1)S(1)}, u32[]{:S(2)}, u32[]{:S(2)}) collective-permute-start(bf16[5,4,128,128]{3,2,1,0:T(8,128)(2,1)S(1)} %collective-permute-done.12.refs_3_), channel_id=1, source_target_pairs={{0,1},{1,0},{2,3},{3,2},{4,5},{5,4},{6,7},{7,6},{8,9},{9,8},{10,11... | collective-permute-start | bytes 1966088 | tf_op jit(solution)/shard_map/ppermute | solution.py:285
  66.2 0.8 copy-start.1
  67.0 17.8 %collective-permute-start.10 = (bf16[4,4,128,128]{3,2,1,0:T(8,128)(2,1)S(1)}, bf16[4,4,128,128]{3,2,1,0:T(8,128)(2,1)}, u32[]{:S(2)}, u32[]{:S(2)}) collective-permute-start(bf16[4,4,128,128]{3,2,1,0:T(8,128)(2,1)S(1)} %collective-permute-done.9.refs_3_), channel_id=1, source_target_pairs={{0,1},{1,0},{2,3},{3,2},{4,5},{5,4},{6,7},{7,6},{8,9},{9,8},{10,11... | collective-permute-start | bytes 1572872 | tf_op jit(solution)/shard_map/ppermute | solution.py:285
  67.5 0.8 copy-start.7
  68.3 26.6 %collective-permute-start.17 = (bf16[3,4,128,128]{3,2,1,0:T(8,128)(2,1)}, bf16[3,4,128,128]{3,2,1,0:T(8,128)(2,1)}, u32[]{:S(2)}, u32[]{:S(2)}) collective-permute-start(bf16[3,4,128,128]{3,2,1,0:T(8,128)(2,1)} %get-tuple-element.37), channel_id=1, source_target_pairs={{0,4},{4,0},{8,12},{12,8},{16,20},{20,16},{24,28},{28,24},{1,5},{5... | collective-permute-start | bytes 1179656 | tf_op jit(solution)/shard_map/ppermute | solution.py:319
  70.3 24.6 %collective-permute-start.16 = (bf16[3,4,128,128]{3,2,1,0:T(8,128)(2,1)S(1)}, bf16[3,4,128,128]{3,2,1,0:T(8,128)(2,1)}, u32[]{:S(2)}, u32[]{:S(2)}) collective-permute-start(bf16[3,4,128,128]{3,2,1,0:T(8,128)(2,1)S(1)} %collective-permute-done.15.refs_3_), channel_id=1, source_target_pairs={{0,1},{1,0},{2,3},{3,2},{4,5},{5,4},{6,7},{7,6},{8,9},{9,8},{10,11... | collective-permute-start | bytes 1179656 | tf_op jit(solution)/shard_map/ppermute | solution.py:285
  70.3 0.7 copy-start.14
  71.0 0.7 copy-start.16
  71.7 0.6 copy-start.18
  72.3 0.7 copy-start.20
  73.9 0.7 copy-start.21
  74.6 0.7 copy-start.23
  76.3 1.0 %copy-start.5 = (bf16[4,4,128,128]{3,2,1,0:T(8,128)(2,1)S(1)}, bf16[4,4,128,128]{3,2,1,0:T(8,128)(2,1)}, u32[]{:S(2)}) copy-start(bf16[4,4,128,128]{3,2,1,0:T(8,128)(2,1)} %copy-done.4) | copy-start | bytes 1572868
  77.3 1.0 %copy-start.8 = (bf16[4,4,128,128]{3,2,1,0:T(8,128)(2,1)S(1)}, bf16[4,4,128,128]{3,2,1,0:T(8,128)(2,1)}, u32[]{:S(2)}) copy-start(bf16[4,4,128,128]{3,2,1,0:T(8,128)(2,1)} %copy-done.7) | copy-start | bytes 1572868
  78.4 6.5 %copy-start.2 = (bf16[4,4,128,128]{3,2,1,0:T(8,128)(2,1)S(1)}, bf16[4,4,128,128]{3,2,1,0:T(8,128)(2,1)}, u32[]{:S(2)}) copy-start(bf16[4,4,128,128]{3,2,1,0:T(8,128)(2,1)} %copy-done.1) | copy-start | bytes 1572868

commit v3 on v2

--- a/solution.py
+++ b/solution.py
@@ -8,7 +8,7 @@
 from jax.sharding import PartitionSpec as P
 
 VMEM_GRANT = 16 << 20
-SECOND_EIGHTHS = (5, 3)
+SECOND_EIGHTHS = (4, 4)
 ANY = pl.BlockSpec(memory_space=pl.ANY)
 SMEM = pl.BlockSpec(memory_space=pltpu.SMEM)
 VMEM = pl.BlockSpec(memory_space=pltpu.VMEM)
@@ -305,7 +305,7 @@
 
     lead = next(n for n, chunk in enumerate(chunks) if chunk[0] >= reach)
     wanted = [(0, chunk) for chunk in chunks] + [(1, side) for side in sides]
-    early = [0, len(chunks) + lead, len(chunks)]
+    early = [0, len(chunks) + lead]
     late = [n for n in range(len(wanted)) if n not in early]
     pieces = dict(zip(early, cut(flips, p_values, s_values, [wanted[n] for n in early])))
     pieces |= zip(late, cut(flips, p_values, s_values, [wanted[n] for n in late]))
@@ -354,7 +354,8 @@
         inputs, specs = [flips, place_of[chunk[0] >= reach]], [SMEM] * 2
         for kind in kinds:
             if kind == "here":
-                inputs.append(in_vmem(here.pop(0)))
+                keep_in = in_vmem if ahead is None or len(here) <= len(passed) else lambda x: x
+                inputs.append(keep_in(here.pop(0)))
             else:
                 inputs.append(in_hbm(fetch_from.pop(0)) if first else ready)
             specs.append(ANY if first and kind == "fetch" else VMEM)
@@ -365,7 +366,7 @@
             specs += [ANY] * 2
         else:
             news = [sides[n]]
-            inputs.append(in_vmem(halo[n]))
+            inputs.append(halo[n] if ahead else in_vmem(halo[n]))
             specs.append(VMEM)
             aliases = {len(inputs): 1, len(inputs) + 1: 0}
             inputs += [in_vmem(window), product]

time: 99.5 us -> 92.1 us (0.926)
  local copies, waits for them, and re-layouts: 11.3 us -> 4.57 us
  starting transfers between devices: 19 us -> 16.1 us
  waiting for transfers between devices: 40.2 us -> 41.8 us
    ppermute x4, waiting for transfers between devices: 0.01 us -> 8.6 us  [steps(): halo.append(lax.ppermute(piece, 'row', pairs))]
    ppermute x5, waiting for transfers between devices: 22.9 us -> 15.7 us  [far_pieces(): held = held + [lax.ppermute(piece, 'col', swap) for piece in held]]
    unnamed x48 -> x24, local copies, waits for them, and re-layouts: 11.3 us -> 4.57 us
    ppermute x4, starting transfers between devices: 11.5 us -> 9.06 us  [steps(): halo.append(lax.ppermute(piece, 'row', pairs))]
  transfers between devices with their start and end apart: 18 -> 18, of which waited for: 6 -> 8; matrix products, arithmetic and copies ran while one was open for 0% -> 0% of each run, Pallas kernels for 24% -> 26%
where the time goes in v3:
time: 92.1 us; the launch traced here: 91.8 us
  waiting for transfers between devices  41.8 us (45%)
  Pallas kernels  29 us (31%)
  starting transfers between devices  16.1 us (17%)
  local copies, waits for them, and re-layouts  4.57 us (5%)
    pallas_call x4, Pallas kernels, steps(): pl.pallas_call(functools.partial(multiply, kinds=tuple(kinds), chunk=chun...  21.2 us
    ppermute x5, waiting for transfers between devices, far_pieces(): held = held + [lax.ppermute(piece, 'col', swap) for piece in held]  15.7 us
    ppermute x1, waiting for transfers between devices, steps(): first_cols = lax.ppermute(s_cols.T, 'row', first_pairs)  11.7 us
    ppermute x4, starting transfers between devices, steps(): halo.append(lax.ppermute(piece, 'row', pairs))  9.06 us
    ppermute x4, waiting for transfers between devices, steps(): halo.append(lax.ppermute(piece, 'row', pairs))  8.6 us
    pallas_call x2, Pallas kernels, cut(): pl.pallas_call(body, out_shape=shapes, in_specs=[SMEM, ANY, ANY], out_spe...  5.79 us
    ppermute x5, starting transfers between devices, far_pieces(): held = held + [lax.ppermute(piece, 'col', swap) for piece in held]  5.66 us
    unnamed x24, local copies, waits for them, and re-layouts  4.57 us
  transfers between devices with their start and end apart: 18, of which 8 were waited for; matrix products, arithmetic and copies ran while one was open for 0% of the time, Pallas kernels for 26%

profile of v3, /device:TPU:0, one launch (start us, length us, event | category | flops | bytes accessed | tf_op | source)
XLA Modules:
  0.0 91.8 jit_solution(14604690247415649041)
XLA Ops:
  0.0 0.0 copy-start.9
  0.0 0.0 copy-start.10
  0.0 0.6 collective-permute-start.6
  0.6 0.1 pad_add_fusion.flip_ref.flips_ref.refs_0_
  0.6 2.5 %shard_map.57 = (bf16[4,4,128,128]{3,2,1,0:T(8,128)(2,1)S(1)}, bf16[4,4,128,128]{3,2,1,0:T(8,128)(2,1)}) custom-call(s32[2]{0:T(128)S(1)} %pad_add_fusion.flip_ref.flips_ref.refs_0_, bf16[16,4,128,128]{3,2,1,0:T(8,128)(2,1)} %refs_0_.3, bf16[16,4,128,128]{3,2,1,0:T(8,128)(2,1)} %refs_6_.1), custom_call_target="tpu_custom_call" | custom-call | tf_op jit(solution)/shard_map/pallas_call | solution.py:87
  3.2 0.0 copy-start.2
  3.2 2.6 %collective-permute-start.5 = (bf16[4,4,128,128]{3,2,1,0:T(8,128)(2,1)S(1)}, bf16[4,4,128,128]{3,2,1,0:T(8,128)(2,1)S(1)}, u32[]{:S(2)}, u32[]{:S(2)}) collective-permute-start(bf16[4,4,128,128]{3,2,1,0:T(8,128)(2,1)S(1)} %get-tuple-element.23.refs_2_), channel_id=1, source_target_pairs={{0,2},{1,3},{2,0},{3,1},{4,6},{5,7},{6,4},{7,5},{8,10},{9,11},{10,... | collective-permute-start | bytes 1572872 | tf_op jit(solution)/shard_map/ppermute | solution.py:275
  5.8 3.2 %shard_map.58 = (bf16[4,4,128,128]{3,2,1,0:T(8,128)(2,1)S(1)}, bf16[4,4,128,128]{3,2,1,0:T(8,128)(2,1)S(1)}, bf16[4,4,128,128]{3,2,1,0:T(8,128)(2,1)S(1)}, bf16[...) custom-call(s32[2]{0:T(128)S(1)} %pad_add_fusion.flip_ref.flips_ref.refs_0_, ...), custom_call_target="tpu_custom_call" | custom-call | tf_op jit(solution)/shard_map/pallas_call | solution.py:87
  9.0 0.0 copy-start.5
  9.0 0.0 copy-start
  9.0 0.0 copy-start.1
  9.1 4.6 %collective-permute-start.8 = (bf16[4,4,128,128]{3,2,1,0:T(8,128)(2,1)S(1)}, bf16[4,4,128,128]{3,2,1,0:T(8,128)(2,1)S(1)}, u32[]{:S(2)}, u32[]{:S(2)}) collective-permute-start(bf16[4,4,128,128]{3,2,1,0:T(8,128)(2,1)S(1)} %get-tuple-element.24), channel_id=1, source_target_pairs={{0,28},{4,8},{8,4},{12,16},{16,12},{20,24},{24,20},{28,0},{1,29},{... | collective-permute-start | bytes 1572872 | tf_op jit(solution)/shard_map/ppermute | solution.py:319
  13.7 0.5 collective-permute-start.9
  14.2 0.0 copy-done.9
  14.2 0.1 collective-permute-start
  14.3 11.7 %collective-permute-done.near_ref = s32[4,16]{1,0:T(4,128)S(1)} collective-permute-done((s32[4,16]{1,0:T(4,128)S(1)}, s32[4,16]{1,0:T(4,128)S(1)}, u32[]{:S(2)}, u32[]{:S(2)}) %collective-permute-start) | collective-permute-done | bytes 288 | tf_op jit(solution)/shard_map/ppermute | solution.py:323
  26.0 0.0 collective-permute-start.1
  26.0 3.6 %collective-permute-done.1.refs_0_ = s32[4,16]{1,0:T(4,128)S(1)} collective-permute-done((s32[4,16]{1,0:T(4,128)S(1)}, s32[4,16]{1,0:T(4,128)S(1)}, u32[]{:S(2)}, u32[]{:S(2)}) %collective-permute-start.1) | collective-permute-done | bytes 288 | tf_op jit(solution)/shard_map/ppermute | solution.py:324
  29.6 0.0 copy-done.10
  29.6 0.5 collective-permute-start.2
  30.1 3.0 %collective-permute-done.2.refs_3_.refs_2_ = s32[4,16]{1,0:T(4,128)S(1)} collective-permute-done((s32[4,16]{1,0:T(4,128)S(1)}, s32[4,16]{1,0:T(4,128)S(1)}, u32[]{:S(2)}, u32[]{:S(2)}) %collective-permute-start.2) | collective-permute-done | bytes 288 | tf_op jit(solution)/shard_map/ppermute | solution.py:275
  33.2 0.0 collective-permute-start.3
  33.2 1.2 %collective-permute-done.3.refs_4_.refs_3_ = s32[4,16]{1,0:T(4,128)S(1)} collective-permute-done((s32[4,16]{1,0:T(4,128)S(1)}, s32[4,16]{1,0:T(4,128)S(1)}, u32[]{:S(2)}, u32[]{:S(2)}) %collective-permute-start.3) | collective-permute-done | bytes 288 | tf_op jit(solution)/shard_map/ppermute | solution.py:285
  34.3 0.2 collective-permute-start.4
  34.5 1.0 %collective-permute-done.4.refs_5_.refs_4_ = s32[4,16]{1,0:T(4,128)S(1)} collective-permute-done((s32[4,16]{1,0:T(4,128)S(1)}, s32[4,16]{1,0:T(4,128)S(1)}, u32[]{:S(2)}, u32[]{:S(2)}) %collective-permute-start.4) | collective-permute-done | bytes 288 | tf_op jit(solution)/shard_map/ppermute | solution.py:285
  35.5 4.4 %collective-permute-start.11 = (bf16[4,4,128,128]{3,2,1,0:T(8,128)(2,1)S(1)}, bf16[4,4,128,128]{3,2,1,0:T(8,128)(2,1)S(1)}, u32[]{:S(2)}, u32[]{:S(2)}) collective-permute-start(bf16[4,4,128,128]{3,2,1,0:T(8,128)(2,1)S(1)} %get-tuple-element.27), channel_id=1, source_target_pairs={{0,28},{4,8},{8,4},{12,16},{16,12},{20,24},{24,20},{28,0},{1,29},{... | collective-permute-start | bytes 1572872 | tf_op jit(solution)/shard_map/ppermute | solution.py:319
  40.0 0.0 collective-permute-done.5.refs_3_
  40.0 0.5 collective-permute-start.12
  40.5 0.0 collective-permute-done.8.refs_7_
  40.5 0.8 copy-done.11
  41.3 1.5 %collective-permute-start.15 = (bf16[4,4,128,128]{3,2,1,0:T(8,128)(2,1)S(1)}, bf16[4,4,128,128]{3,2,1,0:T(8,128)(2,1)S(1)}, u32[]{:S(2)}, u32[]{:S(2)}) collective-permute-start(bf16[4,4,128,128]{3,2,1,0:T(8,128)(2,1)S(1)} %get-tuple-element.35.refs_9_), channel_id=1, source_target_pairs={{0,2},{1,3},{2,0},{3,1},{4,6},{5,7},{6,4},{7,5},{8,10},{9,11},{10,... | collective-permute-start | bytes 1572872 | tf_op jit(solution)/shard_map/ppermute | solution.py:275
  42.8 0.0 collective-permute-done.9.refs_3_
  42.8 0.0 collective-permute-start.7
  42.8 0.8 copy-done.3
  43.6 8.6 %collective-permute-done.11.refs_6_ = bf16[4,4,128,128]{3,2,1,0:T(8,128)(2,1)S(1)} collective-permute-done((bf16[4,4,128,128]{3,2,1,0:T(8,128)(2,1)S(1)}, bf16[4,4,128,128]{3,2,1,0:T(8,128)(2,1)S(1)}, u32[]{:S(2)}, u32[]{:S(2)}) %collective-permute-start.11) | collective-permute-done | bytes 524320 | tf_op jit(solution)/shard_map/ppermute | solution.py:319
  52.2 0.0 collective-permute-start.10
  52.2 2.5 %collective-permute-done.12.refs_3_ = bf16[4,4,128,128]{3,2,1,0:T(8,128)(2,1)S(1)} collective-permute-done((bf16[4,4,128,128]{3,2,1,0:T(8,128)(2,1)S(1)}, bf16[4,4,128,128]{3,2,1,0:T(8,128)(2,1)S(1)}, u32[]{:S(2)}, u32[]{:S(2)}) %collective-permute-start.12) | collective-permute-done | bytes 524320 | tf_op jit(solution)/shard_map/ppermute | solution.py:275
  54.8 0.0 collective-permute-start.14
  54.8 10.2 %collective-permute-done.15.refs_3_ = bf16[4,4,128,128]{3,2,1,0:T(8,128)(2,1)S(1)} collective-permute-done((bf16[4,4,128,128]{3,2,1,0:T(8,128)(2,1)S(1)}, bf16[4,4,128,128]{3,2,1,0:T(8,128)(2,1)S(1)}, u32[]{:S(2)}, u32[]{:S(2)}) %collective-permute-start.15) | collective-permute-done | bytes 524320 | tf_op jit(solution)/shard_map/ppermute | solution.py:275
  64.9 0.0 collective-permute-start.13
  64.9 0.0 collective-permute-done.7.refs_5_
  64.9 0.8 copy-done.6
  65.8 0.0 collective-permute-start.17
  65.8 0.0 copy-done.2
  65.8 0.0 collective-permute-done.6.refs_4_.refs_9_.refs_10_
  65.8 0.0 copy-done.5
  65.8 0.6 collective-permute-start.16
  66.4 0.0 copy-done.8
  66.4 1.0 %shard_map.56.refs_1_ = s32[16,128]{1,0:T(8,128)S(1)} custom-call(s32[1]{0:T(128)} %bitcast.1.first_ref, s32[2]{0:T(128)S(1)} %pad_add_fusion.flip_ref.flips_ref.refs_0_, s32[4,16]{1,0:T(4,128)S(1)} %bitcast.9, s32[4,16]{1,0:T(4,128)S(1)} %collective-permute-done.near_ref, s32[8,16]{1,0:T(8,128)S(1)} %bitcast.5, s32[4,16]{1,0:T(4,128)S(1)} %bitcast.13, ...), custom_call_target="tpu_custom_call" | custom-call | tf_op jit(solution)/shard_map/pallas_call | solution.py:330
  67.3 1.0 %shard_map.55.refs_1_ = s32[16,128]{1,0:T(8,128)S(1)} custom-call(s32[1]{0:T(128)} %bitcast.1.first_ref, s32[2]{0:T(128)S(1)} %pad_add_fusion.flip_ref.flips_ref.refs_0_, s32[4,16]{1,0:T(4,128)S(1)} %bitcast.10, s32[4,16]{1,0:T(4,128)S(1)} %collective-permute-done.near_ref, s32[4,16]{1,0:T(4,128)S(1)} %collective-permute-done.1.refs_0_, ...), custom_call_target="tpu_custom_call" | custom-call | tf_op jit(solution)/shard_map/pallas_call | solution.py:330
  68.4 0.0 copy-start.4
  68.4 1.0 %copy-done.4 = bf16[4,4,128,128]{3,2,1,0:T(8,128)(2,1)S(1)} copy-done((bf16[4,4,128,128]{3,2,1,0:T(8,128)(2,1)S(1)}, bf16[4,4,128,128]{3,2,1,0:T(8,128)(2,1)}, u32[]{:S(2)}) %copy-start.4) | copy-done | bytes 524312
  69.4 1.0 %copy-done.7 = bf16[4,4,128,128]{3,2,1,0:T(8,128)(2,1)S(1)} copy-done((bf16[4,4,128,128]{3,2,1,0:T(8,128)(2,1)S(1)}, bf16[4,4,128,128]{3,2,1,0:T(8,128)(2,1)}, u32[]{:S(2)}) %copy-start.7) | copy-done | bytes 524312
  70.4 6.4 %shard_map.59 = (f32[16,8,128,128]{3,2,1,0:T(8,128)}, bf16[129,128,128]{2,1,0:T(8,128)(2,1)S(1)}, bf16[4,8,128,128]{3,2,1,0:T(8,128)(2,1)S(1)}) custom-call(s32[2]{0:T(128)S(1)} %pad_add_fusion.flip_ref.flips_ref.refs_0_, s32[16,128]{1,0:T(8,128)S(1)} %shard_map.56.refs_1_, bf16[4,4,128,128]{3,2,1,0:T(8,128)(2,1)} %copy-done.2, ...), custom_call_target="tpu_custom_call" | custom-call | tf_op jit(solution)/shard_map/pallas_call | solution.py:392
  76.9 0.0 copy-done
  76.9 0.0 copy-done.1
  76.9 0.0 collective-permute-done.10.refs_5_
  76.9 4.8 %shard_map.60 = (f32[16,8,128,128]{3,2,1,0:T(8,128)}, bf16[129,128,128]{2,1,0:T(8,128)(2,1)S(1)}, bf16[4,8,128,128]{3,2,1,0:T(8,128)(2,1)S(1)}) custom-call(s32[2]{0:T(128)S(1)} %pad_add_fusion.flip_ref.flips_ref.refs_0_, s32[16,128]{1,0:T(8,128)S(1)} %shard_map.56.refs_1_, ...), custom_call_target="tpu_custom_call", output_to_operand_aliasing={{1}: (7, {}), {0}: (8, {})} | custom-call | tf_op jit(solution)/shard_map/pallas_call | solution.py:392
  81.8 0.0 collective-permute-done.14.refs_6_
  81.8 0.0 collective-permute-done.13.refs_5_
  81.8 5.0 %shard_map.61 = (f32[16,8,128,128]{3,2,1,0:T(8,128)}, bf16[129,128,128]{2,1,0:T(8,128)(2,1)S(1)}, bf16[4,8,128,128]{3,2,1,0:T(8,128)(2,1)S(1)}) custom-call(s32[2]{0:T(128)S(1)} %pad_add_fusion.flip_ref.flips_ref.refs_0_, s32[16,128]{1,0:T(8,128)S(1)} %shard_map.55.refs_1_, ...), custom_call_target="tpu_custom_call", output_to_operand_aliasing={{1}: (7, {}), {0}: (8, {})} | custom-call | tf_op jit(solution)/shard_map/pallas_call | solution.py:392
  86.8 0.0 collective-permute-done.17.refs_6_
  86.8 0.0 collective-permute-done.16.refs_5_
  86.8 5.0 %shard_map.62 = (f32[16,8,128,128]{3,2,1,0:T(8,128)}, bf16[129,128,128]{2,1,0:T(8,128)(2,1)S(1)}) custom-call(s32[2]{0:T(128)S(1)} %pad_add_fusion.flip_ref.flips_ref.refs_0_, s32[16,128]{1,0:T(8,128)S(1)} %shard_map.55.refs_1_, bf16[4,8,128,128]{3,2,1,0:T(8,128)(2,1)S(1)} %get-tuple-element.36.refs_2_.refs_4_, ...), custom_call_target="tpu_custom_call", output_to_operand_aliasing={{1}: (7, {}), {0}: (8, {})} | custom-call | tf_op jit(solution)/shard_map/pallas_call | solution.py:392
  (5 shorter events, 0.0 us)
Async XLA Ops:
  0.0 14.2 %copy-start.9 = (s32[16,4]{0,1:T(4,128)S(1)}, s32[16,4]{0,1:T(4,128)}, u32[]{:S(2)}) copy-start(s32[16,4]{0,1:T(4,128)} %param.8) | copy-start | bytes 772
  0.0 29.6 %copy-start.10 = (s32[16,4]{0,1:T(4,128)S(1)}, s32[16,4]{0,1:T(4,128)}, u32[]{:S(2)}) copy-start(s32[16,4]{0,1:T(4,128)} %param.6) | copy-start | bytes 772
  0.0 66.4 %copy-start.8 = (s32[16,8]{0,1:T(8,128)S(1)}, s32[16,8]{0,1:T(8,128)}, u32[]{:S(2)}) copy-start(s32[16,8]{0,1:T(8,128)} %param.9) | copy-start | bytes 1540
  0.0 65.8 %collective-permute-start.6 = (bf16[16,4,128,128]{3,2,1,0:T(8,128)(2,1)}, bf16[16,4,128,128]{3,2,1,0:T(8,128)(2,1)}, u32[]{:S(2)}, u32[]{:S(2)}) collective-permute-start(bf16[16,4,128,128]{3,2,1,0:T(8,128)(2,1)} %refs_0_.3), channel_id=1, source_target_pairs={{0,1},{1,0},{2,3},{3,2},{4,5},{5,4},{6,7},{7,6},{8,9},{9,8},{10,11... | collective-permute-start | bytes 6291464 | tf_op jit(solution)/shard_map/ppermute | solution.py:285
  3.2 62.6 %copy-start.2 = (bf16[4,4,128,128]{3,2,1,0:T(8,128)(2,1)}, bf16[4,4,128,128]{3,2,1,0:T(8,128)(2,1)S(1)}, u32[]{:S(2)}) copy-start(bf16[4,4,128,128]{3,2,1,0:T(8,128)(2,1)S(1)} %get-tuple-element.23.refs_2_) | copy-start | bytes 1572868
  3.2 36.7 %collective-permute-start.5 = (bf16[4,4,128,128]{3,2,1,0:T(8,128)(2,1)S(1)}, bf16[4,4,128,128]{3,2,1,0:T(8,128)(2,1)S(1)}, u32[]{:S(2)}, u32[]{:S(2)}) collective-permute-start(bf16[4,4,128,128]{3,2,1,0:T(8,128)(2,1)S(1)} %get-tuple-element.23.refs_2_), channel_id=1, source_target_pairs={{0,2},{1,3},{2,0},{3,1},{4,6},{5,7},{6,4},{7,5},{8,10},{9,11},{10,... | collective-permute-start | bytes 1572872 | tf_op jit(solution)/shard_map/ppermute | solution.py:275
  9.0 56.8 %copy-start.5 = (bf16[4,4,128,128]{3,2,1,0:T(8,128)(2,1)}, bf16[4,4,128,128]{3,2,1,0:T(8,128)(2,1)S(1)}, u32[]{:S(2)}) copy-start(bf16[4,4,128,128]{3,2,1,0:T(8,128)(2,1)S(1)} %get-tuple-element.25.refs_8_) | copy-start | bytes 1572868
  9.0 67.9 %copy-start = (bf16[4,4,128,128]{3,2,1,0:T(8,128)(2,1)}, bf16[4,4,128,128]{3,2,1,0:T(8,128)(2,1)S(1)}, u32[]{:S(2)}) copy-start(bf16[4,4,128,128]{3,2,1,0:T(8,128)(2,1)S(1)} %get-tuple-element.35.refs_9_) | copy-start | bytes 1572868
  9.0 67.9 %copy-start.1 = (bf16[4,4,128,128]{3,2,1,0:T(8,128)(2,1)}, bf16[4,4,128,128]{3,2,1,0:T(8,128)(2,1)S(1)}, u32[]{:S(2)}) copy-start(bf16[4,4,128,128]{3,2,1,0:T(8,128)(2,1)S(1)} %get-tuple-element.30.refs_9_) | copy-start | bytes 1572868
  9.1 31.4 %collective-permute-start.8 = (bf16[4,4,128,128]{3,2,1,0:T(8,128)(2,1)S(1)}, bf16[4,4,128,128]{3,2,1,0:T(8,128)(2,1)S(1)}, u32[]{:S(2)}, u32[]{:S(2)}) collective-permute-start(bf16[4,4,128,128]{3,2,1,0:T(8,128)(2,1)S(1)} %get-tuple-element.24), channel_id=1, source_target_pairs={{0,28},{4,8},{8,4},{12,16},{16,12},{20,24},{24,20},{28,0},{1,29},{... | collective-permute-start | bytes 1572872 | tf_op jit(solution)/shard_map/ppermute | solution.py:319
  13.7 29.1 %collective-permute-start.9 = (bf16[4,4,128,128]{3,2,1,0:T(8,128)(2,1)S(1)}, bf16[4,4,128,128]{3,2,1,0:T(8,128)(2,1)S(1)}, u32[]{:S(2)}, u32[]{:S(2)}) collective-permute-start(bf16[4,4,128,128]{3,2,1,0:T(8,128)(2,1)S(1)} %get-tuple-element.25.refs_8_), channel_id=1, source_target_pairs={{0,2},{1,3},{2,0},{3,1},{4,6},{5,7},{6,4},{7,5},{8,10},{9,11},{10,... | collective-permute-start | bytes 1572872 | tf_op jit(solution)/shard_map/ppermute | solution.py:275
  14.2 11.8 %collective-permute-start = (s32[4,16]{1,0:T(4,128)S(1)}, s32[4,16]{1,0:T(4,128)S(1)}, u32[]{:S(2)}, u32[]{:S(2)}) collective-permute-start(s32[4,16]{1,0:T(4,128)S(1)} %bitcast.7), channel_id=1, source_target_pairs={{0,28},{4,8},{8,4},{12,16},{16,12},{20,24},{24,20},{28,0},{1,29},{... | collective-permute-start | bytes 776 | tf_op jit(solution)/shard_map/ppermute | solution.py:323
  26.0 3.6 %collective-permute-start.1 = (s32[4,16]{1,0:T(4,128)S(1)}, s32[4,16]{1,0:T(4,128)S(1)}, u32[]{:S(2)}, u32[]{:S(2)}) collective-permute-start(s32[4,16]{1,0:T(4,128)S(1)} %bitcast.8), channel_id=1, source_target_pairs={{0,4},{4,0},{8,12},{12,8},{16,20},{20,16},{24,28},{28,24},{1,5},{5... | collective-permute-start | bytes 776 | tf_op jit(solution)/shard_map/ppermute | solution.py:324
  29.6 3.6 %collective-permute-start.2 = (s32[4,16]{1,0:T(4,128)S(1)}, s32[4,16]{1,0:T(4,128)S(1)}, u32[]{:S(2)}, u32[]{:S(2)}) collective-permute-start(s32[4,16]{1,0:T(4,128)S(1)} %bitcast.11), channel_id=1, source_target_pairs={{0,2},{1,3},{2,0},{3,1},{4,6},{5,7},{6,4},{7,5},{8,10},{9,11},{10,... | collective-permute-start | bytes 776 | tf_op jit(solution)/shard_map/ppermute | solution.py:275
  33.2 1.2 %collective-permute-start.3 = (s32[4,16]{1,0:T(4,128)S(1)}, s32[4,16]{1,0:T(4,128)S(1)}, u32[]{:S(2)}, u32[]{:S(2)}) collective-permute-start(s32[4,16]{1,0:T(4,128)S(1)} %bitcast.12), channel_id=1, source_target_pairs={{0,1},{1,0},{2,3},{3,2},{4,5},{5,4},{6,7},{7,6},{8,9},{9,8},{10,11... | collective-permute-start | bytes 776 | tf_op jit(solution)/shard_map/ppermute | solution.py:285
  34.3 1.2 %collective-permute-start.4 = (s32[4,16]{1,0:T(4,128)S(1)}, s32[4,16]{1,0:T(4,128)S(1)}, u32[]{:S(2)}, u32[]{:S(2)}) collective-permute-start(s32[4,16]{1,0:T(4,128)S(1)} %collective-permute-done.2.refs_3_.refs_2_), channel_id=1, source_target_pairs={{0,1},{1,0},{2,3},{3,2},{4,5},{5,4},{6,7},{7,6},{8,9},{9,8},{10,11... | collective-permute-start | bytes 776 | tf_op jit(solution)/shard_map/ppermute | solution.py:285
  35.5 16.7 %collective-permute-start.11 = (bf16[4,4,128,128]{3,2,1,0:T(8,128)(2,1)S(1)}, bf16[4,4,128,128]{3,2,1,0:T(8,128)(2,1)S(1)}, u32[]{:S(2)}, u32[]{:S(2)}) collective-permute-start(bf16[4,4,128,128]{3,2,1,0:T(8,128)(2,1)S(1)} %get-tuple-element.27), channel_id=1, source_target_pairs={{0,28},{4,8},{8,4},{12,16},{16,12},{20,24},{24,20},{28,0},{1,29},{... | collective-permute-start | bytes 1572872 | tf_op jit(solution)/shard_map/ppermute | solution.py:319
  40.0 14.8 %collective-permute-start.12 = (bf16[4,4,128,128]{3,2,1,0:T(8,128)(2,1)S(1)}, bf16[4,4,128,128]{3,2,1,0:T(8,128)(2,1)S(1)}, u32[]{:S(2)}, u32[]{:S(2)}) collective-permute-start(bf16[4,4,128,128]{3,2,1,0:T(8,128)(2,1)S(1)} %get-tuple-element.30.refs_9_), channel_id=1, source_target_pairs={{0,2},{1,3},{2,0},{3,1},{4,6},{5,7},{6,4},{7,5},{8,10},{9,11},{10,... | collective-permute-start | bytes 1572872 | tf_op jit(solution)/shard_map/ppermute | solution.py:275
  40.5 0.8 copy-start.11
  41.3 23.6 %collective-permute-start.15 = (bf16[4,4,128,128]{3,2,1,0:T(8,128)(2,1)S(1)}, bf16[4,4,128,128]{3,2,1,0:T(8,128)(2,1)S(1)}, u32[]{:S(2)}, u32[]{:S(2)}) collective-permute-start(bf16[4,4,128,128]{3,2,1,0:T(8,128)(2,1)S(1)} %get-tuple-element.35.refs_9_), channel_id=1, source_target_pairs={{0,2},{1,3},{2,0},{3,1},{4,6},{5,7},{6,4},{7,5},{8,10},{9,11},{10,... | collective-permute-start | bytes 1572872 | tf_op jit(solution)/shard_map/ppermute | solution.py:275
  42.8 22.1 %collective-permute-start.7 = (bf16[4,4,128,128]{3,2,1,0:T(8,128)(2,1)S(1)}, bf16[4,4,128,128]{3,2,1,0:T(8,128)(2,1)S(1)}, u32[]{:S(2)}, u32[]{:S(2)}) collective-permute-start(bf16[4,4,128,128]{3,2,1,0:T(8,128)(2,1)S(1)} %collective-permute-done.5.refs_3_), channel_id=1, source_target_pairs={{0,1},{1,0},{2,3},{3,2},{4,5},{5,4},{6,7},{7,6},{8,9},{9,8},{10,11... | collective-permute-start | bytes 1572872 | tf_op jit(solution)/shard_map/ppermute | solution.py:285
  42.8 0.8 copy-start.3
  52.2 24.7 %collective-permute-start.10 = (bf16[4,4,128,128]{3,2,1,0:T(8,128)(2,1)S(1)}, bf16[4,4,128,128]{3,2,1,0:T(8,128)(2,1)}, u32[]{:S(2)}, u32[]{:S(2)}) collective-permute-start(bf16[4,4,128,128]{3,2,1,0:T(8,128)(2,1)S(1)} %collective-permute-done.9.refs_3_), channel_id=1, source_target_pairs={{0,1},{1,0},{2,3},{3,2},{4,5},{5,4},{6,7},{7,6},{8,9},{9,8},{10,11... | collective-permute-start | bytes 1572872 | tf_op jit(solution)/shard_map/ppermute | solution.py:285
  54.8 27.0 %collective-permute-start.14 = (bf16[4,4,128,128]{3,2,1,0:T(8,128)(2,1)}, bf16[4,4,128,128]{3,2,1,0:T(8,128)(2,1)}, u32[]{:S(2)}, u32[]{:S(2)}) collective-permute-start(bf16[4,4,128,128]{3,2,1,0:T(8,128)(2,1)} %get-tuple-element.32), channel_id=1, source_target_pairs={{0,4},{4,0},{8,12},{12,8},{16,20},{20,16},{24,28},{28,24},{1,5},{5... | collective-permute-start | bytes 1572872 | tf_op jit(solution)/shard_map/ppermute | solution.py:319
  64.9 16.9 %collective-permute-start.13 = (bf16[4,4,128,128]{3,2,1,0:T(8,128)(2,1)S(1)}, bf16[4,4,128,128]{3,2,1,0:T(8,128)(2,1)}, u32[]{:S(2)}, u32[]{:S(2)}) collective-permute-start(bf16[4,4,128,128]{3,2,1,0:T(8,128)(2,1)S(1)} %collective-permute-done.12.refs_3_), channel_id=1, source_target_pairs={{0,1},{1,0},{2,3},{3,2},{4,5},{5,4},{6,7},{7,6},{8,9},{9,8},{10,11... | collective-permute-start | bytes 1572872 | tf_op jit(solution)/shard_map/ppermute | solution.py:285
  64.9 0.8 copy-start.6
  65.8 21.0 %collective-permute-start.17 = (bf16[4,4,128,128]{3,2,1,0:T(8,128)(2,1)}, bf16[4,4,128,128]{3,2,1,0:T(8,128)(2,1)}, u32[]{:S(2)}, u32[]{:S(2)}) collective-permute-start(bf16[4,4,128,128]{3,2,1,0:T(8,128)(2,1)} %get-tuple-element.37), channel_id=1, source_target_pairs={{0,4},{4,0},{8,12},{12,8},{16,20},{20,16},{24,28},{28,24},{1,5},{5... | collective-permute-start | bytes 1572872 | tf_op jit(solution)/shard_map/ppermute | solution.py:319
  65.8 21.0 %collective-permute-start.16 = (bf16[4,4,128,128]{3,2,1,0:T(8,128)(2,1)S(1)}, bf16[4,4,128,128]{3,2,1,0:T(8,128)(2,1)}, u32[]{:S(2)}, u32[]{:S(2)}) collective-permute-start(bf16[4,4,128,128]{3,2,1,0:T(8,128)(2,1)S(1)} %collective-permute-done.15.refs_3_), channel_id=1, source_target_pairs={{0,1},{1,0},{2,3},{3,2},{4,5},{5,4},{6,7},{7,6},{8,9},{9,8},{10,11... | collective-permute-start | bytes 1572872 | tf_op jit(solution)/shard_map/ppermute | solution.py:285
  68.4 1.0 %copy-start.4 = (bf16[4,4,128,128]{3,2,1,0:T(8,128)(2,1)S(1)}, bf16[4,4,128,128]{3,2,1,0:T(8,128)(2,1)}, u32[]{:S(2)}) copy-start(bf16[4,4,128,128]{3,2,1,0:T(8,128)(2,1)} %copy-done.3) | copy-start | bytes 1572868
  69.4 1.0 %copy-start.7 = (bf16[4,4,128,128]{3,2,1,0:T(8,128)(2,1)S(1)}, bf16[4,4,128,128]{3,2,1,0:T(8,128)(2,1)}, u32[]{:S(2)}) copy-start(bf16[4,4,128,128]{3,2,1,0:T(8,128)(2,1)} %copy-done.6) | copy-start | bytes 1572868

commit v4 on v3

--- a/solution.py
+++ b/solution.py
@@ -58,16 +58,19 @@
     return jnp.where(flip == 1, start - block_rows + reach, reach + 2 * block_rows - stop)
 
 
-def cut(flips, p_values, s_values, cuts):
+def cut(p_values, s_values, cuts):
     block_rows = p_values.shape[0]
     sources = (p_values, s_values)
 
-    def body(flips_ref, *refs):
+    even = lax.axis_size("row") % 2 == 0
+
+    def body(*refs):
         ins, outs, sems = refs[:2], refs[2:-1], refs[-1]
+        odd = lax.axis_index("row") % 2
         copies = [
             pltpu.make_async_copy(
                 ins[source].at[
-                    pl.ds(local_start(part, block_rows, flips_ref[source]), out.shape[0])
+                    pl.ds(local_start(part, block_rows, odd if even else source), out.shape[0])
                 ],
                 out,
                 sems.at[n],
@@ -87,11 +90,11 @@
         pl.pallas_call(
             body,
             out_shape=shapes,
-            in_specs=[SMEM, ANY, ANY],
+            in_specs=[ANY, ANY],
             out_specs=[VMEM] * len(shapes),
             scratch_shapes=[pltpu.SemaphoreType.DMA((len(cuts),))],
             compiler_params=pltpu.CompilerParams(vmem_limit_bytes=VMEM_GRANT),
-        )(flips, in_hbm(p_values), in_hbm(s_values))
+        )(in_hbm(p_values), in_hbm(s_values))
     )
 
 
@@ -307,8 +310,8 @@
     wanted = [(0, chunk) for chunk in chunks] + [(1, side) for side in sides]
     early = [0, len(chunks) + lead]
     late = [n for n in range(len(wanted)) if n not in early]
-    pieces = dict(zip(early, cut(flips, p_values, s_values, [wanted[n] for n in early])))
-    pieces |= zip(late, cut(flips, p_values, s_values, [wanted[n] for n in late]))
+    pieces = dict(zip(early, cut(p_values, s_values, [wanted[n] for n in early])))
+    pieces |= zip(late, cut(p_values, s_values, [wanted[n] for n in late]))
     own = [pieces[n] for n in range(len(chunks))]
     sent = [pieces[len(chunks) + n] for n in range(len(chunks))]
 

time: 92.1 us -> 91.8 us (level)
  Pallas kernels: 29 us -> 27.9 us
    pallas_call x2, Pallas kernels: 5.79 us -> 4.68 us  [cut(): pl.pallas_call(body, out_shape=shapes, in_specs=[ANY, ANY], out_specs=[VM...]
    unnamed x24 -> x26, local copies, waits for them, and re-layouts: 4.57 us -> 4.49 us
  transfers between devices with their start and end apart: 18 -> 18, of which waited for: 8 -> 8; matrix products, arithmetic and copies ran while one was open for 0% -> 0% of each run, Pallas kernels for 26% -> 25%
where the time goes in v4:
time: 91.8 us; the launch traced here: 91.4 us
  waiting for transfers between devices  42.6 us (46%)
  Pallas kernels  27.9 us (30%)
  starting transfers between devices  16.1 us (18%)
  local copies, waits for them, and re-layouts  4.49 us (5%)
    pallas_call x4, Pallas kernels, steps(): pl.pallas_call(functools.partial(multiply, kinds=tuple(kinds), chunk=chun...  21.2 us
    ppermute x5, waiting for transfers between devices, far_pieces(): held = held + [lax.ppermute(piece, 'col', swap) for piece in held]  15.7 us
    ppermute x1, waiting for transfers between devices, steps(): first_cols = lax.ppermute(s_cols.T, 'row', first_pairs)  11.7 us
    ppermute x4, waiting for transfers between devices, steps(): halo.append(lax.ppermute(piece, 'row', pairs))  9.43 us
    ppermute x4, starting transfers between devices, steps(): halo.append(lax.ppermute(piece, 'row', pairs))  9.06 us
    ppermute x5, starting transfers between devices, far_pieces(): held = held + [lax.ppermute(piece, 'col', swap) for piece in held]  5.67 us
    pallas_call x2, Pallas kernels, cut(): pl.pallas_call(body, out_shape=shapes, in_specs=[ANY, ANY], out_specs=[VM...  4.68 us
    unnamed x26, local copies, waits for them, and re-layouts  4.49 us
  transfers between devices with their start and end apart: 18, of which 8 were waited for; matrix products, arithmetic and copies ran while one was open for 0% of the time, Pallas kernels for 25%

profile of v4, /device:TPU:0, one launch (start us, length us, event | category | flops | bytes accessed | tf_op | source)
XLA Modules:
  0.0 91.4 jit_solution(4151027585895970302)
XLA Ops:
  0.0 0.6 collective-permute-start.6
  0.6 2.0 %shard_map.57 = (bf16[4,4,128,128]{3,2,1,0:T(8,128)(2,1)S(1)}, bf16[4,4,128,128]{3,2,1,0:T(8,128)(2,1)}) custom-call(bf16[16,4,128,128]{3,2,1,0:T(8,128)(2,1)} %refs_0_.3, bf16[16,4,128,128]{3,2,1,0:T(8,128)(2,1)} %refs_6_.1), custom_call_target="tpu_custom_call" | custom-call | tf_op jit(solution)/shard_map/pallas_call | solution.py:90
  2.6 0.0 copy-start.2
  2.6 2.6 %collective-permute-start.5 = (bf16[4,4,128,128]{3,2,1,0:T(8,128)(2,1)S(1)}, bf16[4,4,128,128]{3,2,1,0:T(8,128)(2,1)S(1)}, u32[]{:S(2)}, u32[]{:S(2)}) collective-permute-start(bf16[4,4,128,128]{3,2,1,0:T(8,128)(2,1)S(1)} %get-tuple-element.23.refs_2_), channel_id=1, source_target_pairs={{0,2},{1,3},{2,0},{3,1},{4,6},{5,7},{6,4},{7,5},{8,10},{9,11},{10,... | collective-permute-start | bytes 1572872 | tf_op jit(solution)/shard_map/ppermute | solution.py:278
  5.2 2.7 %shard_map.58 = (bf16[4,4,128,128]{3,2,1,0:T(8,128)(2,1)S(1)}, bf16[4,4,128,128]{3,2,1,0:T(8,128)(2,1)S(1)}, bf16[4,4,128,128]{3,2,1,0:T(8,128)(2,1)S(1)}, bf16[...) custom-call(bf16[16,4,128,128]{3,2,1,0:T(8,128)(2,1)} %refs_0_.3, ...), custom_call_target="tpu_custom_call" | custom-call | tf_op jit(solution)/shard_map/pallas_call | solution.py:90
  7.9 0.0 copy-start.5
  7.9 0.0 copy-start
  7.9 0.0 copy-start.1
  7.9 4.6 %collective-permute-start.8 = (bf16[4,4,128,128]{3,2,1,0:T(8,128)(2,1)S(1)}, bf16[4,4,128,128]{3,2,1,0:T(8,128)(2,1)S(1)}, u32[]{:S(2)}, u32[]{:S(2)}) collective-permute-start(bf16[4,4,128,128]{3,2,1,0:T(8,128)(2,1)S(1)} %get-tuple-element.24), channel_id=1, source_target_pairs={{0,28},{4,8},{8,4},{12,16},{16,12},{20,24},{24,20},{28,0},{1,29},{... | collective-permute-start | bytes 1572872 | tf_op jit(solution)/shard_map/ppermute | solution.py:322
  12.5 0.5 collective-permute-start.9
  13.0 0.0 copy-done.9
  13.0 0.1 collective-permute-start
  13.1 11.7 %collective-permute-done.near_ref = s32[4,16]{1,0:T(4,128)S(1)} collective-permute-done((s32[4,16]{1,0:T(4,128)S(1)}, s32[4,16]{1,0:T(4,128)S(1)}, u32[]{:S(2)}, u32[]{:S(2)}) %collective-permute-start) | collective-permute-done | bytes 288 | tf_op jit(solution)/shard_map/ppermute | solution.py:326
  24.8 0.0 collective-permute-start.1
  24.8 3.6 %collective-permute-done.1.refs_0_ = s32[4,16]{1,0:T(4,128)S(1)} collective-permute-done((s32[4,16]{1,0:T(4,128)S(1)}, s32[4,16]{1,0:T(4,128)S(1)}, u32[]{:S(2)}, u32[]{:S(2)}) %collective-permute-start.1) | collective-permute-done | bytes 288 | tf_op jit(solution)/shard_map/ppermute | solution.py:327
  28.4 0.0 copy-done.10
  28.4 0.5 collective-permute-start.2
  29.0 3.0 %collective-permute-done.2.refs_3_.refs_2_ = s32[4,16]{1,0:T(4,128)S(1)} collective-permute-done((s32[4,16]{1,0:T(4,128)S(1)}, s32[4,16]{1,0:T(4,128)S(1)}, u32[]{:S(2)}, u32[]{:S(2)}) %collective-permute-start.2) | collective-permute-done | bytes 288 | tf_op jit(solution)/shard_map/ppermute | solution.py:278
  32.0 0.0 collective-permute-start.3
  32.0 1.2 %collective-permute-done.3.refs_4_.refs_3_ = s32[4,16]{1,0:T(4,128)S(1)} collective-permute-done((s32[4,16]{1,0:T(4,128)S(1)}, s32[4,16]{1,0:T(4,128)S(1)}, u32[]{:S(2)}, u32[]{:S(2)}) %collective-permute-start.3) | collective-permute-done | bytes 288 | tf_op jit(solution)/shard_map/ppermute | solution.py:288
  33.2 0.2 collective-permute-start.4
  33.3 1.0 %collective-permute-done.4.refs_5_.refs_4_ = s32[4,16]{1,0:T(4,128)S(1)} collective-permute-done((s32[4,16]{1,0:T(4,128)S(1)}, s32[4,16]{1,0:T(4,128)S(1)}, u32[]{:S(2)}, u32[]{:S(2)}) %collective-permute-start.4) | collective-permute-done | bytes 288 | tf_op jit(solution)/shard_map/ppermute | solution.py:288
  34.3 4.4 %collective-permute-start.11 = (bf16[4,4,128,128]{3,2,1,0:T(8,128)(2,1)S(1)}, bf16[4,4,128,128]{3,2,1,0:T(8,128)(2,1)S(1)}, u32[]{:S(2)}, u32[]{:S(2)}) collective-permute-start(bf16[4,4,128,128]{3,2,1,0:T(8,128)(2,1)S(1)} %get-tuple-element.27), channel_id=1, source_target_pairs={{0,28},{4,8},{8,4},{12,16},{16,12},{20,24},{24,20},{28,0},{1,29},{... | collective-permute-start | bytes 1572872 | tf_op jit(solution)/shard_map/ppermute | solution.py:322
  38.8 0.0 collective-permute-done.5.refs_3_
  38.8 0.5 collective-permute-start.12
  39.3 0.0 collective-permute-done.8.refs_7_
  39.3 1.5 %collective-permute-start.15 = (bf16[4,4,128,128]{3,2,1,0:T(8,128)(2,1)S(1)}, bf16[4,4,128,128]{3,2,1,0:T(8,128)(2,1)S(1)}, u32[]{:S(2)}, u32[]{:S(2)}) collective-permute-start(bf16[4,4,128,128]{3,2,1,0:T(8,128)(2,1)S(1)} %get-tuple-element.35.refs_9_), channel_id=1, source_target_pairs={{0,2},{1,3},{2,0},{3,1},{4,6},{5,7},{6,4},{7,5},{8,10},{9,11},{10,... | collective-permute-start | bytes 1572872 | tf_op jit(solution)/shard_map/ppermute | solution.py:278
  40.8 0.0 collective-permute-done.9.refs_3_
  40.8 0.0 collective-permute-start.7
  40.8 0.8 copy-done.3
  41.6 9.4 %collective-permute-done.11.refs_6_ = bf16[4,4,128,128]{3,2,1,0:T(8,128)(2,1)S(1)} collective-permute-done((bf16[4,4,128,128]{3,2,1,0:T(8,128)(2,1)S(1)}, bf16[4,4,128,128]{3,2,1,0:T(8,128)(2,1)S(1)}, u32[]{:S(2)}, u32[]{:S(2)}) %collective-permute-start.11) | collective-permute-done | bytes 524320 | tf_op jit(solution)/shard_map/ppermute | solution.py:322
  51.0 0.0 collective-permute-start.10
  51.0 2.5 %collective-permute-done.12.refs_3_ = bf16[4,4,128,128]{3,2,1,0:T(8,128)(2,1)S(1)} collective-permute-done((bf16[4,4,128,128]{3,2,1,0:T(8,128)(2,1)S(1)}, bf16[4,4,128,128]{3,2,1,0:T(8,128)(2,1)S(1)}, u32[]{:S(2)}, u32[]{:S(2)}) %collective-permute-start.12) | collective-permute-done | bytes 524320 | tf_op jit(solution)/shard_map/ppermute | solution.py:278
  53.6 0.0 collective-permute-start.14
  53.6 10.2 %collective-permute-done.15.refs_3_ = bf16[4,4,128,128]{3,2,1,0:T(8,128)(2,1)S(1)} collective-permute-done((bf16[4,4,128,128]{3,2,1,0:T(8,128)(2,1)S(1)}, bf16[4,4,128,128]{3,2,1,0:T(8,128)(2,1)S(1)}, u32[]{:S(2)}, u32[]{:S(2)}) %collective-permute-start.15) | collective-permute-done | bytes 524320 | tf_op jit(solution)/shard_map/ppermute | solution.py:278
  63.7 0.0 collective-permute-start.13
  63.7 0.0 collective-permute-done.7.refs_5_
  63.7 0.8 copy-done.6
  64.6 0.0 collective-permute-start.17
  64.6 0.0 copy-done.2
  64.6 0.0 collective-permute-done.6.refs_4_.refs_9_.refs_10_
  64.6 0.0 copy-done.5
  64.6 0.0 copy-start.11
  64.6 0.6 collective-permute-start.16
  65.2 0.0 copy-done.12
  65.2 0.8 copy-done.11
  65.9 0.1 pad_add_fusion.flip_ref.refs_0_
  66.0 0.0 copy-done.8
  66.0 1.0 %shard_map.56.refs_1_ = s32[16,128]{1,0:T(8,128)S(1)} custom-call(s32[1]{0:T(128)} %bitcast.1.first_ref, s32[2]{0:T(128)S(1)} %pad_add_fusion.flip_ref.refs_0_, s32[4,16]{1,0:T(4,128)S(1)} %bitcast.9, s32[4,16]{1,0:T(4,128)S(1)} %collective-permute-done.near_ref, s32[8,16]{1,0:T(8,128)S(1)} %bitcast.5, s32[4,16]{1,0:T(4,128)S(1)} %bitcast.13, ...), custom_call_target="tpu_custom_call" | custom-call | tf_op jit(solution)/shard_map/pallas_call | solution.py:333
  67.0 1.0 %shard_map.55.refs_1_ = s32[16,128]{1,0:T(8,128)S(1)} custom-call(s32[1]{0:T(128)} %bitcast.1.first_ref, s32[2]{0:T(128)S(1)} %pad_add_fusion.flip_ref.refs_0_, s32[4,16]{1,0:T(4,128)S(1)} %bitcast.10, s32[4,16]{1,0:T(4,128)S(1)} %collective-permute-done.near_ref, s32[4,16]{1,0:T(4,128)S(1)} %collective-permute-done.1.refs_0_, s32[8,16]{1,0:T(8,128)S(1)} %bitcast.6, ...), custom_call_target="tpu_custom_call" | custom-call | tf_op jit(solution)/shard_map/pallas_call | solution.py:333
  68.0 0.0 copy-start.4
  68.0 1.0 %copy-done.4 = bf16[4,4,128,128]{3,2,1,0:T(8,128)(2,1)S(1)} copy-done((bf16[4,4,128,128]{3,2,1,0:T(8,128)(2,1)S(1)}, bf16[4,4,128,128]{3,2,1,0:T(8,128)(2,1)}, u32[]{:S(2)}) %copy-start.4) | copy-done | bytes 524312
  69.1 1.0 %copy-done.7 = bf16[4,4,128,128]{3,2,1,0:T(8,128)(2,1)S(1)} copy-done((bf16[4,4,128,128]{3,2,1,0:T(8,128)(2,1)S(1)}, bf16[4,4,128,128]{3,2,1,0:T(8,128)(2,1)}, u32[]{:S(2)}) %copy-start.7) | copy-done | bytes 524312
  70.1 6.4 %shard_map.59 = (f32[16,8,128,128]{3,2,1,0:T(8,128)}, bf16[129,128,128]{2,1,0:T(8,128)(2,1)S(1)}, bf16[4,8,128,128]{3,2,1,0:T(8,128)(2,1)S(1)}) custom-call(s32[2]{0:T(128)S(1)} %pad_add_fusion.flip_ref.refs_0_, s32[16,128]{1,0:T(8,128)S(1)} %shard_map.56.refs_1_, bf16[4,4,128,128]{3,2,1,0:T(8,128)(2,1)} %copy-done.2, ...), custom_call_target="tpu_custom_call" | custom-call | tf_op jit(solution)/shard_map/pallas_call | solution.py:395
  76.5 0.0 copy-done
  76.6 0.0 copy-done.1
  76.6 0.0 collective-permute-done.10.refs_5_
  76.6 4.8 %shard_map.60 = (f32[16,8,128,128]{3,2,1,0:T(8,128)}, bf16[129,128,128]{2,1,0:T(8,128)(2,1)S(1)}, bf16[4,8,128,128]{3,2,1,0:T(8,128)(2,1)S(1)}) custom-call(s32[2]{0:T(128)S(1)} %pad_add_fusion.flip_ref.refs_0_, s32[16,128]{1,0:T(8,128)S(1)} %shard_map.56.refs_1_, ...), custom_call_target="tpu_custom_call", output_to_operand_aliasing={{1}: (7, {}), {0}: (8, {})} | custom-call | tf_op jit(solution)/shard_map/pallas_call | solution.py:395
  81.4 0.0 collective-permute-done.14.refs_6_
  81.4 0.0 collective-permute-done.13.refs_5_
  81.4 5.0 %shard_map.61 = (f32[16,8,128,128]{3,2,1,0:T(8,128)}, bf16[129,128,128]{2,1,0:T(8,128)(2,1)S(1)}, bf16[4,8,128,128]{3,2,1,0:T(8,128)(2,1)S(1)}) custom-call(s32[2]{0:T(128)S(1)} %pad_add_fusion.flip_ref.refs_0_, s32[16,128]{1,0:T(8,128)S(1)} %shard_map.55.refs_1_, ...), custom_call_target="tpu_custom_call", output_to_operand_aliasing={{1}: (7, {}), {0}: (8, {})} | custom-call | tf_op jit(solution)/shard_map/pallas_call | solution.py:395
  86.4 0.0 collective-permute-done.17.refs_6_
  86.4 0.0 collective-permute-done.16.refs_5_
  86.5 5.0 %shard_map.62 = (f32[16,8,128,128]{3,2,1,0:T(8,128)}, bf16[129,128,128]{2,1,0:T(8,128)(2,1)S(1)}) custom-call(s32[2]{0:T(128)S(1)} %pad_add_fusion.flip_ref.refs_0_, s32[16,128]{1,0:T(8,128)S(1)} %shard_map.55.refs_1_, bf16[4,8,128,128]{3,2,1,0:T(8,128)(2,1)S(1)} %get-tuple-element.36.refs_2_.refs_4_, ...), custom_call_target="tpu_custom_call", output_to_operand_aliasing={{1}: (7, {}), {0}: (8, {})} | custom-call | tf_op jit(solution)/shard_map/pallas_call | solution.py:395
  (7 shorter events, 0.0 us)
Async XLA Ops:
  0.0 13.0 %copy-start.9 = (s32[16,4]{0,1:T(4,128)S(1)}, s32[16,4]{0,1:T(4,128)}, u32[]{:S(2)}) copy-start(s32[16,4]{0,1:T(4,128)} %param.8) | copy-start | bytes 772
  0.0 28.4 %copy-start.10 = (s32[16,4]{0,1:T(4,128)S(1)}, s32[16,4]{0,1:T(4,128)}, u32[]{:S(2)}) copy-start(s32[16,4]{0,1:T(4,128)} %param.6) | copy-start | bytes 772
  0.0 66.0 %copy-start.8 = (s32[16,8]{0,1:T(8,128)S(1)}, s32[16,8]{0,1:T(8,128)}, u32[]{:S(2)}) copy-start(s32[16,8]{0,1:T(8,128)} %param.9) | copy-start | bytes 1540
  0.0 64.6 %collective-permute-start.6 = (bf16[16,4,128,128]{3,2,1,0:T(8,128)(2,1)}, bf16[16,4,128,128]{3,2,1,0:T(8,128)(2,1)S(1)}, u32[]{:S(2)}, u32[]{:S(2)}) collective-permute-start(bf16[16,4,128,128]{3,2,1,0:T(8,128)(2,1)} %refs_0_.3), channel_id=1, source_target_pairs={{0,1},{1,0},{2,3},{3,2},{4,5},{5,4},{6,7},{7,6},{8,9},{9,8},{10,11... | collective-permute-start | bytes 6291464 | tf_op jit(solution)/shard_map/ppermute | solution.py:288
  2.6 62.0 %copy-start.2 = (bf16[4,4,128,128]{3,2,1,0:T(8,128)(2,1)}, bf16[4,4,128,128]{3,2,1,0:T(8,128)(2,1)S(1)}, u32[]{:S(2)}) copy-start(bf16[4,4,128,128]{3,2,1,0:T(8,128)(2,1)S(1)} %get-tuple-element.23.refs_2_) | copy-start | bytes 1572868
  2.6 36.2 %collective-permute-start.5 = (bf16[4,4,128,128]{3,2,1,0:T(8,128)(2,1)S(1)}, bf16[4,4,128,128]{3,2,1,0:T(8,128)(2,1)S(1)}, u32[]{:S(2)}, u32[]{:S(2)}) collective-permute-start(bf16[4,4,128,128]{3,2,1,0:T(8,128)(2,1)S(1)} %get-tuple-element.23.refs_2_), channel_id=1, source_target_pairs={{0,2},{1,3},{2,0},{3,1},{4,6},{5,7},{6,4},{7,5},{8,10},{9,11},{10,... | collective-permute-start | bytes 1572872 | tf_op jit(solution)/shard_map/ppermute | solution.py:278
  7.9 56.7 %copy-start.5 = (bf16[4,4,128,128]{3,2,1,0:T(8,128)(2,1)}, bf16[4,4,128,128]{3,2,1,0:T(8,128)(2,1)S(1)}, u32[]{:S(2)}) copy-start(bf16[4,4,128,128]{3,2,1,0:T(8,128)(2,1)S(1)} %get-tuple-element.25.refs_8_) | copy-start | bytes 1572868
  7.9 68.7 %copy-start = (bf16[4,4,128,128]{3,2,1,0:T(8,128)(2,1)}, bf16[4,4,128,128]{3,2,1,0:T(8,128)(2,1)S(1)}, u32[]{:S(2)}) copy-start(bf16[4,4,128,128]{3,2,1,0:T(8,128)(2,1)S(1)} %get-tuple-element.35.refs_9_) | copy-start | bytes 1572868
  7.9 68.7 %copy-start.1 = (bf16[4,4,128,128]{3,2,1,0:T(8,128)(2,1)}, bf16[4,4,128,128]{3,2,1,0:T(8,128)(2,1)S(1)}, u32[]{:S(2)}) copy-start(bf16[4,4,128,128]{3,2,1,0:T(8,128)(2,1)S(1)} %get-tuple-element.30.refs_9_) | copy-start | bytes 1572868
  7.9 31.4 %collective-permute-start.8 = (bf16[4,4,128,128]{3,2,1,0:T(8,128)(2,1)S(1)}, bf16[4,4,128,128]{3,2,1,0:T(8,128)(2,1)S(1)}, u32[]{:S(2)}, u32[]{:S(2)}) collective-permute-start(bf16[4,4,128,128]{3,2,1,0:T(8,128)(2,1)S(1)} %get-tuple-element.24), channel_id=1, source_target_pairs={{0,28},{4,8},{8,4},{12,16},{16,12},{20,24},{24,20},{28,0},{1,29},{... | collective-permute-start | bytes 1572872 | tf_op jit(solution)/shard_map/ppermute | solution.py:322
  12.5 28.3 %collective-permute-start.9 = (bf16[4,4,128,128]{3,2,1,0:T(8,128)(2,1)S(1)}, bf16[4,4,128,128]{3,2,1,0:T(8,128)(2,1)S(1)}, u32[]{:S(2)}, u32[]{:S(2)}) collective-permute-start(bf16[4,4,128,128]{3,2,1,0:T(8,128)(2,1)S(1)} %get-tuple-element.25.refs_8_), channel_id=1, source_target_pairs={{0,2},{1,3},{2,0},{3,1},{4,6},{5,7},{6,4},{7,5},{8,10},{9,11},{10,... | collective-permute-start | bytes 1572872 | tf_op jit(solution)/shard_map/ppermute | solution.py:278
  13.0 11.8 %collective-permute-start = (s32[4,16]{1,0:T(4,128)S(1)}, s32[4,16]{1,0:T(4,128)S(1)}, u32[]{:S(2)}, u32[]{:S(2)}) collective-permute-start(s32[4,16]{1,0:T(4,128)S(1)} %bitcast.7), channel_id=1, source_target_pairs={{0,28},{4,8},{8,4},{12,16},{16,12},{20,24},{24,20},{28,0},{1,29},{... | collective-permute-start | bytes 776 | tf_op jit(solution)/shard_map/ppermute | solution.py:326
  24.8 3.6 %collective-permute-start.1 = (s32[4,16]{1,0:T(4,128)S(1)}, s32[4,16]{1,0:T(4,128)S(1)}, u32[]{:S(2)}, u32[]{:S(2)}) collective-permute-start(s32[4,16]{1,0:T(4,128)S(1)} %bitcast.8), channel_id=1, source_target_pairs={{0,4},{4,0},{8,12},{12,8},{16,20},{20,16},{24,28},{28,24},{1,5},{5... | collective-permute-start | bytes 776 | tf_op jit(solution)/shard_map/ppermute | solution.py:327
  28.4 3.6 %collective-permute-start.2 = (s32[4,16]{1,0:T(4,128)S(1)}, s32[4,16]{1,0:T(4,128)S(1)}, u32[]{:S(2)}, u32[]{:S(2)}) collective-permute-start(s32[4,16]{1,0:T(4,128)S(1)} %bitcast.11), channel_id=1, source_target_pairs={{0,2},{1,3},{2,0},{3,1},{4,6},{5,7},{6,4},{7,5},{8,10},{9,11},{10,... | collective-permute-start | bytes 776 | tf_op jit(solution)/shard_map/ppermute | solution.py:278
  32.0 1.2 %collective-permute-start.3 = (s32[4,16]{1,0:T(4,128)S(1)}, s32[4,16]{1,0:T(4,128)S(1)}, u32[]{:S(2)}, u32[]{:S(2)}) collective-permute-start(s32[4,16]{1,0:T(4,128)S(1)} %bitcast.12), channel_id=1, source_target_pairs={{0,1},{1,0},{2,3},{3,2},{4,5},{5,4},{6,7},{7,6},{8,9},{9,8},{10,11... | collective-permute-start | bytes 776 | tf_op jit(solution)/shard_map/ppermute | solution.py:288
  33.2 1.2 %collective-permute-start.4 = (s32[4,16]{1,0:T(4,128)S(1)}, s32[4,16]{1,0:T(4,128)S(1)}, u32[]{:S(2)}, u32[]{:S(2)}) collective-permute-start(s32[4,16]{1,0:T(4,128)S(1)} %collective-permute-done.2.refs_3_.refs_2_), channel_id=1, source_target_pairs={{0,1},{1,0},{2,3},{3,2},{4,5},{5,4},{6,7},{7,6},{8,9},{9,8},{10,11... | collective-permute-start | bytes 776 | tf_op jit(solution)/shard_map/ppermute | solution.py:288
  34.3 16.7 %collective-permute-start.11 = (bf16[4,4,128,128]{3,2,1,0:T(8,128)(2,1)S(1)}, bf16[4,4,128,128]{3,2,1,0:T(8,128)(2,1)S(1)}, u32[]{:S(2)}, u32[]{:S(2)}) collective-permute-start(bf16[4,4,128,128]{3,2,1,0:T(8,128)(2,1)S(1)} %get-tuple-element.27), channel_id=1, source_target_pairs={{0,28},{4,8},{8,4},{12,16},{16,12},{20,24},{24,20},{28,0},{1,29},{... | collective-permute-start | bytes 1572872 | tf_op jit(solution)/shard_map/ppermute | solution.py:322
  38.8 14.8 %collective-permute-start.12 = (bf16[4,4,128,128]{3,2,1,0:T(8,128)(2,1)S(1)}, bf16[4,4,128,128]{3,2,1,0:T(8,128)(2,1)S(1)}, u32[]{:S(2)}, u32[]{:S(2)}) collective-permute-start(bf16[4,4,128,128]{3,2,1,0:T(8,128)(2,1)S(1)} %get-tuple-element.30.refs_9_), channel_id=1, source_target_pairs={{0,2},{1,3},{2,0},{3,1},{4,6},{5,7},{6,4},{7,5},{8,10},{9,11},{10,... | collective-permute-start | bytes 1572872 | tf_op jit(solution)/shard_map/ppermute | solution.py:278
  39.3 25.9 %copy-start.12 = (bf16[4,4,128,128]{3,2,1,0:T(8,128)(2,1)}, bf16[4,4,128,128]{3,2,1,0:T(8,128)(2,1)S(1)}, u32[]{:S(2)}) copy-start(bf16[4,4,128,128]{3,2,1,0:T(8,128)(2,1)S(1)} %collective-permute-done.8.refs_7_) | copy-start | bytes 1572868
  39.3 24.4 %collective-permute-start.15 = (bf16[4,4,128,128]{3,2,1,0:T(8,128)(2,1)S(1)}, bf16[4,4,128,128]{3,2,1,0:T(8,128)(2,1)S(1)}, u32[]{:S(2)}, u32[]{:S(2)}) collective-permute-start(bf16[4,4,128,128]{3,2,1,0:T(8,128)(2,1)S(1)} %get-tuple-element.35.refs_9_), channel_id=1, source_target_pairs={{0,2},{1,3},{2,0},{3,1},{4,6},{5,7},{6,4},{7,5},{8,10},{9,11},{10,... | collective-permute-start | bytes 1572872 | tf_op jit(solution)/shard_map/ppermute | solution.py:278
  40.8 22.9 %collective-permute-start.7 = (bf16[4,4,128,128]{3,2,1,0:T(8,128)(2,1)S(1)}, bf16[4,4,128,128]{3,2,1,0:T(8,128)(2,1)S(1)}, u32[]{:S(2)}, u32[]{:S(2)}) collective-permute-start(bf16[4,4,128,128]{3,2,1,0:T(8,128)(2,1)S(1)} %collective-permute-done.5.refs_3_), channel_id=1, source_target_pairs={{0,1},{1,0},{2,3},{3,2},{4,5},{5,4},{6,7},{7,6},{8,9},{9,8},{10,11... | collective-permute-start | bytes 1572872 | tf_op jit(solution)/shard_map/ppermute | solution.py:288
  40.8 0.8 copy-start.3
  51.0 25.5 %collective-permute-start.10 = (bf16[4,4,128,128]{3,2,1,0:T(8,128)(2,1)S(1)}, bf16[4,4,128,128]{3,2,1,0:T(8,128)(2,1)}, u32[]{:S(2)}, u32[]{:S(2)}) collective-permute-start(bf16[4,4,128,128]{3,2,1,0:T(8,128)(2,1)S(1)} %collective-permute-done.9.refs_3_), channel_id=1, source_target_pairs={{0,1},{1,0},{2,3},{3,2},{4,5},{5,4},{6,7},{7,6},{8,9},{9,8},{10,11... | collective-permute-start | bytes 1572872 | tf_op jit(solution)/shard_map/ppermute | solution.py:288
  53.6 27.8 %collective-permute-start.14 = (bf16[4,4,128,128]{3,2,1,0:T(8,128)(2,1)}, bf16[4,4,128,128]{3,2,1,0:T(8,128)(2,1)}, u32[]{:S(2)}, u32[]{:S(2)}) collective-permute-start(bf16[4,4,128,128]{3,2,1,0:T(8,128)(2,1)} %get-tuple-element.32), channel_id=1, source_target_pairs={{0,4},{4,0},{8,12},{12,8},{16,20},{20,16},{24,28},{28,24},{1,5},{5... | collective-permute-start | bytes 1572872 | tf_op jit(solution)/shard_map/ppermute | solution.py:322
  63.7 17.7 %collective-permute-start.13 = (bf16[4,4,128,128]{3,2,1,0:T(8,128)(2,1)S(1)}, bf16[4,4,128,128]{3,2,1,0:T(8,128)(2,1)}, u32[]{:S(2)}, u32[]{:S(2)}) collective-permute-start(bf16[4,4,128,128]{3,2,1,0:T(8,128)(2,1)S(1)} %collective-permute-done.12.refs_3_), channel_id=1, source_target_pairs={{0,1},{1,0},{2,3},{3,2},{4,5},{5,4},{6,7},{7,6},{8,9},{9,8},{10,11... | collective-permute-start | bytes 1572872 | tf_op jit(solution)/shard_map/ppermute | solution.py:288
  63.7 0.8 copy-start.6
  64.6 21.9 %collective-permute-start.17 = (bf16[4,4,128,128]{3,2,1,0:T(8,128)(2,1)}, bf16[4,4,128,128]{3,2,1,0:T(8,128)(2,1)}, u32[]{:S(2)}, u32[]{:S(2)}) collective-permute-start(bf16[4,4,128,128]{3,2,1,0:T(8,128)(2,1)} %get-tuple-element.37), channel_id=1, source_target_pairs={{0,4},{4,0},{8,12},{12,8},{16,20},{20,16},{24,28},{28,24},{1,5},{5... | collective-permute-start | bytes 1572872 | tf_op jit(solution)/shard_map/ppermute | solution.py:322
  64.6 1.3 %copy-start.11 = (bf16[16,4,128,128]{3,2,1,0:T(8,128)(2,1)}, bf16[16,4,128,128]{3,2,1,0:T(8,128)(2,1)S(1)}, u32[]{:S(2)}) copy-start(bf16[16,4,128,128]{3,2,1,0:T(8,128)(2,1)S(1)} %collective-permute-done.6.refs_4_.refs_9_.refs_10_) | copy-start | bytes 6291460
  64.6 21.8 %collective-permute-start.16 = (bf16[4,4,128,128]{3,2,1,0:T(8,128)(2,1)S(1)}, bf16[4,4,128,128]{3,2,1,0:T(8,128)(2,1)}, u32[]{:S(2)}, u32[]{:S(2)}) collective-permute-start(bf16[4,4,128,128]{3,2,1,0:T(8,128)(2,1)S(1)} %collective-permute-done.15.refs_3_), channel_id=1, source_target_pairs={{0,1},{1,0},{2,3},{3,2},{4,5},{5,4},{6,7},{7,6},{8,9},{9,8},{10,11... | collective-permute-start | bytes 1572872 | tf_op jit(solution)/shard_map/ppermute | solution.py:288
  68.0 1.0 %copy-start.4 = (bf16[4,4,128,128]{3,2,1,0:T(8,128)(2,1)S(1)}, bf16[4,4,128,128]{3,2,1,0:T(8,128)(2,1)}, u32[]{:S(2)}) copy-start(bf16[4,4,128,128]{3,2,1,0:T(8,128)(2,1)} %copy-done.3) | copy-start | bytes 1572868
  69.1 1.0 %copy-start.7 = (bf16[4,4,128,128]{3,2,1,0:T(8,128)(2,1)S(1)}, bf16[4,4,128,128]{3,2,1,0:T(8,128)(2,1)}, u32[]{:S(2)}) copy-start(bf16[4,4,128,128]{3,2,1,0:T(8,128)(2,1)} %copy-done.6) | copy-start | bytes 1572868

commit v5 on v4

--- a/solution.py
+++ b/solution.py
@@ -142,7 +142,7 @@
 def multiply(*refs, kinds, chunk, ahead, block_rows, kept, news, first):
     refs = list(refs)
     take = lambda count: [refs.pop(0) for _ in range(count)]
-    flips_ref, place_ref = take(2)
+    (place_ref,) = take(1)
     p_refs, new_refs = take(len(kinds)), take(len(news))
     take(0 if first else 2)
     ahead_refs = take(kinds.count("fetch") if ahead else 0)
@@ -150,7 +150,7 @@
     next_ref = take(1)[0] if ahead else None
     lefts = take(1)[0] if first else None
     results, new_sem, p_sems, out_sems, next_sem = refs
-    flip = flips_ref[0]
+    flip = lax.axis_index("row") % 2 if lax.axis_size("row") % 2 == 0 else 0
     start = local_start(chunk, block_rows, flip)
     count = chunk[1] - chunk[0]
     s_slots = (window.shape[0] - 1) // (2 * block_rows)
@@ -354,7 +354,7 @@
         kinds += ["here"] * len(passed)
         fetch_from = [far[n][0]] + core
         here = far[n][1:] + passed
-        inputs, specs = [flips, place_of[chunk[0] >= reach]], [SMEM] * 2
+        inputs, specs = [place_of[chunk[0] >= reach]], [SMEM]
         for kind in kinds:
             if kind == "here":
                 keep_in = in_vmem if ahead is None or len(here) <= len(passed) else lambda x: x

time: 91.8 us -> 90.2 us (0.983)
  local copies, waits for them, and re-layouts: 4.49 us -> 2.64 us
    unnamed x26 -> x24, local copies, waits for them, and re-layouts: 4.49 us -> 2.64 us
  transfers between devices with their start and end apart: 18 -> 18, of which waited for: 8 -> 8; matrix products, arithmetic and copies ran while one was open for 0% -> 0% of each run, Pallas kernels for 25% -> 26%
where the time goes in v5:
time: 90.2 us; the launch traced here: 89.9 us
  waiting for transfers between devices  42.8 us (47%)
  Pallas kernels  28.2 us (31%)
  starting transfers between devices  16.1 us (18%)
  local copies, waits for them, and re-layouts  2.64 us (3%)
    pallas_call x4, Pallas kernels, steps(): pl.pallas_call(functools.partial(multiply, kinds=tuple(kinds), chunk=chun...  21.5 us
    ppermute x5, waiting for transfers between devices, far_pieces(): held = held + [lax.ppermute(piece, 'col', swap) for piece in held]  15.1 us
    ppermute x1, waiting for transfers between devices, steps(): first_cols = lax.ppermute(s_cols.T, 'row', first_pairs)  11.7 us
    ppermute x4, waiting for transfers between devices, steps(): halo.append(lax.ppermute(piece, 'row', pairs))  10.2 us
    ppermute x4, starting transfers between devices, steps(): halo.append(lax.ppermute(piece, 'row', pairs))  9.06 us
    ppermute x5, starting transfers between devices, far_pieces(): held = held + [lax.ppermute(piece, 'col', swap) for piece in held]  5.67 us
    pallas_call x2, Pallas kernels, cut(): pl.pallas_call(body, out_shape=shapes, in_specs=[ANY, ANY], out_specs=[VM...  4.69 us
    ppermute x1, waiting for transfers between devices, steps(): second_cols = lax.ppermute(s_cols.T, 'row', second_pairs)  3.58 us
  transfers between devices with their start and end apart: 18, of which 8 were waited for; matrix products, arithmetic and copies ran while one was open for 0% of the time, Pallas kernels for 26%

profile of v5, /device:TPU:0, one launch (start us, length us, event | category | flops | bytes accessed | tf_op | source)
XLA Modules:
  0.0 89.9 jit_solution(3377200087918367302)
XLA Ops:
  0.0 0.0 copy-start.9
  0.0 0.6 collective-permute-start.6
  0.6 2.0 %shard_map.57 = (bf16[4,4,128,128]{3,2,1,0:T(8,128)(2,1)S(1)}, bf16[4,4,128,128]{3,2,1,0:T(8,128)(2,1)}) custom-call(bf16[16,4,128,128]{3,2,1,0:T(8,128)(2,1)} %refs_0_.3, bf16[16,4,128,128]{3,2,1,0:T(8,128)(2,1)} %refs_5_.1), custom_call_target="tpu_custom_call" | custom-call | tf_op jit(solution)/shard_map/pallas_call | solution.py:90
  2.6 0.0 copy-start.2
  2.6 2.6 %collective-permute-start.5 = (bf16[4,4,128,128]{3,2,1,0:T(8,128)(2,1)S(1)}, bf16[4,4,128,128]{3,2,1,0:T(8,128)(2,1)S(1)}, u32[]{:S(2)}, u32[]{:S(2)}) collective-permute-start(bf16[4,4,128,128]{3,2,1,0:T(8,128)(2,1)S(1)} %get-tuple-element.23.refs_1_), channel_id=1, source_target_pairs={{0,2},{1,3},{2,0},{3,1},{4,6},{5,7},{6,4},{7,5},{8,10},{9,11},{10,... | collective-permute-start | bytes 1572872 | tf_op jit(solution)/shard_map/ppermute | solution.py:278
  5.2 2.7 %shard_map.58 = (bf16[4,4,128,128]{3,2,1,0:T(8,128)(2,1)S(1)}, bf16[4,4,128,128]{3,2,1,0:T(8,128)(2,1)S(1)}, bf16[4,4,128,128]{3,2,1,0:T(8,128)(2,1)S(1)}, bf16[...) custom-call(bf16[16,4,128,128]{3,2,1,0:T(8,128)(2,1)} %refs_0_.3, ...), custom_call_target="tpu_custom_call" | custom-call | tf_op jit(solution)/shard_map/pallas_call | solution.py:90
  7.9 0.0 copy-start.3
  7.9 0.0 copy-start
  7.9 0.0 copy-start.1
  7.9 4.6 %collective-permute-start.8 = (bf16[4,4,128,128]{3,2,1,0:T(8,128)(2,1)S(1)}, bf16[4,4,128,128]{3,2,1,0:T(8,128)(2,1)S(1)}, u32[]{:S(2)}, u32[]{:S(2)}) collective-permute-start(bf16[4,4,128,128]{3,2,1,0:T(8,128)(2,1)S(1)} %get-tuple-element.24), channel_id=1, source_target_pairs={{0,28},{4,8},{8,4},{12,16},{16,12},{20,24},{24,20},{28,0},{1,29},{... | collective-permute-start | bytes 1572872 | tf_op jit(solution)/shard_map/ppermute | solution.py:322
  12.5 0.5 collective-permute-start.9
  13.0 0.0 copy-done.9
  13.1 0.1 collective-permute-start
  13.1 11.7 %collective-permute-done.near_ref = s32[4,16]{1,0:T(4,128)S(1)} collective-permute-done((s32[4,16]{1,0:T(4,128)S(1)}, s32[4,16]{1,0:T(4,128)S(1)}, u32[]{:S(2)}, u32[]{:S(2)}) %collective-permute-start) | collective-permute-done | bytes 288 | tf_op jit(solution)/shard_map/ppermute | solution.py:326
  24.8 0.0 collective-permute-start.1
  24.8 3.6 %collective-permute-done.1.refs_0_ = s32[4,16]{1,0:T(4,128)S(1)} collective-permute-done((s32[4,16]{1,0:T(4,128)S(1)}, s32[4,16]{1,0:T(4,128)S(1)}, u32[]{:S(2)}, u32[]{:S(2)}) %collective-permute-start.1) | collective-permute-done | bytes 288 | tf_op jit(solution)/shard_map/ppermute | solution.py:327
  28.4 0.0 copy-done.10
  28.4 0.5 collective-permute-start.2
  29.0 3.0 %collective-permute-done.2.refs_3_.refs_2_ = s32[4,16]{1,0:T(4,128)S(1)} collective-permute-done((s32[4,16]{1,0:T(4,128)S(1)}, s32[4,16]{1,0:T(4,128)S(1)}, u32[]{:S(2)}, u32[]{:S(2)}) %collective-permute-start.2) | collective-permute-done | bytes 288 | tf_op jit(solution)/shard_map/ppermute | solution.py:278
  32.0 0.0 collective-permute-start.3
  32.0 1.2 %collective-permute-done.3.refs_4_.refs_3_ = s32[4,16]{1,0:T(4,128)S(1)} collective-permute-done((s32[4,16]{1,0:T(4,128)S(1)}, s32[4,16]{1,0:T(4,128)S(1)}, u32[]{:S(2)}, u32[]{:S(2)}) %collective-permute-start.3) | collective-permute-done | bytes 288 | tf_op jit(solution)/shard_map/ppermute | solution.py:288
  33.2 0.2 collective-permute-start.4
  33.3 1.0 %collective-permute-done.4.refs_5_.refs_4_ = s32[4,16]{1,0:T(4,128)S(1)} collective-permute-done((s32[4,16]{1,0:T(4,128)S(1)}, s32[4,16]{1,0:T(4,128)S(1)}, u32[]{:S(2)}, u32[]{:S(2)}) %collective-permute-start.4) | collective-permute-done | bytes 288 | tf_op jit(solution)/shard_map/ppermute | solution.py:288
  34.3 4.4 %collective-permute-start.11 = (bf16[4,4,128,128]{3,2,1,0:T(8,128)(2,1)S(1)}, bf16[4,4,128,128]{3,2,1,0:T(8,128)(2,1)S(1)}, u32[]{:S(2)}, u32[]{:S(2)}) collective-permute-start(bf16[4,4,128,128]{3,2,1,0:T(8,128)(2,1)S(1)} %get-tuple-element.27), channel_id=1, source_target_pairs={{0,28},{4,8},{8,4},{12,16},{16,12},{20,24},{24,20},{28,0},{1,29},{... | collective-permute-start | bytes 1572872 | tf_op jit(solution)/shard_map/ppermute | solution.py:322
  38.8 0.0 collective-permute-done.5.refs_2_
  38.8 0.5 collective-permute-start.12
  39.3 0.0 collective-permute-done.8.refs_6_
  39.3 1.5 %collective-permute-start.15 = (bf16[4,4,128,128]{3,2,1,0:T(8,128)(2,1)S(1)}, bf16[4,4,128,128]{3,2,1,0:T(8,128)(2,1)}, u32[]{:S(2)}, u32[]{:S(2)}) collective-permute-start(bf16[4,4,128,128]{3,2,1,0:T(8,128)(2,1)S(1)} %get-tuple-element.35.refs_8_), channel_id=1, source_target_pairs={{0,2},{1,3},{2,0},{3,1},{4,6},{5,7},{6,4},{7,5},{8,10},{9,11},{10,... | collective-permute-start | bytes 1572872 | tf_op jit(solution)/shard_map/ppermute | solution.py:278
  40.8 0.0 collective-permute-done.9.refs_2_
  40.8 0.0 collective-permute-start.7
  40.8 10.2 %collective-permute-done.11.refs_5_ = bf16[4,4,128,128]{3,2,1,0:T(8,128)(2,1)S(1)} collective-permute-done((bf16[4,4,128,128]{3,2,1,0:T(8,128)(2,1)S(1)}, bf16[4,4,128,128]{3,2,1,0:T(8,128)(2,1)S(1)}, u32[]{:S(2)}, u32[]{:S(2)}) %collective-permute-start.11) | collective-permute-done | bytes 524320 | tf_op jit(solution)/shard_map/ppermute | solution.py:322
  51.0 0.8 copy-done.4
  51.8 0.0 collective-permute-start.10
  51.8 1.9 %collective-permute-done.12.refs_2_ = bf16[4,4,128,128]{3,2,1,0:T(8,128)(2,1)} collective-permute-done((bf16[4,4,128,128]{3,2,1,0:T(8,128)(2,1)S(1)}, bf16[4,4,128,128]{3,2,1,0:T(8,128)(2,1)}, u32[]{:S(2)}, u32[]{:S(2)}) %collective-permute-start.12) | collective-permute-done | bytes 524320 | tf_op jit(solution)/shard_map/ppermute | solution.py:278
  53.7 0.0 collective-permute-start.14
  53.7 10.2 %collective-permute-done.15.refs_2_ = bf16[4,4,128,128]{3,2,1,0:T(8,128)(2,1)} collective-permute-done((bf16[4,4,128,128]{3,2,1,0:T(8,128)(2,1)S(1)}, bf16[4,4,128,128]{3,2,1,0:T(8,128)(2,1)}, u32[]{:S(2)}, u32[]{:S(2)}) %collective-permute-start.15) | collective-permute-done | bytes 524320 | tf_op jit(solution)/shard_map/ppermute | solution.py:278
  63.8 0.0 collective-permute-start.13
  63.8 0.0 collective-permute-done.7.refs_4_
  63.9 0.0 copy-done.11
  63.9 0.0 copy-start.6
  63.9 0.8 copy-done.6
  64.7 0.0 collective-permute-start.17
  64.7 0.0 collective-permute-done.6.refs_3_.refs_8_.refs_9_
  64.7 0.5 collective-permute-start.16
  65.2 0.1 pad_add_fusion.flip_ref
  65.2 0.0 copy-done.8
  65.2 1.0 %shard_map.56.refs_0_ = s32[16,128]{1,0:T(8,128)S(1)} custom-call(s32[1]{0:T(128)} %bitcast.first_ref, s32[2]{0:T(128)S(1)} %pad_add_fusion.flip_ref, s32[4,16]{1,0:T(4,128)S(1)} %bitcast.9, s32[4,16]{1,0:T(4,128)S(1)} %collective-permute-done.near_ref, s32[8,16]{1,0:T(8,128)S(1)} %bitcast.5, s32[4,16]{1,0:T(4,128)S(1)} %bitcast.13, ...), custom_call_target="tpu_custom_call" | custom-call | tf_op jit(solution)/shard_map/pallas_call | solution.py:333
  66.2 1.0 %shard_map.55.refs_0_ = s32[16,128]{1,0:T(8,128)S(1)} custom-call(s32[1]{0:T(128)} %bitcast.first_ref, s32[2]{0:T(128)S(1)} %pad_add_fusion.flip_ref, s32[4,16]{1,0:T(4,128)S(1)} %bitcast.10, s32[4,16]{1,0:T(4,128)S(1)} %collective-permute-done.near_ref, s32[4,16]{1,0:T(4,128)S(1)} %collective-permute-done.1.refs_0_, s32[8,16]{1,0:T(8,128)S(1)} %bitcast.6, ...), custom_call_target="tpu_custom_call" | custom-call | tf_op jit(solution)/shard_map/pallas_call | solution.py:333
  67.2 0.0 copy-done.2
  67.3 0.0 copy-done.3
  67.3 0.0 copy-start.7
  67.3 1.0 %copy-done.7 = bf16[4,4,128,128]{3,2,1,0:T(8,128)(2,1)S(1)} copy-done((bf16[4,4,128,128]{3,2,1,0:T(8,128)(2,1)S(1)}, bf16[4,4,128,128]{3,2,1,0:T(8,128)(2,1)}, u32[]{:S(2)}) %copy-start.7) | copy-done | bytes 524312
  68.3 6.3 %shard_map.59 = (f32[16,8,128,128]{3,2,1,0:T(8,128)}, bf16[129,128,128]{2,1,0:T(8,128)(2,1)S(1)}, bf16[4,8,128,128]{3,2,1,0:T(8,128)(2,1)S(1)}) custom-call(s32[16,128]{1,0:T(8,128)S(1)} %shard_map.56.refs_0_, bf16[4,4,128,128]{3,2,1,0:T(8,128)(2,1)} %copy-done.2, bf16[4,4,128,128]{3,2,1,0:T(8,128)(2,1)S(1)} %collective-permute-done.5.refs_2_, ...), custom_call_target="tpu_custom_call" | custom-call | tf_op jit(solution)/shard_map/pallas_call | solution.py:395
  74.7 0.0 copy-done
  74.7 0.0 copy-done.1
  74.7 0.0 collective-permute-done.10.refs_4_
  74.7 0.0 copy-done.5
  74.7 4.8 %shard_map.60 = (f32[16,8,128,128]{3,2,1,0:T(8,128)}, bf16[129,128,128]{2,1,0:T(8,128)(2,1)S(1)}, bf16[4,8,128,128]{3,2,1,0:T(8,128)(2,1)S(1)}) custom-call(s32[16,128]{1,0:T(8,128)S(1)} %shard_map.56.refs_0_, bf16[4,8,128,128]{3,2,1,0:T(8,128)(2,1)S(1)} %get-tuple-element.26.refs_1_.refs_3_, ...), custom_call_target="tpu_custom_call", output_to_operand_aliasing={{1}: (6, {}), {0}: (7, {})} | custom-call | tf_op jit(solution)/shard_map/pallas_call | solution.py:395
  79.5 0.0 collective-permute-done.14.refs_5_
  79.6 0.0 collective-permute-done.13.refs_4_
  79.6 5.2 %shard_map.61 = (f32[16,8,128,128]{3,2,1,0:T(8,128)}, bf16[129,128,128]{2,1,0:T(8,128)(2,1)S(1)}, bf16[4,8,128,128]{3,2,1,0:T(8,128)(2,1)S(1)}) custom-call(s32[16,128]{1,0:T(8,128)S(1)} %shard_map.55.refs_0_, bf16[4,8,128,128]{3,2,1,0:T(8,128)(2,1)S(1)} %get-tuple-element.31.refs_1_.refs_3_, ...), custom_call_target="tpu_custom_call", output_to_operand_aliasing={{1}: (6, {}), {0}: (7, {})} | custom-call | tf_op jit(solution)/shard_map/pallas_call | solution.py:395
  84.7 0.0 collective-permute-done.17.refs_5_
  84.7 0.0 collective-permute-done.16.refs_4_
  84.7 5.2 %shard_map.62 = (f32[16,8,128,128]{3,2,1,0:T(8,128)}, bf16[129,128,128]{2,1,0:T(8,128)(2,1)S(1)}) custom-call(s32[16,128]{1,0:T(8,128)S(1)} %shard_map.55.refs_0_, bf16[4,8,128,128]{3,2,1,0:T(8,128)(2,1)S(1)} %get-tuple-element.36.refs_1_.refs_3_, ...), custom_call_target="tpu_custom_call", output_to_operand_aliasing={{1}: (6, {}), {0}: (7, {})} | custom-call | tf_op jit(solution)/shard_map/pallas_call | solution.py:395
  (5 shorter events, 0.0 us)
Async XLA Ops:
  0.0 13.1 %copy-start.9 = (s32[16,4]{0,1:T(4,128)S(1)}, s32[16,4]{0,1:T(4,128)}, u32[]{:S(2)}) copy-start(s32[16,4]{0,1:T(4,128)} %param.8) | copy-start | bytes 772
  0.0 28.4 %copy-start.10 = (s32[16,4]{0,1:T(4,128)S(1)}, s32[16,4]{0,1:T(4,128)}, u32[]{:S(2)}) copy-start(s32[16,4]{0,1:T(4,128)} %param.6) | copy-start | bytes 772
  0.0 65.2 %copy-start.8 = (s32[16,8]{0,1:T(8,128)S(1)}, s32[16,8]{0,1:T(8,128)}, u32[]{:S(2)}) copy-start(s32[16,8]{0,1:T(8,128)} %param.9) | copy-start | bytes 1540
  0.0 64.7 %collective-permute-start.6 = (bf16[16,4,128,128]{3,2,1,0:T(8,128)(2,1)}, bf16[16,4,128,128]{3,2,1,0:T(8,128)(2,1)}, u32[]{:S(2)}, u32[]{:S(2)}) collective-permute-start(bf16[16,4,128,128]{3,2,1,0:T(8,128)(2,1)} %refs_0_.3), channel_id=1, source_target_pairs={{0,1},{1,0},{2,3},{3,2},{4,5},{5,4},{6,7},{7,6},{8,9},{9,8},{10,11... | collective-permute-start | bytes 6291464 | tf_op jit(solution)/shard_map/ppermute | solution.py:288
  2.6 64.7 %copy-start.2 = (bf16[4,4,128,128]{3,2,1,0:T(8,128)(2,1)}, bf16[4,4,128,128]{3,2,1,0:T(8,128)(2,1)S(1)}, u32[]{:S(2)}) copy-start(bf16[4,4,128,128]{3,2,1,0:T(8,128)(2,1)S(1)} %get-tuple-element.23.refs_1_) | copy-start | bytes 1572868
  2.6 36.2 %collective-permute-start.5 = (bf16[4,4,128,128]{3,2,1,0:T(8,128)(2,1)S(1)}, bf16[4,4,128,128]{3,2,1,0:T(8,128)(2,1)S(1)}, u32[]{:S(2)}, u32[]{:S(2)}) collective-permute-start(bf16[4,4,128,128]{3,2,1,0:T(8,128)(2,1)S(1)} %get-tuple-element.23.refs_1_), channel_id=1, source_target_pairs={{0,2},{1,3},{2,0},{3,1},{4,6},{5,7},{6,4},{7,5},{8,10},{9,11},{10,... | collective-permute-start | bytes 1572872 | tf_op jit(solution)/shard_map/ppermute | solution.py:278
  7.9 59.4 %copy-start.3 = (bf16[4,4,128,128]{3,2,1,0:T(8,128)(2,1)}, bf16[4,4,128,128]{3,2,1,0:T(8,128)(2,1)S(1)}, u32[]{:S(2)}) copy-start(bf16[4,4,128,128]{3,2,1,0:T(8,128)(2,1)S(1)} %get-tuple-element.25.refs_7_) | copy-start | bytes 1572868
  7.9 66.8 %copy-start = (bf16[4,4,128,128]{3,2,1,0:T(8,128)(2,1)}, bf16[4,4,128,128]{3,2,1,0:T(8,128)(2,1)S(1)}, u32[]{:S(2)}) copy-start(bf16[4,4,128,128]{3,2,1,0:T(8,128)(2,1)S(1)} %get-tuple-element.35.refs_8_) | copy-start | bytes 1572868
  7.9 66.8 %copy-start.1 = (bf16[4,4,128,128]{3,2,1,0:T(8,128)(2,1)}, bf16[4,4,128,128]{3,2,1,0:T(8,128)(2,1)S(1)}, u32[]{:S(2)}) copy-start(bf16[4,4,128,128]{3,2,1,0:T(8,128)(2,1)S(1)} %get-tuple-element.30.refs_8_) | copy-start | bytes 1572868
  7.9 31.4 %collective-permute-start.8 = (bf16[4,4,128,128]{3,2,1,0:T(8,128)(2,1)S(1)}, bf16[4,4,128,128]{3,2,1,0:T(8,128)(2,1)S(1)}, u32[]{:S(2)}, u32[]{:S(2)}) collective-permute-start(bf16[4,4,128,128]{3,2,1,0:T(8,128)(2,1)S(1)} %get-tuple-element.24), channel_id=1, source_target_pairs={{0,28},{4,8},{8,4},{12,16},{16,12},{20,24},{24,20},{28,0},{1,29},{... | collective-permute-start | bytes 1572872 | tf_op jit(solution)/shard_map/ppermute | solution.py:322
  12.5 28.3 %collective-permute-start.9 = (bf16[4,4,128,128]{3,2,1,0:T(8,128)(2,1)S(1)}, bf16[4,4,128,128]{3,2,1,0:T(8,128)(2,1)S(1)}, u32[]{:S(2)}, u32[]{:S(2)}) collective-permute-start(bf16[4,4,128,128]{3,2,1,0:T(8,128)(2,1)S(1)} %get-tuple-element.25.refs_7_), channel_id=1, source_target_pairs={{0,2},{1,3},{2,0},{3,1},{4,6},{5,7},{6,4},{7,5},{8,10},{9,11},{10,... | collective-permute-start | bytes 1572872 | tf_op jit(solution)/shard_map/ppermute | solution.py:278
  13.1 11.8 %collective-permute-start = (s32[4,16]{1,0:T(4,128)S(1)}, s32[4,16]{1,0:T(4,128)S(1)}, u32[]{:S(2)}, u32[]{:S(2)}) collective-permute-start(s32[4,16]{1,0:T(4,128)S(1)} %bitcast.7), channel_id=1, source_target_pairs={{0,28},{4,8},{8,4},{12,16},{16,12},{20,24},{24,20},{28,0},{1,29},{... | collective-permute-start | bytes 776 | tf_op jit(solution)/shard_map/ppermute | solution.py:326
  24.8 3.6 %collective-permute-start.1 = (s32[4,16]{1,0:T(4,128)S(1)}, s32[4,16]{1,0:T(4,128)S(1)}, u32[]{:S(2)}, u32[]{:S(2)}) collective-permute-start(s32[4,16]{1,0:T(4,128)S(1)} %bitcast.8), channel_id=1, source_target_pairs={{0,4},{4,0},{8,12},{12,8},{16,20},{20,16},{24,28},{28,24},{1,5},{5... | collective-permute-start | bytes 776 | tf_op jit(solution)/shard_map/ppermute | solution.py:327
  28.4 3.6 %collective-permute-start.2 = (s32[4,16]{1,0:T(4,128)S(1)}, s32[4,16]{1,0:T(4,128)S(1)}, u32[]{:S(2)}, u32[]{:S(2)}) collective-permute-start(s32[4,16]{1,0:T(4,128)S(1)} %bitcast.11), channel_id=1, source_target_pairs={{0,2},{1,3},{2,0},{3,1},{4,6},{5,7},{6,4},{7,5},{8,10},{9,11},{10,... | collective-permute-start | bytes 776 | tf_op jit(solution)/shard_map/ppermute | solution.py:278
  32.0 1.2 %collective-permute-start.3 = (s32[4,16]{1,0:T(4,128)S(1)}, s32[4,16]{1,0:T(4,128)S(1)}, u32[]{:S(2)}, u32[]{:S(2)}) collective-permute-start(s32[4,16]{1,0:T(4,128)S(1)} %bitcast.12), channel_id=1, source_target_pairs={{0,1},{1,0},{2,3},{3,2},{4,5},{5,4},{6,7},{7,6},{8,9},{9,8},{10,11... | collective-permute-start | bytes 776 | tf_op jit(solution)/shard_map/ppermute | solution.py:288
  33.2 1.2 %collective-permute-start.4 = (s32[4,16]{1,0:T(4,128)S(1)}, s32[4,16]{1,0:T(4,128)S(1)}, u32[]{:S(2)}, u32[]{:S(2)}) collective-permute-start(s32[4,16]{1,0:T(4,128)S(1)} %collective-permute-done.2.refs_3_.refs_2_), channel_id=1, source_target_pairs={{0,1},{1,0},{2,3},{3,2},{4,5},{5,4},{6,7},{7,6},{8,9},{9,8},{10,11... | collective-permute-start | bytes 776 | tf_op jit(solution)/shard_map/ppermute | solution.py:288
  34.3 16.7 %collective-permute-start.11 = (bf16[4,4,128,128]{3,2,1,0:T(8,128)(2,1)S(1)}, bf16[4,4,128,128]{3,2,1,0:T(8,128)(2,1)S(1)}, u32[]{:S(2)}, u32[]{:S(2)}) collective-permute-start(bf16[4,4,128,128]{3,2,1,0:T(8,128)(2,1)S(1)} %get-tuple-element.27), channel_id=1, source_target_pairs={{0,28},{4,8},{8,4},{12,16},{16,12},{20,24},{24,20},{28,0},{1,29},{... | collective-permute-start | bytes 1572872 | tf_op jit(solution)/shard_map/ppermute | solution.py:322
  38.8 14.9 %collective-permute-start.12 = (bf16[4,4,128,128]{3,2,1,0:T(8,128)(2,1)S(1)}, bf16[4,4,128,128]{3,2,1,0:T(8,128)(2,1)}, u32[]{:S(2)}, u32[]{:S(2)}) collective-permute-start(bf16[4,4,128,128]{3,2,1,0:T(8,128)(2,1)S(1)} %get-tuple-element.30.refs_8_), channel_id=1, source_target_pairs={{0,2},{1,3},{2,0},{3,1},{4,6},{5,7},{6,4},{7,5},{8,10},{9,11},{10,... | collective-permute-start | bytes 1572872 | tf_op jit(solution)/shard_map/ppermute | solution.py:278
  39.3 24.5 %copy-start.11 = (bf16[4,4,128,128]{3,2,1,0:T(8,128)(2,1)}, bf16[4,4,128,128]{3,2,1,0:T(8,128)(2,1)S(1)}, u32[]{:S(2)}) copy-start(bf16[4,4,128,128]{3,2,1,0:T(8,128)(2,1)S(1)} %collective-permute-done.8.refs_6_) | copy-start | bytes 1572868
  39.3 24.5 %collective-permute-start.15 = (bf16[4,4,128,128]{3,2,1,0:T(8,128)(2,1)S(1)}, bf16[4,4,128,128]{3,2,1,0:T(8,128)(2,1)}, u32[]{:S(2)}, u32[]{:S(2)}) collective-permute-start(bf16[4,4,128,128]{3,2,1,0:T(8,128)(2,1)S(1)} %get-tuple-element.35.refs_8_), channel_id=1, source_target_pairs={{0,2},{1,3},{2,0},{3,1},{4,6},{5,7},{6,4},{7,5},{8,10},{9,11},{10,... | collective-permute-start | bytes 1572872 | tf_op jit(solution)/shard_map/ppermute | solution.py:278
  40.8 23.0 %collective-permute-start.7 = (bf16[4,4,128,128]{3,2,1,0:T(8,128)(2,1)S(1)}, bf16[4,4,128,128]{3,2,1,0:T(8,128)(2,1)S(1)}, u32[]{:S(2)}, u32[]{:S(2)}) collective-permute-start(bf16[4,4,128,128]{3,2,1,0:T(8,128)(2,1)S(1)} %collective-permute-done.5.refs_2_), channel_id=1, source_target_pairs={{0,1},{1,0},{2,3},{3,2},{4,5},{5,4},{6,7},{7,6},{8,9},{9,8},{10,11... | collective-permute-start | bytes 1572872 | tf_op jit(solution)/shard_map/ppermute | solution.py:288
  51.0 0.8 copy-start.4
  51.8 22.9 %collective-permute-start.10 = (bf16[4,4,128,128]{3,2,1,0:T(8,128)(2,1)S(1)}, bf16[4,4,128,128]{3,2,1,0:T(8,128)(2,1)}, u32[]{:S(2)}, u32[]{:S(2)}) collective-permute-start(bf16[4,4,128,128]{3,2,1,0:T(8,128)(2,1)S(1)} %collective-permute-done.9.refs_2_), channel_id=1, source_target_pairs={{0,1},{1,0},{2,3},{3,2},{4,5},{5,4},{6,7},{7,6},{8,9},{9,8},{10,11... | collective-permute-start | bytes 1572872 | tf_op jit(solution)/shard_map/ppermute | solution.py:288
  53.7 25.9 %collective-permute-start.14 = (bf16[4,4,128,128]{3,2,1,0:T(8,128)(2,1)}, bf16[4,4,128,128]{3,2,1,0:T(8,128)(2,1)}, u32[]{:S(2)}, u32[]{:S(2)}) collective-permute-start(bf16[4,4,128,128]{3,2,1,0:T(8,128)(2,1)} %get-tuple-element.32), channel_id=1, source_target_pairs={{0,4},{4,0},{8,12},{12,8},{16,20},{20,16},{24,28},{28,24},{1,5},{5... | collective-permute-start | bytes 1572872 | tf_op jit(solution)/shard_map/ppermute | solution.py:322
  63.8 15.7 %collective-permute-start.13 = (bf16[4,4,128,128]{3,2,1,0:T(8,128)(2,1)}, bf16[4,4,128,128]{3,2,1,0:T(8,128)(2,1)}, u32[]{:S(2)}, u32[]{:S(2)}) collective-permute-start(bf16[4,4,128,128]{3,2,1,0:T(8,128)(2,1)} %collective-permute-done.12.refs_2_), channel_id=1, source_target_pairs={{0,1},{1,0},{2,3},{3,2},{4,5},{5,4},{6,7},{7,6},{8,9},{9,8},{10,11... | collective-permute-start | bytes 1572872 | tf_op jit(solution)/shard_map/ppermute | solution.py:288
  63.9 0.8 copy-start.6
  64.7 20.1 %collective-permute-start.17 = (bf16[4,4,128,128]{3,2,1,0:T(8,128)(2,1)}, bf16[4,4,128,128]{3,2,1,0:T(8,128)(2,1)}, u32[]{:S(2)}, u32[]{:S(2)}) collective-permute-start(bf16[4,4,128,128]{3,2,1,0:T(8,128)(2,1)} %get-tuple-element.37), channel_id=1, source_target_pairs={{0,4},{4,0},{8,12},{12,8},{16,20},{20,16},{24,28},{28,24},{1,5},{5... | collective-permute-start | bytes 1572872 | tf_op jit(solution)/shard_map/ppermute | solution.py:322
  64.7 20.1 %collective-permute-start.16 = (bf16[4,4,128,128]{3,2,1,0:T(8,128)(2,1)}, bf16[4,4,128,128]{3,2,1,0:T(8,128)(2,1)}, u32[]{:S(2)}, u32[]{:S(2)}) collective-permute-start(bf16[4,4,128,128]{3,2,1,0:T(8,128)(2,1)} %collective-permute-done.15.refs_2_), channel_id=1, source_target_pairs={{0,1},{1,0},{2,3},{3,2},{4,5},{5,4},{6,7},{7,6},{8,9},{9,8},{10,11... | collective-permute-start | bytes 1572872 | tf_op jit(solution)/shard_map/ppermute | solution.py:288
  67.3 1.0 %copy-start.7 = (bf16[4,4,128,128]{3,2,1,0:T(8,128)(2,1)S(1)}, bf16[4,4,128,128]{3,2,1,0:T(8,128)(2,1)}, u32[]{:S(2)}) copy-start(bf16[4,4,128,128]{3,2,1,0:T(8,128)(2,1)} %copy-done.6) | copy-start | bytes 1572868
  68.3 6.4 %copy-start.5 = (bf16[4,4,128,128]{3,2,1,0:T(8,128)(2,1)S(1)}, bf16[4,4,128,128]{3,2,1,0:T(8,128)(2,1)}, u32[]{:S(2)}) copy-start(bf16[4,4,128,128]{3,2,1,0:T(8,128)(2,1)} %copy-done.4) | copy-start | bytes 1572868
